TPU v7x, 128 devices: a whole 4x4x4 slice. The times are simulated.
128 devices in a mesh: mem: 4 (over x), space: 32 (over y, z, core).
Axes of the slice: x: 4, y: 4, z: 4, core: 2. Of those that a mesh axis runs over, the one named last changes fastest.
Arguments:
- log_perm: float32 [8, 128, 128, 128], P('mem', 'space'), may hold values from -4 to 4
- saturation: float32 [128, 128, 128], P('space'), may hold values from 0.1 to 0.9
- pressure_init: float32 [128, 128, 128], P('space'), may hold values from -3 to 3
- wells: int32 [64], replicated, may hold values from 0 to 2097151
- well_rate: float32 [64], replicated, may hold values from -4 to 4
- obs_index: int32 [512, 8], replicated, may hold values from 0 to 2097151, as said below
- obs_weight: float32 [512, 8], replicated, may hold values from -2 to 2
- obs_value: float32 [512], replicated, may hold values from -5 to 5
- obs_var: float32 [512], replicated, may hold values from 0.1 to 1
- noise: float32 [8, 512], replicated, may hold values from -5 to 5
Outputs:
- updated_perm: float32 [8, 128, 128, 128], P(None, 'space', 'mem')
Inputs may be any that keep to these rules, and one draw needn't show every extreme that they name: `obs_index`: observation o reads only cells of the grid row o % 128 along the first dimension.
All inputs are finite; a program needn't handle non-finite values.
Results may differ from a plain program's by a relative error of at most 0.00007.
Values sent between devices are 32-bit elements; how exact they have to be, the bound alone decides.
No kernel may reach another device: no remote copies, remote signals or barrier semaphores. Data moves between devices by JAX's collectives and lax.ppermute only.
A program may use at most 128 MiB of HBM per device.

v0:
```python
import jax
import jax.numpy as jnp
from jax import lax
from jax.sharding import PartitionSpec as P

SWEEPS = 6


water_visc = 1.0
oil_visc = 4.0
time_step = 0.1
storage = 1.0
inflation = 4.0


def padded(cells, sides, width):
    for axis, dim in sides:
        count = lax.axis_size(axis)
        ends = count - 1
        head = lax.slice_in_dim(cells, 0, width, axis=dim)
        tail = lax.slice_in_dim(cells, cells.shape[dim] - width, cells.shape[dim], axis=dim)
        cells = jnp.concatenate(
            [
                lax.ppermute(tail, axis, [(i, (i + 1) % count) for i in range(ends)]),
                cells,
                lax.ppermute(head, axis, [((i + 1) % count, i) for i in range(ends)]),
            ],
            axis=dim,
        )
    return cells


def pad_plane(field):
    return jnp.pad(field, ((0, 0), (0, 0), (1, 1), (1, 1)))


def beside_all(field):
    return [
        field[:, 2:, 1:-1, 1:-1],
        field[:, :-2, 1:-1, 1:-1],
        field[:, 1:-1, 2:, 1:-1],
        field[:, 1:-1, :-2, 1:-1],
        field[:, 1:-1, 1:-1, 2:],
        field[:, 1:-1, 1:-1, :-2],
    ]


def middle(field):
    return field[:, 1:-1, 1:-1, 1:-1]


def props(perm, sat):
    water = sat * sat / water_visc
    oil = (1.0 - sat) * (1.0 - sat) / oil_visc
    total = water + oil
    return (perm * total, water / total)


def saturate(perm_pad, sat_pad, press_pad, source):
    lam, frac = props(perm_pad, sat_pad)
    lam_mid, frac_mid, press_mid = (middle(lam), middle(frac), middle(press_pad))
    outflow = jnp.zeros_like(lam_mid)
    for lam_next, frac_next, press_next in zip(
        beside_all(lam), beside_all(frac), beside_all(press_pad)
    ):
        flux = 0.5 * (lam_mid + lam_next) * (press_mid - press_next)
        outflow = outflow + jnp.maximum(flux, 0.0) * frac_mid + jnp.minimum(flux, 0.0) * frac_next
    water = jnp.maximum(source, 0.0) + jnp.minimum(source, 0.0) * frac_mid
    return jnp.clip(middle(sat_pad) + time_step * (water - outflow), 0.0, 1.0)


def pressure(perm_pad, sat_pad, press_pad, source):
    lam, frac = props(perm_pad, sat_pad)
    lam_mid = middle(lam)
    numer = storage * middle(press_pad) + source
    denom = storage + jnp.zeros_like(lam_mid)
    for lam_next, press_next in zip(beside_all(lam), beside_all(press_pad)):
        trans = 0.5 * (lam_mid + lam_next)
        numer = numer + trans * press_next
        denom = denom + trans
    return numer / denom


def sources(wells, well_rate, first_row, rows, ny, nz):
    plane = ny * nz
    well_x = wells // plane
    rest = wells - well_x * plane
    local_x = well_x - first_row
    valid = (local_x >= 0) & (local_x < rows)
    target = jnp.where(valid, local_x * plane + rest, 0)
    field = jnp.zeros((rows * plane,), jnp.float32).at[target].add(jnp.where(valid, well_rate, 0.0))
    return field.reshape(rows, ny, nz)


def body(
    log_perm,
    saturation,
    pressure_init,
    wells,
    well_rate,
    obs_index,
    obs_weight,
    obs_value,
    obs_var,
    noise,
):
    members, width, ny, nz = log_perm.shape
    shape = (members, width, ny, nz)
    perm = jnp.exp(log_perm)
    sat = jnp.broadcast_to(saturation, shape)
    press = jnp.broadcast_to(pressure_init, shape)
    place = lax.axis_index("space")
    source = sources(wells, well_rate, place * width, width, ny, nz)
    stacked = padded(jnp.stack([perm, sat, press]), (("space", 2),), 1)
    perm_pad = pad_plane(stacked[0])
    sat_ext = stacked[1]
    press_ext = stacked[2]
    for sweep in range(SWEEPS):
        sat = saturate(perm_pad, pad_plane(sat_ext), pad_plane(press_ext), source)
        sat_ext = padded(sat, (("space", 1),), 1)
        press = pressure(perm_pad, pad_plane(sat_ext), pad_plane(press_ext), source)
        if sweep + 1 < SWEEPS:
            press_ext = padded(press, (("space", 1),), 1)
    cells = width * ny * nz
    flat = press.reshape(members, cells)
    local = obs_index - place * cells
    valid = (local >= 0) & (local < cells)
    picked = jnp.take(flat, jnp.where(valid, local, 0), axis=1)
    partial_value = jnp.sum(picked * jnp.where(valid, obs_weight, 0.0)[None], axis=2)
    summed = lax.psum(partial_value, "space")
    predicted = lax.all_gather(summed, "mem", axis=0, tiled=True)
    ensemble = predicted.shape[0]
    high = lax.Precision.HIGHEST
    dev = predicted - jnp.mean(predicted, axis=0, keepdims=True)
    cov = jnp.dot(dev.T, dev, precision=high) / (ensemble - 1) + inflation * jnp.diag(obs_var)
    resid = obs_value[None, :] + jnp.sqrt(inflation * obs_var)[None, :] * noise - predicted
    factor = jnp.linalg.cholesky(cov)
    half = lax.linalg.triangular_solve(factor, resid.T, left_side=True, lower=True)
    solved = lax.linalg.triangular_solve(factor, half, left_side=True, lower=True, transpose_a=True)
    weights = jnp.dot(dev, solved, precision=high) / (ensemble - 1)
    mixing = (
        jnp.eye(ensemble, dtype=jnp.float32) + weights - jnp.mean(weights, axis=0, keepdims=True)
    )
    columns = lax.all_to_all(log_perm, "mem", split_axis=2, concat_axis=0, tiled=True)
    return jnp.tensordot(mixing.T, columns, axes=1, precision=high)


def solution(mesh):
    placed = (
        P("mem", "space", None, None),
        P("space", None, None),
        P("space", None, None),
        P(),
        P(),
        P(),
        P(),
        P(),
        P(),
        P(),
    )
    return jax.shard_map(
        body, mesh=mesh, in_specs=placed, out_specs=P(None, "space", "mem", None), check_vma=False
    )
```

profile of v0, /device:TPU:0, one launch (start us, length us, event | category | flops | bytes accessed | tf_op | source)
XLA Modules:
  0.0 506.8 jit_solution(8930795188840093129)
XLA Ops:
  6.8 3.5 collective-permute-done.1
  12.8 2.6 fusion.189
  15.4 7.9 %collective-permute-start.2 = (f32[2,1,128,128]{3,2,1,0:T(8,128)S(1)}, f32[2,1,128,128]{3,2,1,0:T(8,128)S(1)}, u32[]{:S(2)}, u32[]{:S(2)}) collective-permute-start(f32[2,1,128,128]{3,2,1,0:T(8,128)S(1)} %get-tuple-element.64), channel_id=1, source_target_pairs={{0,1},{1,2},{2,3},{3,4},{4,5},{5,6},{6,7},{7,8},{8,9},{9,10},{10,1... | collective-permute-start | bytes 393224 | tf_op jit(solution)/shard_map/ppermute | solution.py:24
  24.6 1.9 collective-permute-done.3
  29.9 5.9 %collective-permute-start.5 = (f32[2,1,128,128]{3,2,1,0:T(8,128)S(1)}, f32[2,1,128,128]{3,2,1,0:T(8,128)S(1)}, u32[]{:S(2)}, u32[]{:S(2)}) collective-permute-start(f32[2,1,128,128]{3,2,1,0:T(8,128)S(1)} %get-tuple-element.63), channel_id=1, source_target_pairs={{0,1},{1,2},{2,3},{3,4},{4,5},{5,6},{6,7},{7,8},{8,9},{9,10},{10,1... | collective-permute-start | bytes 393224 | tf_op jit(solution)/shard_map/ppermute | solution.py:24
  37.3 2.7 fusion.155
  40.0 4.6 collective-permute-start.6
  46.0 3.9 collective-permute-done.7
  53.5 6.3 %collective-permute-start.9 = (f32[2,1,128,128]{3,2,1,0:T(8,128)S(1)}, f32[2,1,128,128]{3,2,1,0:T(8,128)S(1)}, u32[]{:S(2)}, u32[]{:S(2)}) collective-permute-start(f32[2,1,128,128]{3,2,1,0:T(8,128)S(1)} %get-tuple-element.59), channel_id=1, source_target_pairs={{0,1},{1,2},{2,3},{3,4},{4,5},{5,6},{6,7},{7,8},{8,9},{9,10},{10,1... | collective-permute-start | bytes 393224 | tf_op jit(solution)/shard_map/ppermute | solution.py:24
  61.0 2.6 fusion.121
  63.7 4.6 collective-permute-start.10
  69.6 3.9 collective-permute-done.11
  77.1 6.1 %collective-permute-start.13 = (f32[2,1,128,128]{3,2,1,0:T(8,128)S(1)}, f32[2,1,128,128]{3,2,1,0:T(8,128)S(1)}, u32[]{:S(2)}, u32[]{:S(2)}) collective-permute-start(f32[2,1,128,128]{3,2,1,0:T(8,128)S(1)} %get-tuple-element.55), channel_id=1, source_target_pairs={{0,1},{1,2},{2,3},{3,4},{4,5},{5,6},{6,7},{7,8},{8,9},{9,10},{10,1... | collective-permute-start | bytes 393224 | tf_op jit(solution)/shard_map/ppermute | solution.py:24
  84.7 2.6 fusion.87
  88.1 4.6 collective-permute-start.14
  95.2 4.3 all-to-all-start
  100.1 3.3 multiply_divide_fusion.1
  103.5 1.4 fusion.103
  107.7 5.5 %collective-permute-start.17 = (f32[2,1,128,128]{3,2,1,0:T(8,128)}, f32[2,1,128,128]{3,2,1,0:T(8,128)S(1)}, u32[]{:S(2)}, u32[]{:S(2)}) collective-permute-start(f32[2,1,128,128]{3,2,1,0:T(8,128)} %get-tuple-element.51), channel_id=1, source_target_pairs={{0,1},{1,2},{2,3},{3,4},{4,5},{5,6},{6,7},{7,8},{8,9},{9,10},{10,1... | collective-permute-start | bytes 393224 | tf_op jit(solution)/shard_map/ppermute | solution.py:24
  115.8 1.7 select_maximum_fusion.6
  117.5 3.7 fusion.53
  121.2 4.0 collective-permute-start.18
  125.2 1.7 collective-permute-start.19
  127.0 6.7 %collective-permute-done.19 = f32[2,1,128,128]{3,2,1,0:T(8,128)S(1)} collective-permute-done((f32[2,1,128,128]{3,2,1,0:T(8,128)S(1)}, f32[2,1,128,128]{3,2,1,0:T(8,128)S(1)}, u32[]{:S(2)}, u32[]{:S(2)}) %collective-permute-start.19) | collective-permute-done | bytes 131104 | tf_op jit(solution)/shard_map/ppermute | solution.py:26
  137.2 7.6 %collective-permute-start.21 = (f32[2,1,128,128]{3,2,1,0:T(8,128)S(1)}, f32[2,1,128,128]{3,2,1,0:T(8,128)S(1)}, u32[]{:S(2)}, u32[]{:S(2)}) collective-permute-start(f32[2,1,128,128]{3,2,1,0:T(8,128)S(1)} %get-tuple-element.47), channel_id=1, source_target_pairs={{0,1},{1,2},{2,3},{3,4},{4,5},{5,6},{6,7},{7,8},{8,9},{9,10},{10,1... | collective-permute-start | bytes 393224 | tf_op jit(solution)/shard_map/ppermute | solution.py:24
  146.3 2.7 fusion.19
  149.9 8.1 %collective-permute-start.22 = (f32[2,1,128,128]{3,2,1,0:T(8,128)}, f32[2,1,128,128]{3,2,1,0:T(8,128)}, u32[]{:S(2)}, u32[]{:S(2)}) collective-permute-start(f32[2,1,128,128]{3,2,1,0:T(8,128)} %get-tuple-element.44), channel_id=1, source_target_pairs={{0,1},{1,2},{2,3},{3,4},{4,5},{5,6},{6,7},{7,8},{8,9},{9,10},{10,1... | collective-permute-start | bytes 393224 | tf_op jit(solution)/shard_map/ppermute | solution.py:24
  160.9 2.1 copy.33
  163.0 1.4 collective-permute-done.23
  164.4 2.1 pad_multiply_fusion
  167.8 16.7 %copy.27 = f32[2,4,128,128]{0,3,2,1:T(8,128)} copy(f32[2,4,128,128]{3,2,1,0:T(8,128)S(1)} %fusion.35) | data formatting | bytes 1048576 | tf_op jit(solution)/shard_map/div | solution.py:81
  184.5 24.7 %gather_fusion = f32[4096,2]{1,0:T(8,128)} fusion(f32[2,65536]{0,1:T(8,128)} %bitcast.85, s32[4096]{0:T(1024)S(1)} %broadcast_clamp_fusion), kind=kCustom, calls=%fused_computation | custom fusion | bytes 81920 | tf_op jit(solution)/shard_map/jit(_take)/gather | solution.py:128
  209.1 4.3 fusion.1
  213.4 139.6 %psum.7 = f32[2,512]{0,1:T(8,128)S(1)} all-reduce(f32[2,512]{0,1:T(8,128)S(1)} %bitcast.96), channel_id=1, replica_groups=mesh['mem'=4,'space'=32] {'space'}, use_global_device_ids=true, to_apply=%region_2.3 | all-reduce | flops 1024 | bytes 8192 | tf_op jit(solution)/shard_map/psum | solution.py:130
  353.1 12.6 %all-gather = f32[4,2,512]{2,1,0:T(2,128)S(1)} all-gather(f32[1,2,512]{2,1,0:T(2,128)S(1)} %copy.30), channel_id=1, replica_groups=mesh['mem'=4,'space'=32] {'mem'}, dimensions={0}, use_global_device_ids=true | all-gather | bytes 20480 | tf_op jit(solution)/shard_map/all_gather | solution.py:131
  367.4 11.7 %cholesky.103 = f32[128,128]{1,0:T(8,128)S(1)} custom-call(f32[128,128]{1,0:T(8,128)S(1)} %cholesky.263), custom_call_target="Cholesky" | custom-call | tf_op jit(solution)/shard_map/jit(cholesky)/cholesky | solution.py:137
  379.3 9.8 %custom-call.32 = f32[1,128,128]{1,2,0:T(8,128)S(1)} custom-call(f32[1,128,128]{2,1,0:T(8,128)S(1)} %get-tuple-element.77), custom_call_target="InvertDiagBlocksLowerTriangular" | custom-call | tf_op jit(solution)/shard_map/jit(cholesky)/cholesky | solution.py:137
  389.8 11.7 %cholesky.215 = f32[128,128]{1,0:T(8,128)S(1)} custom-call(f32[128,128]{1,0:T(8,128)S(1)} %cholesky.267), custom_call_target="Cholesky" | custom-call | tf_op jit(solution)/shard_map/jit(cholesky)/cholesky | solution.py:137
  401.5 10.0 %custom-call.33 = f32[1,128,128]{1,2,0:T(8,128)S(1)} custom-call(f32[1,128,128]{2,1,0:T(8,128)S(1)} %get-tuple-element.74), custom_call_target="InvertDiagBlocksLowerTriangular" | custom-call | tf_op jit(solution)/shard_map/jit(cholesky)/cholesky | solution.py:137
  412.2 11.7 %cholesky.236 = f32[128,128]{1,0:T(8,128)S(1)} custom-call(f32[128,128]{1,0:T(8,128)S(1)} %cholesky.272), custom_call_target="Cholesky" | custom-call | tf_op jit(solution)/shard_map/jit(cholesky)/cholesky | solution.py:137
  424.6 9.8 %custom-call.34 = f32[1,128,128]{1,2,0:T(8,128)S(1)} custom-call(f32[1,128,128]{2,1,0:T(8,128)S(1)} %get-tuple-element.71), custom_call_target="InvertDiagBlocksLowerTriangular" | custom-call | tf_op jit(solution)/shard_map/jit(cholesky)/cholesky | solution.py:137
  435.0 11.9 %cholesky.253 = f32[128,128]{1,0:T(8,128)S(1)} custom-call(f32[128,128]{1,0:T(8,128)S(1)} %convolution_subtract_fusion.2), custom_call_target="Cholesky" | custom-call | tf_op jit(solution)/shard_map/jit(cholesky)/cholesky | solution.py:137
  451.0 10.5 %while.2 = (s32[]{:T(128)}, f32[512,512]{1,0:T(8,128)S(1)}, s32[4,2]{0,1:T(2,128)S(1)}, f32[4,128,128]{2,1,0:T(8,128)}) while((s32[]{:T(128)}, f32[512,512]{1,0:T(8,128)S(1)}, s32[4,2]{0,1:T(2,128)S(1)}, f32[4,128,128]{2,1,0:T(8,128)}) %tuple.55), condition=%wide.while_cond.clone, body=%wide.while_body.sunk.clone | while | flops 2 | bytes 132697 | solution.py:139
  451.7 2.0 bitcast_dynamic-update-slice_fusion.3
  454.3 2.0 bitcast_dynamic-update-slice_fusion.3
  456.9 2.0 bitcast_dynamic-update-slice_fusion.3
  459.6 2.0 bitcast_dynamic-update-slice_fusion.3
  461.5 40.1 %custom-call.35 = f32[4,128,128]{1,2,0:T(8,128)S(1)} custom-call(f32[4,128,128]{2,1,0:T(8,128)} %get-tuple-element.12), custom_call_target="InvertDiagBlocksLowerTriangular" | custom-call | tf_op jit(solution)/shard_map/triangular_solve | solution.py:139
  (180 shorter events, 60.7 us)
Async XLA Ops:
  0.0 2.2 copy-start.14
  2.2 3.5 copy-start.22
  2.2 3.5 copy-start.24
  3.0 3.8 collective-permute-start
  4.3 6.0 %collective-permute-start.1 = (f32[3,2,1,128,128]{4,3,2,1,0:T(8,128)S(1)}, f32[3,2,1,128,128]{4,3,2,1,0:T(8,128)}, u32[]{:S(2)}, u32[]{:S(2)}) collective-permute-start(f32[3,2,1,128,128]{4,3,2,1,0:T(8,128)S(1)} %get-tuple-element.31), channel_id=1, source_target_pairs={{1,0},{2,1},{3,2},{4,3},{5,4},{6,5},{7,6},{8,7},{9,8},{10,9},{11,1... | collective-permute-start | bytes 1179656 | tf_op jit(solution)/shard_map/ppermute | solution.py:26
  15.4 9.2 %collective-permute-start.2 = (f32[2,1,128,128]{3,2,1,0:T(8,128)S(1)}, f32[2,1,128,128]{3,2,1,0:T(8,128)S(1)}, u32[]{:S(2)}, u32[]{:S(2)}) collective-permute-start(f32[2,1,128,128]{3,2,1,0:T(8,128)S(1)} %get-tuple-element.64), channel_id=1, source_target_pairs={{0,1},{1,2},{2,3},{3,4},{4,5},{5,6},{6,7},{7,8},{8,9},{9,10},{10,1... | collective-permute-start | bytes 393224 | tf_op jit(solution)/shard_map/ppermute | solution.py:24
  23.2 3.2 collective-permute-start.3
  28.6 7.2 %collective-permute-start.4 = (f32[2,1,128,128]{3,2,1,0:T(8,128)S(1)}, f32[2,1,128,128]{3,2,1,0:T(8,128)S(1)}, u32[]{:S(2)}, u32[]{:S(2)}) collective-permute-start(f32[2,1,128,128]{3,2,1,0:T(8,128)S(1)} %get-tuple-element.62), channel_id=1, source_target_pairs={{1,0},{2,1},{3,2},{4,3},{5,4},{6,5},{7,6},{8,7},{9,8},{10,9},{11,1... | collective-permute-start | bytes 393224 | tf_op jit(solution)/shard_map/ppermute | solution.py:26
  29.9 6.8 %collective-permute-start.5 = (f32[2,1,128,128]{3,2,1,0:T(8,128)S(1)}, f32[2,1,128,128]{3,2,1,0:T(8,128)S(1)}, u32[]{:S(2)}, u32[]{:S(2)}) collective-permute-start(f32[2,1,128,128]{3,2,1,0:T(8,128)S(1)} %get-tuple-element.63), channel_id=1, source_target_pairs={{0,1},{1,2},{2,3},{3,4},{4,5},{5,6},{6,7},{7,8},{8,9},{9,10},{10,1... | collective-permute-start | bytes 393224 | tf_op jit(solution)/shard_map/ppermute | solution.py:24
  40.0 5.9 %collective-permute-start.6 = (f32[2,1,128,128]{3,2,1,0:T(8,128)S(1)}, f32[2,1,128,128]{3,2,1,0:T(8,128)S(1)}, u32[]{:S(2)}, u32[]{:S(2)}) collective-permute-start(f32[2,1,128,128]{3,2,1,0:T(8,128)S(1)} %get-tuple-element.60), channel_id=1, source_target_pairs={{0,1},{1,2},{2,3},{3,4},{4,5},{5,6},{6,7},{7,8},{8,9},{9,10},{10,1... | collective-permute-start | bytes 393224 | tf_op jit(solution)/shard_map/ppermute | solution.py:24
  44.7 5.2 %collective-permute-start.7 = (f32[2,1,128,128]{3,2,1,0:T(8,128)S(1)}, f32[2,1,128,128]{3,2,1,0:T(8,128)S(1)}, u32[]{:S(2)}, u32[]{:S(2)}) collective-permute-start(f32[2,1,128,128]{3,2,1,0:T(8,128)S(1)} %get-tuple-element.61), channel_id=1, source_target_pairs={{1,0},{2,1},{3,2},{4,3},{5,4},{6,5},{7,6},{8,7},{9,8},{10,9},{11,1... | collective-permute-start | bytes 393224 | tf_op jit(solution)/shard_map/ppermute | solution.py:26
  52.2 7.6 %collective-permute-start.8 = (f32[2,1,128,128]{3,2,1,0:T(8,128)S(1)}, f32[2,1,128,128]{3,2,1,0:T(8,128)S(1)}, u32[]{:S(2)}, u32[]{:S(2)}) collective-permute-start(f32[2,1,128,128]{3,2,1,0:T(8,128)S(1)} %get-tuple-element.58), channel_id=1, source_target_pairs={{1,0},{2,1},{3,2},{4,3},{5,4},{6,5},{7,6},{8,7},{9,8},{10,9},{11,1... | collective-permute-start | bytes 393224 | tf_op jit(solution)/shard_map/ppermute | solution.py:26
  53.5 7.1 %collective-permute-start.9 = (f32[2,1,128,128]{3,2,1,0:T(8,128)S(1)}, f32[2,1,128,128]{3,2,1,0:T(8,128)S(1)}, u32[]{:S(2)}, u32[]{:S(2)}) collective-permute-start(f32[2,1,128,128]{3,2,1,0:T(8,128)S(1)} %get-tuple-element.59), channel_id=1, source_target_pairs={{0,1},{1,2},{2,3},{3,4},{4,5},{5,6},{6,7},{7,8},{8,9},{9,10},{10,1... | collective-permute-start | bytes 393224 | tf_op jit(solution)/shard_map/ppermute | solution.py:24
  63.7 5.9 %collective-permute-start.10 = (f32[2,1,128,128]{3,2,1,0:T(8,128)S(1)}, f32[2,1,128,128]{3,2,1,0:T(8,128)S(1)}, u32[]{:S(2)}, u32[]{:S(2)}) collective-permute-start(f32[2,1,128,128]{3,2,1,0:T(8,128)S(1)} %get-tuple-element.56), channel_id=1, source_target_pairs={{0,1},{1,2},{2,3},{3,4},{4,5},{5,6},{6,7},{7,8},{8,9},{9,10},{10,1... | collective-permute-start | bytes 393224 | tf_op jit(solution)/shard_map/ppermute | solution.py:24
  68.3 5.2 %collective-permute-start.11 = (f32[2,1,128,128]{3,2,1,0:T(8,128)S(1)}, f32[2,1,128,128]{3,2,1,0:T(8,128)S(1)}, u32[]{:S(2)}, u32[]{:S(2)}) collective-permute-start(f32[2,1,128,128]{3,2,1,0:T(8,128)S(1)} %get-tuple-element.57), channel_id=1, source_target_pairs={{1,0},{2,1},{3,2},{4,3},{5,4},{6,5},{7,6},{8,7},{9,8},{10,9},{11,1... | collective-permute-start | bytes 393224 | tf_op jit(solution)/shard_map/ppermute | solution.py:26
  75.8 11.6 %copy-start.5 = (f32[2,4,128,128]{3,2,1,0:T(8,128)}, f32[2,4,128,128]{3,2,1,0:T(8,128)S(1)}, u32[]{:S(2)}) copy-start(f32[2,4,128,128]{3,2,1,0:T(8,128)S(1)} %fusion.137) | copy-start | bytes 1572868
  75.8 7.4 %collective-permute-start.12 = (f32[2,1,128,128]{3,2,1,0:T(8,128)S(1)}, f32[2,1,128,128]{3,2,1,0:T(8,128)S(1)}, u32[]{:S(2)}, u32[]{:S(2)}) collective-permute-start(f32[2,1,128,128]{3,2,1,0:T(8,128)S(1)} %get-tuple-element.54), channel_id=1, source_target_pairs={{1,0},{2,1},{3,2},{4,3},{5,4},{6,5},{7,6},{8,7},{9,8},{10,9},{11,1... | collective-permute-start | bytes 393224 | tf_op jit(solution)/shard_map/ppermute | solution.py:26
  77.1 7.1 %collective-permute-start.13 = (f32[2,1,128,128]{3,2,1,0:T(8,128)S(1)}, f32[2,1,128,128]{3,2,1,0:T(8,128)S(1)}, u32[]{:S(2)}, u32[]{:S(2)}) collective-permute-start(f32[2,1,128,128]{3,2,1,0:T(8,128)S(1)} %get-tuple-element.55), channel_id=1, source_target_pairs={{0,1},{1,2},{2,3},{3,4},{4,5},{5,6},{6,7},{7,8},{8,9},{9,10},{10,1... | collective-permute-start | bytes 393224 | tf_op jit(solution)/shard_map/ppermute | solution.py:24
  84.7 2.7 copy-start
  84.7 9.4 %copy-start.11 = (f32[2,4,128,128]{3,2,1,0:T(8,128)S(1)}, f32[2,4,128,128]{3,2,1,0:T(8,128)}, u32[]{:S(2)}) copy-start(f32[2,4,128,128]{3,2,1,0:T(8,128)} %param.10) | copy-start | bytes 1572868
  88.1 11.3 %collective-permute-start.14 = (f32[2,1,128,128]{3,2,1,0:T(8,128)S(1)}, f32[2,1,128,128]{3,2,1,0:T(8,128)S(1)}, u32[]{:S(2)}, u32[]{:S(2)}) collective-permute-start(f32[2,1,128,128]{3,2,1,0:T(8,128)S(1)} %get-tuple-element.52), channel_id=1, source_target_pairs={{0,1},{1,2},{2,3},{3,4},{4,5},{5,6},{6,7},{7,8},{8,9},{9,10},{10,1... | collective-permute-start | bytes 393224 | tf_op jit(solution)/shard_map/ppermute | solution.py:24
  92.7 7.4 %collective-permute-start.15 = (f32[2,1,128,128]{3,2,1,0:T(8,128)S(1)}, f32[2,1,128,128]{3,2,1,0:T(8,128)}, u32[]{:S(2)}, u32[]{:S(2)}) collective-permute-start(f32[2,1,128,128]{3,2,1,0:T(8,128)S(1)} %get-tuple-element.53), channel_id=1, source_target_pairs={{1,0},{2,1},{3,2},{4,3},{5,4},{6,5},{7,6},{8,7},{9,8},{10,9},{11,1... | collective-permute-start | bytes 393224 | tf_op jit(solution)/shard_map/ppermute | solution.py:26
  95.2 65.7 %all-to-all-start = ((f32[2,4,128,128]{3,1,0,2:T(4,128)}), f32[2,4,128,128]{3,1,0,2:T(4,128)}, u32[]{:S(2)}, u32[]{:S(2)}) async-start(f32[2,4,128,128]{3,1,0,2:T(4,128)} %copy.32), calls=%async_computation | async-start | bytes 1048576 | tf_op jit(solution)/shard_map/all_to_all | solution.py:144
  99.5 4.0 copy-start.1
  99.5 4.0 copy-start.6
  103.5 9.7 %copy-start.17 = (s32[512,8]{0,1:T(8,128)S(1)}, s32[512,8]{0,1:T(8,128)}, u32[]{:S(2)}) copy-start(s32[512,8]{0,1:T(8,128)} %param.15) | copy-start | bytes 49156
  104.9 0.8 copy-start.7
  106.4 9.4 %collective-permute-start.16 = (f32[2,1,128,128]{3,2,1,0:T(8,128)}, f32[2,1,128,128]{3,2,1,0:T(8,128)S(1)}, u32[]{:S(2)}, u32[]{:S(2)}) collective-permute-start(f32[2,1,128,128]{3,2,1,0:T(8,128)} %get-tuple-element.50), channel_id=1, source_target_pairs={{1,0},{2,1},{3,2},{4,3},{5,4},{6,5},{7,6},{8,7},{9,8},{10,9},{11,1... | collective-permute-start | bytes 393224 | tf_op jit(solution)/shard_map/ppermute | solution.py:26
  107.7 8.1 %collective-permute-start.17 = (f32[2,1,128,128]{3,2,1,0:T(8,128)}, f32[2,1,128,128]{3,2,1,0:T(8,128)S(1)}, u32[]{:S(2)}, u32[]{:S(2)}) collective-permute-start(f32[2,1,128,128]{3,2,1,0:T(8,128)} %get-tuple-element.51), channel_id=1, source_target_pairs={{0,1},{1,2},{2,3},{3,4},{4,5},{5,6},{6,7},{7,8},{8,9},{9,10},{10,1... | collective-permute-start | bytes 393224 | tf_op jit(solution)/shard_map/ppermute | solution.py:24
  115.7 1.7 copy-start.2
  115.8 1.7 copy-start.8
  117.5 9.4 %copy-start.19 = (f32[512,8]{0,1:T(8,128)S(1)}, f32[512,8]{0,1:T(8,128)}, u32[]{:S(2)}) copy-start(f32[512,8]{0,1:T(8,128)} %param.16) | copy-start | bytes 49156
  121.2 5.7 %collective-permute-start.18 = (f32[2,1,128,128]{3,2,1,0:T(8,128)S(1)}, f32[2,1,128,128]{3,2,1,0:T(8,128)S(1)}, u32[]{:S(2)}, u32[]{:S(2)}) collective-permute-start(f32[2,1,128,128]{3,2,1,0:T(8,128)S(1)} %get-tuple-element.48), channel_id=1, source_target_pairs={{0,1},{1,2},{2,3},{3,4},{4,5},{5,6},{6,7},{7,8},{8,9},{9,10},{10,1... | collective-permute-start | bytes 393224 | tf_op jit(solution)/shard_map/ppermute | solution.py:24
  125.2 8.4 %collective-permute-start.19 = (f32[2,1,128,128]{3,2,1,0:T(8,128)S(1)}, f32[2,1,128,128]{3,2,1,0:T(8,128)S(1)}, u32[]{:S(2)}, u32[]{:S(2)}) collective-permute-start(f32[2,1,128,128]{3,2,1,0:T(8,128)S(1)} %get-tuple-element.49), channel_id=1, source_target_pairs={{1,0},{2,1},{3,2},{4,3},{5,4},{6,5},{7,6},{8,7},{9,8},{10,9},{11,1... | collective-permute-start | bytes 393224 | tf_op jit(solution)/shard_map/ppermute | solution.py:26
  135.9 13.1 %copy-start.3 = (f32[2,4,128,128]{3,2,1,0:T(8,128)}, f32[2,4,128,128]{3,2,1,0:T(8,128)S(1)}, u32[]{:S(2)}) copy-start(f32[2,4,128,128]{3,2,1,0:T(8,128)S(1)} %fusion.69) | copy-start | bytes 1572868
  135.9 8.9 %collective-permute-start.20 = (f32[2,1,128,128]{3,2,1,0:T(8,128)S(1)}, f32[2,1,128,128]{3,2,1,0:T(8,128)S(1)}, u32[]{:S(2)}, u32[]{:S(2)}) collective-permute-start(f32[2,1,128,128]{3,2,1,0:T(8,128)S(1)} %get-tuple-element.46), channel_id=1, source_target_pairs={{1,0},{2,1},{3,2},{4,3},{5,4},{6,5},{7,6},{8,7},{9,8},{10,9},{11,1... | collective-permute-start | bytes 393224 | tf_op jit(solution)/shard_map/ppermute | solution.py:26
  137.2 8.5 %collective-permute-start.21 = (f32[2,1,128,128]{3,2,1,0:T(8,128)S(1)}, f32[2,1,128,128]{3,2,1,0:T(8,128)S(1)}, u32[]{:S(2)}, u32[]{:S(2)}) collective-permute-start(f32[2,1,128,128]{3,2,1,0:T(8,128)S(1)} %get-tuple-element.47), channel_id=1, source_target_pairs={{0,1},{1,2},{2,3},{3,4},{4,5},{5,6},{6,7},{7,8},{8,9},{9,10},{10,1... | collective-permute-start | bytes 393224 | tf_op jit(solution)/shard_map/ppermute | solution.py:24
  146.3 13.0 %copy-start.18 = (f32[512]{0:T(512)S(1)}, f32[512]{0:T(512)}, u32[]{:S(2)}) copy-start(f32[512]{0:T(512)} %param.18) | copy-start | bytes 6148
  146.3 13.0 %copy-start.20 = (pred[512,8]{0,1:T(8,128)(4,1)S(1)}, pred[512,8]{0,1:T(8,128)(4,1)}, u32[]{:S(2)}) copy-start(pred[512,8]{0,1:T(8,128)(4,1)} %get-tuple-element.21) | copy-start | bytes 12292
  149.0 0.9 copy-start.10
  149.9 13.1 %collective-permute-start.22 = (f32[2,1,128,128]{3,2,1,0:T(8,128)}, f32[2,1,128,128]{3,2,1,0:T(8,128)}, u32[]{:S(2)}, u32[]{:S(2)}) collective-permute-start(f32[2,1,128,128]{3,2,1,0:T(8,128)} %get-tuple-element.44), channel_id=1, source_target_pairs={{0,1},{1,2},{2,3},{3,4},{4,5},{5,6},{6,7},{7,8},{8,9},{9,10},{10,1... | collective-permute-start | bytes 393224 | tf_op jit(solution)/shard_map/ppermute | solution.py:24
  158.0 6.4 %collective-permute-start.23 = (f32[2,1,128,128]{3,2,1,0:T(8,128)}, f32[2,1,128,128]{3,2,1,0:T(8,128)}, u32[]{:S(2)}, u32[]{:S(2)}) collective-permute-start(f32[2,1,128,128]{3,2,1,0:T(8,128)} %get-tuple-element.45), channel_id=1, source_target_pairs={{1,0},{2,1},{3,2},{4,3},{5,4},{6,5},{7,6},{8,7},{9,8},{10,9},{11,1... | collective-permute-start | bytes 393224 | tf_op jit(solution)/shard_map/ppermute | solution.py:26
  163.0 3.4 copy-start.4
  184.4 24.7 %copy-start.13 = (f32[512,8]{1,0:T(8,128)S(1)}, f32[512,8]{1,0:T(8,128)}, u32[]{:S(2)}) copy-start(f32[512,8]{1,0:T(8,128)} %copy.29) | copy-start | bytes 49156
  184.4 24.7 %copy-start.15 = (pred[512,8]{1,0:T(8,128)(4,1)S(1)}, pred[512,8]{1,0:T(8,128)(4,1)}, u32[]{:S(2)}) copy-start(pred[512,8]{1,0:T(8,128)(4,1)} %copy.26) | copy-start | bytes 12292
  434.6 67.1 %copy-start.21 = (f32[8,512]{1,0:T(8,128)S(1)}, f32[8,512]{1,0:T(8,128)}, u32[]{:S(2)}) copy-start(f32[8,512]{1,0:T(8,128)} %param.19) | copy-start | bytes 49156
  434.6 67.1 %copy-start.23 = (f32[512]{0:T(512)S(1)}, f32[512]{0:T(512)}, u32[]{:S(2)}) copy-start(f32[512]{0:T(512)} %param.17) | copy-start | bytes 6148
  451.0 53.9 %copy-start.12 = (f32[2,4,4,32,128]{4,0,2,3,1:T(2,128)S(1)}, f32[2,4,4,32,128]{4,0,2,3,1:T(2,128)}, u32[]{:S(2)}) copy-start(f32[2,4,4,32,128]{4,0,2,3,1:T(2,128)} %copy.33) | copy-start | bytes 1572868
  (2 other events, 1.5 us)
where the time goes:
time: 516 us; the launch traced here: 507 us
  other arithmetic  166 us (32%)
  blocking collectives  152 us (29%)
  starting transfers between devices  86.5 us (17%)
  local copies, waits for them, and re-layouts  66.6 us (13%)
  waiting for transfers between devices  24.8 us (5%)
  matrix products  6.63 us (1%)
    psum x1, blocking collectives, body(): summed = lax.psum(partial_value, 'space')  140 us
    another operation x14, other arithmetic, body(): factor = jnp.linalg.cholesky(cov)  78.8 us
    ppermute x12, starting transfers between devices, padded(): lax.ppermute(tail, axis, [(i, (i + 1) % count) for i in range(ends)])  66.4 us
    another operation x3, other arithmetic, body(): lax.linalg.triangular_solve(factor, half, left_side=True, lower=True, tra...  40.2 us
    gather x1, local copies, waits for them, and re-layouts, body(): picked = jnp.take(flat, jnp.where(valid, local, 0), axis=1)  24.7 us
    ppermute x12, waiting for transfers between devices, padded(): lax.ppermute(head, axis, [((i + 1) % count, i) for i in range(ends)])  21.2 us
    min x6, other arithmetic, saturate(): return jnp.clip(middle(sat_pad) + time_step * (water - outflow), 0.0, 1.0)  16.8 us
    div x1, local copies, waits for them, and re-layouts, pressure(): return numer / denom  16.7 us
  transfers between devices with their start and end apart: 25, of which 10 were waited for; matrix products, arithmetic and copies ran while one was open for 5% of the time, Pallas kernels for 0%

commit v1 on v0

v1 whole, which is shorter than its diff:
```python
import functools

import jax
import jax.numpy as jnp
from jax import lax
from jax.experimental import pallas as pl
from jax.experimental.pallas import tpu as pltpu
from jax.sharding import PartitionSpec as P


INFLATION = 4.0
STEP = 0.1
PAD = 8
CHUNK = 32
HIGH = lax.Precision.HIGHEST
ANY = pl.BlockSpec(memory_space=pl.ANY)
SMEM = pl.BlockSpec(memory_space=pltpu.SMEM)
VMEM = pl.BlockSpec(memory_space=pltpu.VMEM)

S0, P0, S1, P1, S2, L2 = (0, 1), (2, 3, 4), (5, 6, 7), (8, 9, 10), 11, 12
PLANES = 13


def spot(row):
    return row + 1 + (row >= 4)


class Tile:
    def __init__(self, lam_a, lam_b, frac_a, frac_b, p_a, p_b, s_a, s_b, perm, q, ny, cut):
        self.lam = (lam_a, lam_b)
        self.frac = (frac_a, frac_b)
        self.p = (p_a, p_b)
        self.s = (s_a, s_b)
        self.perm = perm
        self.q = q
        self.ny = ny
        self.cut = cut

    def clear(self):
        for ref in self.lam + self.frac + self.p:
            wide = ref.shape[2]
            edge = jnp.zeros((PAD, wide), jnp.float32)

            def one(r, carry, ref=ref, edge=edge):
                ref[r, 0:PAD, :] = edge
                ref[r, PAD + self.ny : PAD + self.ny + PAD, :] = edge
                return carry

            lax.fori_loop(0, ref.shape[0], one, 0)
            ref[5, :, :] = jnp.zeros(ref.shape[1:], jnp.float32)

    def rows(self, first, last, fn):
        def one(row, carry):
            far = row >= 4
            st = row + 1 + far.astype(jnp.int32)
            joined = 1 - self.cut
            up = st + 1 + jnp.where(row == 3, joined, 0)
            down = st - 1 - jnp.where(row == 4, joined, 0)
            for y0 in range(0, self.ny, CHUNK):
                fn(row, st, up, down, y0)
            return carry

        lax.fori_loop(first, last + 1, one, 0)

    def props(self, level, first, last):
        def fn(row, st, up, down, y0):
            inner = pl.ds(y0, CHUNK)
            sat = self.s[level][st, inner, :]
            lam, frac = props(self.perm[row, inner, :], sat)
            self.lam[level][st, pl.ds(PAD + y0, CHUNK), :] = lam
            self.frac[level][st, pl.ds(PAD + y0, CHUNK), :] = frac

        self.rows(first, last, fn)

    def saturate(self, level, first, last):
        lam_r, frac_r, p_r = self.lam[level], self.frac[level], self.p[level]
        new = 1 - level
        lanes = lam_r.shape[2]
        lane = lax.broadcasted_iota(jnp.int32, (CHUNK, lanes), 1)
        is_first, is_last = lane == 0, lane == lanes - 1

        def fn(row, st, up, down, y0):
            inner = pl.ds(PAD + y0, CHUNK)
            lam, frac, press = lam_r[st, inner, :], frac_r[st, inner, :], p_r[st, inner, :]

            def face(index, where):
                flux = (lam + lam_r[index, where, :]) * (press - p_r[index, where, :])
                return flux * jnp.where(flux > 0.0, frac, frac_r[index, where, :])

            out = face(up, inner) + face(down, inner)
            out = out + face(st, pl.ds(PAD + y0 + 1, CHUNK))
            out = out + face(st, pl.ds(PAD + y0 - 1, CHUNK))
            flux = (lam + pltpu.roll(lam, lanes - 1, 1)) * (press - pltpu.roll(press, lanes - 1, 1))
            moved = flux * jnp.where(flux > 0.0, frac, pltpu.roll(frac, lanes - 1, 1))
            edge = jnp.maximum(lam * press, 0.0) * frac
            out = out + jnp.where(is_last, edge, moved)
            out = out + jnp.where(is_first, edge, pltpu.roll(-moved, 1, 1))
            q = self.q[row, pl.ds(y0, CHUNK), :]
            water = jnp.maximum(q, 0.0) + jnp.minimum(q, 0.0) * frac
            sat = self.s[level][st, pl.ds(y0, CHUNK), :]
            sat = jnp.clip(sat + STEP * (water - out), 0.0, 1.0)
            self.s[new][st, pl.ds(y0, CHUNK), :] = sat
            lam, frac = props(self.perm[row, pl.ds(y0, CHUNK), :], sat)
            self.lam[new][st, inner, :] = lam
            self.frac[new][st, inner, :] = frac

        self.rows(first, last, fn)

    def pressure(self, level, first, last):
        new = 1 - level
        lam_r, p_r, out_r = self.lam[new], self.p[level], self.p[new]
        lanes = lam_r.shape[2]
        lane = lax.broadcasted_iota(jnp.int32, (CHUNK, lanes), 1)
        not_first, not_last = lane > 0, lane < lanes - 1

        def fn(row, st, up, down, y0):
            inner = pl.ds(PAD + y0, CHUNK)
            lam, press = lam_r[st, inner, :], p_r[st, inner, :]
            numer = press + self.q[row, pl.ds(y0, CHUNK), :]
            denom = jnp.ones_like(lam)
            for index, where in (
                (up, inner),
                (down, inner),
                (st, pl.ds(PAD + y0 + 1, CHUNK)),
                (st, pl.ds(PAD + y0 - 1, CHUNK)),
            ):
                trans = lam + lam_r[index, where, :]
                numer = numer + trans * p_r[index, where, :]
                denom = denom + trans
            for shift, mask in ((lanes - 1, not_last), (1, not_first)):
                trans = lam + jnp.where(mask, pltpu.roll(lam, shift, 1), 0.0)
                numer = numer + trans * jnp.where(mask, pltpu.roll(press, shift, 1), 0.0)
                denom = denom + trans
            out_r[st, inner, :] = numer / denom

        self.rows(first, last, fn)

    def expand(self):
        self.props(0, 2, 5)
        self.props(1, 0, 2)
        self.props(1, 5, 7)
        self.saturate(0, 3, 4)
        self.pressure(0, 2, 5)
        self.saturate(1, 1, 6)
        self.pressure(1, 0, 7)

    def shrink(self):
        self.saturate(0, 1, 6)
        self.pressure(0, 2, 5)
        self.saturate(1, 3, 4)


def props(perm_half, sat):
    water = sat * sat
    oil = (1.0 - sat) * (1.0 - sat) * 0.25
    total = water + oil
    return perm_half * total, water / total


def tile_scratch(ny, nz):
    tall = ny + 2 * PAD
    wide = [pltpu.VMEM((11, tall, nz), jnp.float32) for _ in range(6)]
    flat = [pltpu.VMEM((11, ny, nz), jnp.float32) for _ in range(2)]
    own = [pltpu.VMEM((8, ny, nz), jnp.float32) for _ in range(2)]
    return wide + flat + own


def issue(pairs, sems, first):
    copies = []
    for n, (src, dst) in enumerate(pairs):
        copy = pltpu.make_async_copy(src, dst, sems.at[first + n])
        copy.start()
        copies.append(copy)
    return copies


def drain(copies):
    for copy in copies:
        copy.wait()


def beyond(tile, row):
    return jnp.where(tile.cut == 1, 5, spot(row))


def give_early(tile, keep, send, send_early):
    pairs = []
    inner = pl.ds(PAD, tile.ny)
    for d in range(2):
        pairs.append((tile.s[0].at[spot(d)], keep.at[S0[d]]))
    for d in range(3):
        pairs.append((tile.p[0].at[spot(d), inner], keep.at[P0[d]]))
    if send_early:
        for d in range(2):
            pairs.append((tile.s[0].at[spot(7 - d)], send.at[S0[d]]))
        for d in range(3):
            pairs.append((tile.p[0].at[spot(7 - d), inner], send.at[P0[d]]))
    return pairs


def give_late(tile, out, near, base):
    row, step = near
    inner = pl.ds(PAD, tile.ny)
    pairs = []
    for n, d in enumerate((1, 2, 3)):
        pairs.append((tile.s[1].at[spot(row + step * d)], out.at[S1[n] - base]))
    for n, d in enumerate((2, 3, 4)):
        st = beyond(tile, row + step * d) if d == 4 else spot(row + step * d)
        pairs.append((tile.p[1].at[st, inner], out.at[P1[n] - base]))
    return pairs


def give_last(tile, out, near, base):
    row, step = near
    inner = pl.ds(PAD, tile.ny)
    return [
        (tile.s[0].at[spot(row + step * 3)], out.at[S2 - base]),
        (tile.lam[0].at[beyond(tile, row + step * 4), inner], out.at[L2 - base]),
    ]


def take_side(tile, src, early, late, base_row, step):
    del src
    inner = pl.ds(PAD, tile.ny)
    pairs = []
    for d in range(2):
        pairs.append((early(S0[d]), tile.s[0].at[base_row + step * d]))
    for d in range(3):
        pairs.append((early(P0[d]), tile.p[0].at[base_row + step * d, inner]))
    for n, d in enumerate((1, 2, 3)):
        pairs.append((late(S1[n]), tile.s[1].at[base_row + step * d]))
    for n, d in enumerate((2, 3, 4)):
        pairs.append((late(P1[n]), tile.p[1].at[base_row + step * d, inner]))
    return pairs


def take_last(tile, late, base_row, step):
    inner = pl.ds(PAD, tile.ny)
    return [
        (late(S2), tile.s[0].at[base_row + step * 3]),
        (late(L2), tile.lam[0].at[base_row + step * 4, inner]),
    ]


def advance(tile, keep, send, sems, first, send_early):
    base = 0 if send_early else S1[0]
    early = issue(give_early(tile, keep, send, send_early), sems, first)
    first += len(early)
    tile.saturate(0, 1, 6)
    tile.pressure(0, 2, 5)
    late = issue(
        give_late(tile, send, (7, -1), base) + give_late(tile, keep, (0, 1), 0), sems, first
    )
    first += len(late)
    drain(early)
    tile.saturate(1, 3, 4)
    last = issue(
        give_last(tile, send, (7, -1), base) + give_last(tile, keep, (0, 1), 0), sems, first
    )
    drain(late)
    drain(last)


def first_kernel(flags, own_log, own_sat, own_press, swapped, q, keep, send, perm_out, *refs):
    tile = Tile(*refs[:10], own_log.shape[1], jnp.int32(0))
    raw, sems = refs[10], refs[11]
    odd = flags[0]
    inner = pl.ds(PAD, tile.ny)

    def place(n):
        return jnp.where(odd == 1, 3 - n, n)

    pairs = [(own_log, raw.at[pl.ds(0, 4)]), (swapped.at[pl.ds(0, 4)], raw.at[pl.ds(4, 4)])]
    pairs.append((q, tile.q))
    for n in range(4):
        pairs.append((own_sat.at[place(n)], tile.s[0].at[spot(n)]))
        pairs.append((own_press.at[place(n)], tile.p[0].at[spot(n), inner]))
        pairs.append((swapped.at[4 + place(n)], tile.s[0].at[spot(4 + n)]))
        pairs.append((swapped.at[8 + place(n)], tile.p[0].at[spot(4 + n), inner]))
    copies = issue(pairs, sems, 0)
    tile.clear()
    drain(copies)

    def halve(row, carry):
        at = row - (row & 3) + place(row & 3)
        for y0 in range(0, tile.ny, CHUNK):
            tile.perm[row, pl.ds(y0, CHUNK), :] = 0.5 * jnp.exp(raw[at, pl.ds(y0, CHUNK), :])
        return carry

    lax.fori_loop(0, 8, halve, 0)
    perm_copy = issue([(tile.perm, perm_out)], sems, len(pairs))
    tile.props(0, 0, 7)
    advance(tile, keep, send, sems, len(pairs) + 1, False)
    drain(perm_copy)


def second_kernel(flags, kept, raw_in, late_in, perm_own, q, keep, send, perm_out, *refs):
    tile = Tile(*refs[:10], kept.shape[1], flags[1])
    raw, sems = refs[10], refs[11]
    odd = flags[0]

    def place(n, count):
        return jnp.where(odd == 1, n, count - 1 - n)

    def early(plane):
        if plane in S0:
            return raw_in.at[4 + place(plane, 2)]
        return raw_in.at[6 + place(plane - 2, 3)]

    pairs = [(raw_in.at[pl.ds(0, 4)], raw), (q, tile.q)]
    for d in range(4):
        pairs.append((perm_own.at[d], tile.perm.at[3 - d]))
    pairs += take_side(tile, None, lambda n: kept.at[n], lambda n: kept.at[n], 4, -1)
    pairs += take_side(tile, None, early, lambda n: late_in.at[n - S1[0]], 6, 1)
    last = take_last(tile, lambda n: kept.at[n], 4, -1)
    last += take_last(tile, lambda n: late_in.at[n - S1[0]], 6, 1)
    copies = issue(pairs, sems, 0)
    tile.clear()
    drain(copies)

    def halve(d, carry):
        for y0 in range(0, tile.ny, CHUNK):
            where = pl.ds(y0, CHUNK)
            tile.perm[4 + d, where, :] = 0.5 * jnp.exp(raw[place(d, 4), where, :])
        return carry

    lax.fori_loop(0, 4, halve, 0)
    first = len(pairs)
    perm_copy = issue([(tile.perm, perm_out)], sems, first)
    first = fill(tile, last, sems, first + 1)
    advance(tile, keep, send, sems, first, True)
    drain(perm_copy)


def fill(tile, last, sems, first):
    tile.props(0, 2, 5)
    tile.props(1, 0, 2)
    tile.props(1, 5, 7)
    tile.saturate(0, 3, 4)
    tile.pressure(0, 2, 5)
    copies = issue(last, sems, first)
    drain(copies)
    tile.props(0, 0, 0)
    tile.props(0, 7, 7)
    tile.saturate(1, 1, 6)
    tile.pressure(1, 0, 7)
    return first + len(copies)


def load_both(tile, kept, got, perm, q, sems):
    pairs = [(perm, tile.perm), (q, tile.q)]
    pairs += take_side(tile, None, lambda n: kept.at[n], lambda n: kept.at[n], 4, -1)
    pairs += take_side(tile, None, lambda n: got.at[n], lambda n: got.at[n], 6, 1)
    last = take_last(tile, lambda n: kept.at[n], 4, -1)
    last += take_last(tile, lambda n: got.at[n], 6, 1)
    copies = issue(pairs, sems, 0)
    tile.clear()
    drain(copies)
    return fill(tile, last, sems, len(pairs))


def third_kernel(flags, kept, got, perm, q, keep, send, *refs):
    tile = Tile(*refs[:10], kept.shape[1], jnp.int32(0))
    first = load_both(tile, kept, got, perm, q, refs[10])
    advance(tile, keep, send, refs[10], first, True)


def last_kernel(flags, index, weight, kept, got, perm, q, values, *refs):
    tile = Tile(*refs[:10], kept.shape[1], flags[1])
    sems, picked = refs[10], refs[11]
    load_both(tile, kept, got, perm, q, sems)
    odd, offset = flags[0], flags[2]
    lanes = kept.shape[2]
    lane = lax.broadcasted_iota(jnp.int32, (1, lanes), 1)
    picked[...] = jnp.zeros_like(picked)
    count = index.shape[0] // 8

    def one(n, carry):
        slot = n & 7
        row = jnp.where(odd == 1, slot, 7 - slot)
        st = row + 1 + (row >= 4).astype(jnp.int32)
        total = jnp.zeros((1, lanes), jnp.float32)
        for t in range(8):
            cell = index[n * 8 + t]
            y = lax.shift_right_logical(cell, 7) & (tile.ny - 1)
            values_row = tile.p[0][st, pl.ds(PAD + y, 1), :]
            total = total + jnp.where(lane == (cell & (lanes - 1)), values_row, 0.0) * weight[n * 8 + t]
        picked[pl.ds(offset + n, 1), :] = total
        return carry

    lax.fori_loop(0, count, one, 0)
    ones = jnp.ones((values.shape[0], lanes), jnp.float32)
    values[...] = lax.dot_general(
        ones, picked[...], (((1,), (1,)), ((), ())), precision=HIGH, preferred_element_type=jnp.float32
    )


def source_kernel(flags, wells, rate, whole, edge):
    ny, nz = whole.shape[1], whole.shape[2]
    odd, chip = flags[0], flags[3]
    lane = lax.broadcasted_iota(jnp.int32, (1, nz), 1)
    whole[...] = jnp.zeros_like(whole)
    edge[...] = jnp.zeros_like(edge)
    total = flags[4]

    def one(n, carry):
        cell = wells[n]
        x = lax.shift_right_logical(cell, 14)
        y = lax.shift_right_logical(cell, 7) & (ny - 1)
        add = jnp.where(lane == (cell & (nz - 1)), rate[n], 0.0)
        behind = jnp.where(odd == 1, chip * 8 + 11 - x, x - chip * 8 + 4) & (total - 1)
        inside = behind - 4

        @pl.when((inside >= 0) & (inside < 8))
        def _():
            where = (inside, pl.ds(y, 1), slice(None))
            whole[where] = whole[where] + add

        @pl.when(behind < 8)
        def _():
            where = (7 - behind, pl.ds(y, 1), slice(None))
            edge[where] = edge[where] + add

        return carry

    lax.fori_loop(0, wells.shape[0], one, 0)


def solve_kernel(values, obs, var, noise, columns, out, coef):
    groups = obs.shape[0]
    ens = noise.shape[1]
    half = ens // 2
    spaces = groups * 8
    parts = []
    for g in range(groups):
        sides = []
        for core in range(2):
            total = None
            for near in range(4):
                chip = (4 * g + near - core) % (4 * groups)
                row = values[pl.ds(2 * chip + core, half, stride=spaces), :]
                total = row if total is None else total + row
            sides.append(total)
        parts.append(jnp.concatenate(sides, axis=0))
    small = jnp.zeros((ens, ens), jnp.float32)
    right = jnp.zeros((ens, ens), jnp.float32)
    dims = (((1,), (1,)), ((), ()))
    for g in range(groups):
        predicted = parts[g]
        dev = predicted - jnp.mean(predicted, axis=0, keepdims=True)
        spread = INFLATION * var[pl.ds(g, 1), :]
        resid = obs[pl.ds(g, 1), :] + jnp.sqrt(spread) * noise[g] - predicted
        scaled = dev / spread
        small = small + lax.dot_general(
            scaled, dev, dims, precision=HIGH, preferred_element_type=jnp.float32
        )
        right = right + lax.dot_general(
            scaled, resid, dims, precision=HIGH, preferred_element_type=jnp.float32
        )
    row = lax.broadcasted_iota(jnp.int32, (ens, ens), 0)
    col = lax.broadcasted_iota(jnp.int32, (ens, ens), 1)
    left = small + jnp.where(row == col, ens - 1.0, 0.0)
    for k in range(ens):
        pivot = left[k : k + 1, k : k + 1]
        left_row = left[k : k + 1, :] / pivot
        right_row = right[k : k + 1, :] / pivot
        factor = left[:, k : k + 1]
        here = row == k
        left = jnp.where(here, left_row, left - factor * left_row)
        right = jnp.where(here, right_row, right - factor * right_row)
    mixing = right - jnp.mean(right, axis=0, keepdims=True) + jnp.where(row == col, 1.0, 0.0)
    rows, wide = columns.shape[2], columns.shape[3]

    def natural(place):
        return 2 * place if place < half else 2 * (place - half) + 1

    for j in range(ens):
        for m in range(ens):
            at = natural(j) * ens + natural(m)
            coef[at] = jnp.broadcast_to(mixing[j : j + 1, m : m + 1], (8, wide))

    def one(n, carry):
        part = [columns[j, n] for j in range(ens)]
        for m in range(ens):
            for r0 in range(0, rows, 8):
                total = coef[m] * part[0][r0 : r0 + 8]
                for j in range(1, ens):
                    total = total + coef[j * ens + m] * part[j][r0 : r0 + 8]
                out[m, n, r0 : r0 + 8, :] = total
        return carry

    lax.fori_loop(0, columns.shape[1], one, 0)


def body(
    log_perm,
    saturation,
    pressure_init,
    wells,
    well_rate,
    obs_index,
    obs_weight,
    obs_value,
    obs_var,
    noise,
):
    width, ny, nz = log_perm.shape[1:]
    spaces = lax.axis_size("space")
    mems = lax.axis_size("mem")
    place = lax.axis_index("space")
    odd = place % 2
    chip = place // 2
    chips = spaces // 2
    rows = spaces * width
    around = (chip + odd) % chips
    cut = jnp.where(odd == 1, chip == chips - 1, chip == 0).astype(jnp.int32)
    per = obs_index.shape[0] // rows
    slots = 8 * per
    flags = jnp.stack([odd, cut, (around % 4) * slots, chip, jnp.int32(rows)]).astype(jnp.int32)

    def take(field, start, size):
        return lax.dynamic_slice_in_dim(field, start, size, axis=0)

    other = take(log_perm, 1 - odd, 1)[0]
    mine = take(log_perm, odd, 1)[0]
    swap_out = jnp.concatenate([other, saturation, pressure_init])
    edge_out = jnp.concatenate([other, take(saturation, odd * 2, 2), take(pressure_init, odd, 3)])
    swapped = lax.ppermute(swap_out, "space", [(i, i ^ 1) for i in range(spaces)])
    edge_in = lax.ppermute(
        edge_out,
        "space",
        [(i, (i + 1) % spaces if i % 2 else (i - 1) % spaces) for i in range(spaces)],
    )
    plane = functools.partial(jax.ShapeDtypeStruct, dtype=jnp.float32)
    grid = (ny, nz)
    sems = pltpu.SemaphoreType.DMA((96,))
    q_tile, q_edge = pl.pallas_call(
        source_kernel,
        out_shape=(plane((8,) + grid), plane((8,) + grid)),
        in_specs=[SMEM, SMEM, SMEM],
        out_specs=(VMEM, VMEM),
        name="sources",
    )(flags, wells, well_rate)
    keep, send, perm_tile = pl.pallas_call(
        first_kernel,
        out_shape=(plane((PLANES,) + grid), plane((8,) + grid), plane((8,) + grid)),
        in_specs=[SMEM] + [ANY] * 5,
        out_specs=(ANY,) * 3,
        scratch_shapes=tile_scratch(ny, nz) + [pltpu.VMEM((8,) + grid, jnp.float32), sems],
        name="first",
    )(flags, mine, saturation, pressure_init, swapped, q_tile)
    onward = [(i, (i + (-2 if i % 2 else 2)) % spaces) for i in range(spaces)]
    back = [(b, a) for a, b in onward]
    got = lax.ppermute(send, "space", onward)
    keep, send, perm_edge = pl.pallas_call(
        second_kernel,
        out_shape=(plane((PLANES,) + grid), plane((PLANES,) + grid), plane((8,) + grid)),
        in_specs=[SMEM] + [ANY] * 5,
        out_specs=(ANY,) * 3,
        scratch_shapes=tile_scratch(ny, nz) + [pltpu.VMEM((4,) + grid, jnp.float32), sems],
        name="second",
    )(flags, keep, edge_in, got, perm_tile, q_edge)
    got = lax.ppermute(send, "space", back)
    keep, send = pl.pallas_call(
        third_kernel,
        out_shape=(plane((PLANES,) + grid), plane((PLANES,) + grid)),
        in_specs=[SMEM] + [ANY] * 4,
        out_specs=(ANY,) * 2,
        scratch_shapes=tile_scratch(ny, nz) + [sems],
        name="third",
    )(flags, keep, got, perm_tile, q_tile)
    got = lax.ppermute(send, "space", onward)

    def local(table):
        table = jnp.roll(table.reshape(per, rows, -1), 4, axis=1)
        return lax.dynamic_slice_in_dim(table, around * 8, 8, axis=1).reshape(-1)

    devices = mems * spaces
    values = pl.pallas_call(
        last_kernel,
        out_shape=plane((devices, nz)),
        in_specs=[SMEM] * 3 + [ANY] * 4,
        out_specs=VMEM,
        scratch_shapes=tile_scratch(ny, nz) + [sems, pltpu.VMEM((nz, nz), jnp.float32)],
        name="last",
    )(flags, local(obs_index), local(obs_weight), keep, got, perm_edge, q_edge)
    values = lax.all_to_all(
        values.reshape(devices, 1, nz), ("mem", "space"), 0, 0, tiled=True
    ).reshape(devices, nz)

    def ordered(table):
        table = jnp.roll(table.reshape(-1, per, rows), 4, axis=2)
        table = table.reshape(-1, per, chips // 4, 4, 8).transpose(2, 0, 3, 1, 4)
        return table.reshape(chips // 4, -1, 4 * slots)

    columns = lax.all_to_all(log_perm, "mem", split_axis=2, concat_axis=0, tiled=True)
    mixed_noise = ordered(jnp.concatenate([noise[0::2], noise[1::2]]))
    return pl.pallas_call(
        solve_kernel,
        out_shape=plane(columns.shape),
        in_specs=[VMEM] * 5,
        out_specs=VMEM,
        scratch_shapes=[pltpu.VMEM((noise.shape[0] ** 2, 8, nz), jnp.float32)],
        name="solve",
    )(values, ordered(obs_value)[:, 0], ordered(obs_var)[:, 0], mixed_noise, columns)


def solution(mesh):
    placed = (
        P("mem", "space", None, None),
        P("space", None, None),
        P("space", None, None),
        P(),
        P(),
        P(),
        P(),
        P(),
        P(),
        P(),
    )
    return jax.shard_map(
        body, mesh=mesh, in_specs=placed, out_specs=P(None, "space", "mem", None), check_vma=False
    )
```

time: 516 us -> 116 us (0.22); the launches traced: 507 us -> 115 us
  other arithmetic: 166 us -> 0.49 us
  blocking collectives: 152 us -> 0 us
  starting transfers between devices: 86.5 us -> 16.8 us
  local copies, waits for them, and re-layouts: 66.6 us -> 14.9 us
  Pallas kernels: 0 us -> 44.7 us
  waiting for transfers between devices: 24.8 us -> 38.2 us
  matrix products: 6.63 us -> 0 us
    psum x1 -> x0, blocking collectives: 140 us -> none  [body(): summed = lax.psum(partial_value, 'space')]
    another operation x18 -> x0, other arithmetic: 119 us -> none  [the longest x14 78.8 us: body(): factor = jnp.linalg.cholesky(cov)]
    ppermute x24 -> x5, starting transfers between devices: 82.2 us -> 7.06 us  [the longest x1 6.76 us: body(): lax.ppermute(edge_out, 'space', [(i, (i + 1) % spaces if i % 2 else (i -...]
    pallas_call x0 -> x6, Pallas kernels: none -> 44.7 us  [the longest x1 11.2 us: body(): pl.pallas_call(third_kernel, out_shape=(plane((PLANES,) + grid), plane((P...]
    gather x1 -> x0, local copies, waits for them, and re-layouts: 24.7 us -> none  [body(): picked = jnp.take(flat, jnp.where(valid, local, 0), axis=1)]
    div x2 -> x0, local copies, waits for them, and re-layouts: 17 us -> none  [the longest x1 16.7 us: pressure(): return numer / denom]
    min x6 -> x0, other arithmetic: 16.8 us -> none  [saturate(): return jnp.clip(middle(sat_pad) + time_step * (water - outflow), 0.0, 1.0)]
    div x14 -> x0, other arithmetic: 15.2 us -> none  [the longest x6 7.72 us: pressure(): return numer / denom]
  transfers between devices with their start and end apart: 25 -> 7, of which waited for: 10 -> 4; matrix products, arithmetic and copies ran while one was open for 5% -> 7% of each run, Pallas kernels for 0% -> 17%
where the time goes in v1:
time: 116 us; the launch traced here: 115 us
  Pallas kernels  44.7 us (39%)
  waiting for transfers between devices  38.2 us (33%)
  starting transfers between devices  16.8 us (14%)
  local copies, waits for them, and re-layouts  14.9 us (13%)
    ppermute x2, waiting for transfers between devices, body(): got = lax.ppermute(send, 'space', onward)  17.6 us
    ppermute x1, waiting for transfers between devices, body(): got = lax.ppermute(send, 'space', back)  12.9 us
    pallas_call x1, Pallas kernels, body(): pl.pallas_call(third_kernel, out_shape=(plane((PLANES,) + grid), plane((P...  11.2 us
    pallas_call x1, Pallas kernels, body(): pl.pallas_call(second_kernel, out_shape=(plane((PLANES,) + grid), plane((...  11.1 us
    pallas_call x1, Pallas kernels, body(): pl.pallas_call(last_kernel, out_shape=plane((devices, nz)), in_specs=[SME...  9.59 us
    all_to_all x1, waiting for transfers between devices, body(): lax.all_to_all(values.reshape(devices, 1, nz), ('mem', 'space'), 0, 0, ti...  7.72 us
    ppermute x1, starting transfers between devices, body(): lax.ppermute(edge_out, 'space', [(i, (i + 1) % spaces if i % 2 else (i -...  6.76 us
    unnamed x29, local copies, waits for them, and re-layouts  6.59 us
  transfers between devices with their start and end apart: 7, of which 4 were waited for; matrix products, arithmetic and copies ran while one was open for 7% of the time, Pallas kernels for 17%

profile of v1, /device:TPU:0, one launch (start us, length us, event | category | flops | bytes accessed | tf_op | source)
XLA Modules:
  0.0 115.4 jit_solution(15115964807733478330)
XLA Ops:
  0.0 1.8 %dynamic-slice_bitcast_fusion = (f32[4,128,128]{2,1,0:T(8,128)S(1)}, f32[4,128,128]{2,1,0:T(8,128)}) fusion(f32[2,4,128,128]{3,2,1,0:T(8,128)} %param.10, s32[]{:T(128)S(6)} %select_n.46, s32[]{:T(128)S(6)} %select_n.45), kind=kLoop, calls=%fused_computation.2 | loop fusion | bytes 1048584 | tf_op jit(solution)/shard_map/squeeze | solution.py:524
  1.9 0.1 collective-permute-start
  2.1 6.8 %collective-permute-start.1 = (f32[9,128,128]{2,1,0:T(8,128)S(1)}, f32[9,128,128]{2,1,0:T(8,128)S(1)}, u32[]{:S(2)}, u32[]{:S(2)}) collective-permute-start(f32[9,128,128]{2,1,0:T(8,128)S(1)} %pad_maximum_fusion.1), channel_id=1, source_target_pairs={{0,31},{1,2},{2,1},{3,4},{4,3},{5,6},{6,5},{7,8},{8,7},{9,10},{10,... | collective-permute-start | bytes 1769480 | tf_op jit(solution)/shard_map/ppermute | solution.py:529
  8.9 0.7 stack.23.flags
  9.5 3.2 %sources.1 = (f32[8,128,128]{2,1,0:T(8,128)}, f32[8,128,128]{2,1,0:T(8,128)}) custom-call(s32[5]{0:T(128)} %stack.23.flags, s32[64]{0:T(128)} %wells.1, f32[64]{0:T(128)} %rate.1), custom_call_target="tpu_custom_call" | custom-call | tf_op jit(solution)/shard_map/sources/pallas_call | solution.py:537
  12.8 0.9 copy-done.5
  13.7 6.5 %first.1 = (f32[13,128,128]{2,1,0:T(8,128)}, f32[8,128,128]{2,1,0:T(8,128)}, f32[8,128,128]{2,1,0:T(8,128)}) custom-call(s32[5]{0:T(128)} %stack.23.flags, f32[4,128,128]{2,1,0:T(8,128)} %get-tuple-element.26.own_log, f32[4,128,128]{2,1,0:T(8,128)} %own_sat.1, f32[4,128,128]{2,1,0:T(8,128)} %own_press.1, f32[12,128,128]{2,1,0:T(8,128)} %copy-done.5, ...), custom_call_target="tpu_custom_call" | custom-call | tf_op jit(solution)/shard_map/first/pallas_call | solution.py:544
  20.2 0.1 collective-permute-start.2
  20.3 12.7 %collective-permute-done.2.late_in = f32[8,128,128]{2,1,0:T(8,128)S(1)} collective-permute-done((f32[8,128,128]{2,1,0:T(8,128)}, f32[8,128,128]{2,1,0:T(8,128)S(1)}, u32[]{:S(2)}, u32[]{:S(2)}) %collective-permute-start.2) | collective-permute-done | bytes 524320 | tf_op jit(solution)/shard_map/ppermute | solution.py:554
  32.9 0.8 copy-done.7
  33.7 11.1 %second.1 = (f32[13,128,128]{2,1,0:T(8,128)}, f32[13,128,128]{2,1,0:T(8,128)}, f32[8,128,128]{2,1,0:T(8,128)}) custom-call(s32[5]{0:T(128)} %stack.23.flags, f32[13,128,128]{2,1,0:T(8,128)} %get-tuple-element.16.kept, f32[9,128,128]{2,1,0:T(8,128)} %copy-done.6, f32[8,128,128]{2,1,0:T(8,128)} %copy-done.7, f32[8,128,128]{2,1,0:T(8,128)} %get-tuple-element.18.perm_own.perm, ...), custom_call_target="tpu_custom_call" | custom-call | tf_op jit(solution)/shard_map/second/pallas_call | solution.py:555
  44.8 0.1 collective-permute-start.3
  44.9 12.9 %collective-permute-done.3.got = f32[13,128,128]{2,1,0:T(8,128)S(1)} collective-permute-done((f32[13,128,128]{2,1,0:T(8,128)}, f32[13,128,128]{2,1,0:T(8,128)S(1)}, u32[]{:S(2)}, u32[]{:S(2)}) %collective-permute-start.3) | collective-permute-done | bytes 852000 | tf_op jit(solution)/shard_map/ppermute | solution.py:563
  57.8 0.9 copy-done.3
  58.7 11.2 %third.1 = (f32[13,128,128]{2,1,0:T(8,128)}, f32[13,128,128]{2,1,0:T(8,128)}) custom-call(s32[5]{0:T(128)} %stack.23.flags, f32[13,128,128]{2,1,0:T(8,128)} %get-tuple-element.20.kept, f32[13,128,128]{2,1,0:T(8,128)} %copy-done.3, f32[8,128,128]{2,1,0:T(8,128)} %get-tuple-element.18.perm_own.perm, f32[8,128,128]{2,1,0:T(8,128)} %get-tuple-element.15.q), custom_call_target="tpu_custom_call" | custom-call | tf_op jit(solution)/shard_map/third/pallas_call | solution.py:564
  69.9 0.1 collective-permute-start.4
  70.0 1.1 copy.26
  71.1 4.4 %all-to-all-start.1 = ((f32[2,4,128,128]{3,1,0,2:T(4,128)}), f32[2,4,128,128]{3,1,0,2:T(4,128)S(1)}, u32[]{:S(2)}, u32[]{:S(2)}) async-start(f32[2,4,128,128]{3,1,0,2:T(4,128)} %copy.26), calls=%async_computation.1 | async-start | bytes 1048576 | tf_op jit(solution)/shard_map/all_to_all | solution.py:596
  75.5 0.1 slice.56
  75.6 0.6 copy-done.10
  76.2 0.1 slice.58
  76.3 0.1 dynamic-slice_add_fusion
  76.4 0.1 dynamic-slice_maximum_fusion
  76.5 0.6 copy-done.11
  77.2 0.1 copy.20
  77.2 0.7 reshape.40.index
  78.0 0.7 reshape.42.weight
  78.6 0.1 slice.60
  78.7 0.1 pad_maximum_fusion.2
  78.8 0.3 reshape.50
  79.2 0.2 copy.25
  79.4 0.8 reshape.51.noise
  80.2 0.1 slice.48
  80.3 0.1 pad_maximum_fusion.3
  80.3 0.1 reshape.46
  80.5 0.7 squeeze_reshape.6.obs
  81.2 0.1 slice.50
  81.2 4.9 %collective-permute-done.4.got = f32[13,128,128]{2,1,0:T(8,128)S(1)} collective-permute-done((f32[13,128,128]{2,1,0:T(8,128)}, f32[13,128,128]{2,1,0:T(8,128)S(1)}, u32[]{:S(2)}, u32[]{:S(2)}) %collective-permute-start.4) | collective-permute-done | bytes 852000 | tf_op jit(solution)/shard_map/ppermute | solution.py:572
  86.2 0.9 copy-done.4
  87.1 9.6 %last.1 = f32[128,128]{1,0:T(8,128)} custom-call(s32[5]{0:T(128)} %stack.23.flags, s32[256]{0:T(256)} %reshape.40.index, f32[256]{0:T(256)} %reshape.42.weight, f32[13,128,128]{2,1,0:T(8,128)} %get-tuple-element.22.kept, f32[13,128,128]{2,1,0:T(8,128)} %copy-done.4, f32[8,128,128]{2,1,0:T(8,128)} %get-tuple-element.24.perm, f32[8,128,128]{2,1,0:T(8,128)} %get-tuple-element.19.q), custom_call_target="tpu_custom_call" | custom-call | tf_op jit(solution)/shard_map/last/pallas_call | solution.py:579
  96.7 5.3 %all-to-all-start = ((f32[128,1,128]{2,1,0:T(1,128)}), f32[128,1,128]{2,1,0:T(1,128)S(1)}, u32[]{:S(2)}, u32[]{:S(2)}) async-start(f32[128,1,128]{2,1,0:T(1,128)} %bitcast.39), calls=%async_computation | async-start | bytes 131072 | tf_op jit(solution)/shard_map/all_to_all | solution.py:587
  102.0 0.1 pad_maximum_fusion.4
  102.1 0.1 reshape.48
  102.2 0.7 squeeze_reshape.7.var
  102.9 0.9 copy.27
  103.8 7.7 %all-to-all-done = f32[128,1,128]{2,1,0:T(1,128)S(1)} async-done(((f32[128,1,128]{2,1,0:T(1,128)}), f32[128,1,128]{2,1,0:T(1,128)S(1)}, u32[]{:S(2)}, u32[]{:S(2)}) %all-to-all-start) | async-done | bytes 65568 | tf_op jit(solution)/shard_map/all_to_all | solution.py:587
  111.5 0.6 copy-done.8
  112.2 3.2 %solve.1 = f32[8,4,32,128]{3,2,1,0:T(8,128)} custom-call(f32[128,128]{1,0:T(8,128)} %bitcast.40, f32[4,128]{1,0:T(4,128)} %squeeze_reshape.6.obs, f32[4,128]{1,0:T(4,128)} %squeeze_reshape.7.var, f32[4,8,128]{2,1,0:T(8,128)} %reshape.51.noise, f32[8,4,32,128]{3,2,1,0:T(8,128)} %bitcast.37), custom_call_target="tpu_custom_call" | custom-call | tf_op jit(solution)/shard_map/solve/pallas_call | solution.py:598
  (34 shorter events, 0.3 us)
Async XLA Ops:
  0.0 1.8 %copy-start.1 = (f32[4,128,128]{2,1,0:T(8,128)S(1)}, f32[4,128,128]{2,1,0:T(8,128)}, u32[]{:S(2)}) copy-start(f32[4,128,128]{2,1,0:T(8,128)} %own_press.1) | copy-start | bytes 786436
  0.0 1.8 %copy-start.2 = (f32[4,128,128]{2,1,0:T(8,128)S(1)}, f32[4,128,128]{2,1,0:T(8,128)}, u32[]{:S(2)}) copy-start(f32[4,128,128]{2,1,0:T(8,128)} %own_sat.1) | copy-start | bytes 786436
  1.9 10.9 %collective-permute-start = (f32[12,128,128]{2,1,0:T(8,128)S(1)}, f32[12,128,128]{2,1,0:T(8,128)S(1)}, u32[]{:S(2)}, u32[]{:S(2)}) collective-permute-start(f32[12,128,128]{2,1,0:T(8,128)S(1)} %pad_maximum_fusion), channel_id=1, source_target_pairs={{0,1},{1,0},{2,3},{3,2},{4,5},{5,4},{6,7},{7,6},{8,9},{9,8},{10,11... | collective-permute-start | bytes 2359304 | tf_op jit(solution)/shard_map/ppermute | solution.py:528
  2.1 18.1 %collective-permute-start.1 = (f32[9,128,128]{2,1,0:T(8,128)S(1)}, f32[9,128,128]{2,1,0:T(8,128)S(1)}, u32[]{:S(2)}, u32[]{:S(2)}) collective-permute-start(f32[9,128,128]{2,1,0:T(8,128)S(1)} %pad_maximum_fusion.1), channel_id=1, source_target_pairs={{0,31},{1,2},{2,1},{3,4},{4,3},{5,6},{6,5},{7,8},{8,7},{9,10},{10,... | collective-permute-start | bytes 1769480 | tf_op jit(solution)/shard_map/ppermute | solution.py:529
  12.8 0.9 copy-start.5
  20.2 12.8 %collective-permute-start.2 = (f32[8,128,128]{2,1,0:T(8,128)}, f32[8,128,128]{2,1,0:T(8,128)S(1)}, u32[]{:S(2)}, u32[]{:S(2)}) collective-permute-start(f32[8,128,128]{2,1,0:T(8,128)} %get-tuple-element.17), channel_id=1, source_target_pairs={{0,2},{1,31},{2,4},{3,1},{4,6},{5,3},{6,8},{7,5},{8,10},{9,7},{10,... | collective-permute-start | bytes 1572872 | tf_op jit(solution)/shard_map/ppermute | solution.py:554
  20.3 12.7 %copy-start.6 = (f32[9,128,128]{2,1,0:T(8,128)}, f32[9,128,128]{2,1,0:T(8,128)S(1)}, u32[]{:S(2)}) copy-start(f32[9,128,128]{2,1,0:T(8,128)S(1)} %collective-permute-done.1.raw_in) | copy-start | bytes 1769476
  32.9 0.8 copy-start.7
  44.8 13.0 %collective-permute-start.3 = (f32[13,128,128]{2,1,0:T(8,128)}, f32[13,128,128]{2,1,0:T(8,128)S(1)}, u32[]{:S(2)}, u32[]{:S(2)}) collective-permute-start(f32[13,128,128]{2,1,0:T(8,128)} %get-tuple-element.21), channel_id=1, source_target_pairs={{2,0},{31,1},{4,2},{1,3},{6,4},{3,5},{8,6},{5,7},{10,8},{7,9},{12,... | collective-permute-start | bytes 2555912 | tf_op jit(solution)/shard_map/ppermute | solution.py:563
  57.8 0.9 copy-start.3
  58.7 11.3 %copy-start = (f32[2,4,128,128]{3,2,1,0:T(8,128)S(1)}, f32[2,4,128,128]{3,2,1,0:T(8,128)}, u32[]{:S(2)}) copy-start(f32[2,4,128,128]{3,2,1,0:T(8,128)} %param.10) | copy-start | bytes 1572868
  69.9 16.3 %collective-permute-start.4 = (f32[13,128,128]{2,1,0:T(8,128)}, f32[13,128,128]{2,1,0:T(8,128)S(1)}, u32[]{:S(2)}, u32[]{:S(2)}) collective-permute-start(f32[13,128,128]{2,1,0:T(8,128)} %get-tuple-element.23), channel_id=1, source_target_pairs={{0,2},{1,31},{2,4},{3,1},{4,6},{5,3},{6,8},{7,5},{8,10},{9,7},{10,... | collective-permute-start | bytes 2555912 | tf_op jit(solution)/shard_map/ppermute | solution.py:572
  71.1 4.4 %copy-start.9 = (s32[512,8]{0,1:T(8,128)S(1)}, s32[512,8]{0,1:T(8,128)}, u32[]{:S(2)}) copy-start(s32[512,8]{0,1:T(8,128)} %param.15) | copy-start | bytes 49156
  71.1 25.6 %all-to-all-start.1 = ((f32[2,4,128,128]{3,1,0,2:T(4,128)}), f32[2,4,128,128]{3,1,0,2:T(4,128)S(1)}, u32[]{:S(2)}, u32[]{:S(2)}) async-start(f32[2,4,128,128]{3,1,0,2:T(4,128)} %copy.26), calls=%async_computation.1 | async-start | bytes 1048576 | tf_op jit(solution)/shard_map/all_to_all | solution.py:596
  75.5 0.7 copy-start.10
  76.4 0.7 copy-start.11
  79.3 0.9 copy-start.12
  79.3 1.8 %copy-start.13 = (f32[512]{0:T(512)S(1)}, f32[512]{0:T(512)}, u32[]{:S(2)}) copy-start(f32[512]{0:T(512)} %param.18) | copy-start | bytes 6148
  86.2 0.9 copy-start.4
  96.7 14.9 %all-to-all-start = ((f32[128,1,128]{2,1,0:T(1,128)}), f32[128,1,128]{2,1,0:T(1,128)S(1)}, u32[]{:S(2)}, u32[]{:S(2)}) async-start(f32[128,1,128]{2,1,0:T(1,128)} %bitcast.39), calls=%async_computation | async-start | bytes 131072 | tf_op jit(solution)/shard_map/all_to_all | solution.py:587
  111.5 0.6 copy-start.8

commit v2 on v1

v2 whole, which is shorter than its diff:
```python
import jax
import jax.numpy as jnp
from jax import lax
from jax.experimental import pallas as pl
from jax.experimental.pallas import tpu as pltpu
from jax.sharding import PartitionSpec as P


INFLATION = 4.0
STEP = 0.1
PAD = 8
CHUNK = 32
HIGH = lax.Precision.HIGHEST
FAR = pl.BlockSpec(memory_space=pltpu.HBM)
SMEM = pl.BlockSpec(memory_space=pltpu.SMEM)
VMEM = pl.BlockSpec(memory_space=pltpu.VMEM)

S0, P0, S1, P1, S2, L2 = (0, 1), (2, 3, 4), (5, 6, 7), (8, 9, 10), 11, 12
PLANES = 13
TABLES = 5
PARAMS = pltpu.CompilerParams(vmem_limit_bytes=12 << 20)


def spot(row):
    return row + 1 + (row >= 4)


class Tile:
    def __init__(self, lam_a, lam_b, frac_a, frac_b, p_a, p_b, s_a, s_b, perm, q, q_row, cut):
        self.lam = (lam_a, lam_b)
        self.frac = (frac_a, frac_b)
        self.p = (p_a, p_b)
        self.s = (s_a, s_b)
        self.perm = perm
        self.q = q
        self.q_row = q_row
        self.ny = perm.shape[1]
        self.cut = cut

    def clear(self):
        for ref in self.lam + self.frac + self.p:
            tall, wide = ref.shape[1:]
            edge = jnp.zeros((PAD, wide), jnp.float32)
            for r in range(ref.shape[0]):
                ref[r, 0:PAD, :] = edge
                ref[r, tall - PAD : tall, :] = edge
            ref[5, :, :] = jnp.zeros((tall, wide), jnp.float32)

    def rows(self, first, last, fn):
        def one(row, carry):
            far = row >= 4
            st = row + 1 + far.astype(jnp.int32)
            joined = 1 - self.cut
            up = st + 1 + jnp.where(row == 3, joined, 0)
            down = st - 1 - jnp.where(row == 4, joined, 0)
            for y0 in range(0, self.ny, CHUNK):
                fn(row, st, up, down, y0)
            return carry

        lax.fori_loop(first, last + 1, one, 0)

    def props(self, level, first, last):
        def fn(row, st, up, down, y0):
            inner = pl.ds(y0, CHUNK)
            sat = self.s[level][st, inner, :]
            lam, frac = props(self.perm[row, inner, :], sat)
            self.lam[level][st, pl.ds(PAD + y0, CHUNK), :] = lam
            self.frac[level][st, pl.ds(PAD + y0, CHUNK), :] = frac

        self.rows(first, last, fn)

    def saturate(self, level, first, last):
        lam_r, frac_r, p_r = self.lam[level], self.frac[level], self.p[level]
        new = 1 - level
        lanes = lam_r.shape[2]
        lane = lax.broadcasted_iota(jnp.int32, (CHUNK, lanes), 1)
        is_first, is_last = lane == 0, lane == lanes - 1

        def fn(row, st, up, down, y0):
            inner = pl.ds(PAD + y0, CHUNK)
            lam, frac, press = lam_r[st, inner, :], frac_r[st, inner, :], p_r[st, inner, :]

            def face(index, where):
                flux = (lam + lam_r[index, where, :]) * (press - p_r[index, where, :])
                return flux * jnp.where(flux > 0.0, frac, frac_r[index, where, :])

            out = face(up, inner) + face(down, inner)
            out = out + face(st, pl.ds(PAD + y0 + 1, CHUNK))
            out = out + face(st, pl.ds(PAD + y0 - 1, CHUNK))
            flux = (lam + pltpu.roll(lam, lanes - 1, 1)) * (press - pltpu.roll(press, lanes - 1, 1))
            moved = flux * jnp.where(flux > 0.0, frac, pltpu.roll(frac, lanes - 1, 1))
            edge = jnp.maximum(lam * press, 0.0) * frac
            out = out + jnp.where(is_last, edge, moved)
            out = out + jnp.where(is_first, edge, pltpu.roll(-moved, 1, 1))
            q = self.q[self.q_row(row), pl.ds(y0, CHUNK), :]
            water = q * jnp.where(q > 0.0, 1.0, frac)
            sat = self.s[level][st, pl.ds(y0, CHUNK), :]
            sat = jnp.clip(sat + STEP * (water - out), 0.0, 1.0)
            self.s[new][st, pl.ds(y0, CHUNK), :] = sat
            lam, frac = props(self.perm[row, pl.ds(y0, CHUNK), :], sat)
            self.lam[new][st, inner, :] = lam
            self.frac[new][st, inner, :] = frac

        self.rows(first, last, fn)

    def pressure(self, level, first, last):
        new = 1 - level
        lam_r, p_r, out_r = self.lam[new], self.p[level], self.p[new]
        lanes = lam_r.shape[2]
        lane = lax.broadcasted_iota(jnp.int32, (CHUNK, lanes), 1)
        not_first, not_last = lane > 0, lane < lanes - 1

        def fn(row, st, up, down, y0):
            inner = pl.ds(PAD + y0, CHUNK)
            lam, press = lam_r[st, inner, :], p_r[st, inner, :]
            numer = press + self.q[self.q_row(row), pl.ds(y0, CHUNK), :]
            denom = jnp.ones_like(lam)
            for index, where in (
                (up, inner),
                (down, inner),
                (st, pl.ds(PAD + y0 + 1, CHUNK)),
                (st, pl.ds(PAD + y0 - 1, CHUNK)),
            ):
                trans = lam + lam_r[index, where, :]
                numer = numer + trans * p_r[index, where, :]
                denom = denom + trans
            for shift, mask in ((lanes - 1, not_last), (1, not_first)):
                trans = lam + jnp.where(mask, pltpu.roll(lam, shift, 1), 0.0)
                numer = numer + trans * jnp.where(mask, pltpu.roll(press, shift, 1), 0.0)
                denom = denom + trans
            out_r[st, inner, :] = numer / denom

        self.rows(first, last, fn)


def props(perm_half, sat):
    water = sat * sat
    oil = (1.0 - sat) * (1.0 - sat) * 0.25
    total = water + oil
    return perm_half * total, water / total


def near(array):
    return pltpu.with_memory_space_constraint(array, pltpu.VMEM)


def tile_scratch(ny, nz):
    tall = ny + 2 * PAD
    wide = [pltpu.VMEM((11, tall, nz), jnp.float32) for _ in range(6)]
    flat = [pltpu.VMEM((count, ny, nz), jnp.float32) for count in (11, 11, 13)]
    return wide + flat


def issue(pairs, sems, first):
    copies = []
    for n, (src, dst) in enumerate(pairs):
        copy = pltpu.make_async_copy(src, dst, sems.at[first + n])
        copy.start()
        copies.append(copy)
    return copies


def drain(copies):
    for copy in copies:
        copy.wait()


def beyond(tile, row):
    return jnp.where(tile.cut == 1, 5, spot(row))


def give_early(tile, keep, send, send_early):
    pairs = []
    inner = pl.ds(PAD, tile.ny)
    for d in range(2):
        pairs.append((tile.s[0].at[spot(d)], keep.at[S0[d]]))
    for d in range(3):
        pairs.append((tile.p[0].at[spot(d), inner], keep.at[P0[d]]))
    if send_early:
        for d in range(2):
            pairs.append((tile.s[0].at[spot(7 - d)], send.at[S0[d]]))
        for d in range(3):
            pairs.append((tile.p[0].at[spot(7 - d), inner], send.at[P0[d]]))
    return pairs


def give_late(tile, out, near, base):
    row, step = near
    inner = pl.ds(PAD, tile.ny)
    pairs = []
    for n, d in enumerate((1, 2, 3)):
        pairs.append((tile.s[1].at[spot(row + step * d)], out.at[S1[n] - base]))
    for n, d in enumerate((2, 3, 4)):
        st = beyond(tile, row + step * d) if d == 4 else spot(row + step * d)
        pairs.append((tile.p[1].at[st, inner], out.at[P1[n] - base]))
    return pairs


def give_last(tile, out, near, base):
    row, step = near
    inner = pl.ds(PAD, tile.ny)
    return [
        (tile.s[0].at[spot(row + step * 3)], out.at[S2 - base]),
        (tile.lam[0].at[beyond(tile, row + step * 4), inner], out.at[L2 - base]),
    ]


def take(tile, early, late, base_row, step):
    inner = pl.ds(PAD, tile.ny)
    start, s_next, p_next, last = [], [], [], []
    for d in range(2):
        start.append((early(S0[d]), tile.s[0].at[base_row + step * d]))
    for d in range(3):
        start.append((early(P0[d]), tile.p[0].at[base_row + step * d, inner]))
    for n, d in enumerate((1, 2, 3)):
        s_next.append((late(S1[n]), tile.s[1].at[base_row + step * d]))
    for n, d in enumerate((2, 3, 4)):
        p_next.append((late(P1[n]), tile.p[1].at[base_row + step * d, inner]))
    last.append((late(S2), tile.s[0].at[base_row + step * 3]))
    last.append((late(L2), tile.lam[0].at[base_row + step * 4, inner]))
    return start, s_next, p_next, last


def advance(tile, keep, send, sems, first, send_early):
    base = 0 if send_early else S1[0]
    early = issue(give_early(tile, keep, send, send_early), sems, first)
    first += len(early)
    tile.saturate(0, 1, 6)
    tile.pressure(0, 2, 5)
    late = issue(
        give_late(tile, send, (7, -1), base) + give_late(tile, keep, (0, 1), 0), sems, first
    )
    first += len(late)
    drain(early)
    tile.saturate(1, 3, 4)
    last = issue(
        give_last(tile, send, (7, -1), base) + give_last(tile, keep, (0, 1), 0), sems, first
    )
    drain(late)
    drain(last)


def first_kernel(flags, log_perm, own_sat, own_press, swapped, q, keep, send, perm, *refs):
    tile = Tile(*refs[:8], perm, refs[8], lambda row: row + 4, jnp.int32(0))
    raw, sems = refs[9], refs[10]
    odd = flags[0]
    inner = pl.ds(PAD, tile.ny)

    def place(n):
        return jnp.where(odd == 1, 3 - n, n)

    pairs = [(q, tile.q), (log_perm.at[odd], raw)]
    for n in range(4):
        pairs.append((own_sat.at[place(n)], tile.s[0].at[spot(n)]))
        pairs.append((own_press.at[place(n)], tile.p[0].at[spot(n), inner]))
        pairs.append((swapped.at[4 + place(n)], tile.s[0].at[spot(4 + n)]))
        pairs.append((swapped.at[8 + place(n)], tile.p[0].at[spot(4 + n), inner]))
    copies = issue(pairs, sems, 0)
    tile.clear()

    def halve(n, carry):
        for y0 in range(0, tile.ny, CHUNK):
            where = pl.ds(y0, CHUNK)
            perm[4 + n, where, :] = 0.5 * jnp.exp(swapped[place(n), where, :])
        return carry

    lax.fori_loop(0, 4, halve, 0)
    drain(copies)

    def halve_own(n, carry):
        for y0 in range(0, tile.ny, CHUNK):
            where = pl.ds(y0, CHUNK)
            perm[n, where, :] = 0.5 * jnp.exp(raw[place(n), where, :])
        return carry

    lax.fori_loop(0, 4, halve_own, 0)
    tile.props(0, 0, 7)
    advance(tile, keep, send, sems, len(pairs), False)


def fill(tile, q, sides, sems):
    groups = [sum((side[n] for side in sides), []) for n in range(4)]
    groups[0].append((q, tile.q))
    first, copies = 0, []
    for group in groups[:3]:
        copies.append(issue(group, sems, first))
        first += len(group)
    tile.clear()
    drain(copies[0])
    tile.props(0, 2, 5)
    tile.saturate(0, 3, 4)
    drain(copies[1])
    tile.props(1, 0, 2)
    tile.props(1, 5, 7)
    tile.pressure(0, 2, 5)
    drain(copies[2])
    last = issue(groups[3], sems, first)
    drain(last)
    tile.props(0, 0, 0)
    tile.props(0, 7, 7)
    tile.saturate(1, 1, 6)
    tile.pressure(1, 0, 7)
    return first + len(last)


def edge_q(cut):
    return lambda row: jnp.where((cut == 1) & (row >= 4), row, 7 - row)


def second_kernel(flags, kept, raw_in, late_in, perm_own, q, *refs):
    keep, send, perm = refs[TABLES : TABLES + 3]
    refs = refs[TABLES + 3 :]
    tile = Tile(*refs[:8], perm, refs[8], edge_q(flags[1]), flags[1])
    sems = refs[9]
    straight = flags[0] ^ flags[1]

    def place(n, count):
        return jnp.where(straight == 1, n, count - 1 - n)

    def early(plane):
        if plane in S0:
            return raw_in.at[4 + place(plane, 2)]
        return raw_in.at[6 + place(plane - 2, 3)]

    def permeability(d, carry):
        for y0 in range(0, tile.ny, CHUNK):
            where = pl.ds(y0, CHUNK)
            perm[3 - d, where, :] = perm_own[d, where, :]
            perm[4 + d, where, :] = 0.5 * jnp.exp(raw_in[place(d, 4), where, :])
        return carry

    lax.fori_loop(0, 4, permeability, 0)
    sides = (
        take(tile, lambda n: kept.at[n], lambda n: kept.at[n], 4, -1),
        take(tile, early, lambda n: late_in.at[n - S1[0]], 6, 1),
    )
    first = fill(tile, q, sides, sems)
    advance(tile, keep, send, sems, first, True)


def both_sides(tile, kept, got):
    return (
        take(tile, lambda n: kept.at[n], lambda n: kept.at[n], 4, -1),
        take(tile, lambda n: got.at[n], lambda n: got.at[n], 6, 1),
    )


def third_kernel(flags, kept, got, perm, q, columns, keep, send, *refs):
    del columns
    tile = Tile(*refs[:8], perm, refs[8], lambda row: row + 4, jnp.int32(0))
    first = fill(tile, q, both_sides(tile, kept, got), refs[9])
    advance(tile, keep, send, refs[9], first, True)


def last_kernel(flags, index, weight, kept, got, perm, q, values, *refs):
    tile = Tile(*refs[:8], perm, refs[8], edge_q(flags[1]), flags[1])
    sems, picked = refs[9], refs[10]
    fill(tile, q, both_sides(tile, kept, got), sems)
    odd, cut, offset = flags[0], flags[1], flags[2]
    lanes = kept.shape[2]
    lane = lax.broadcasted_iota(jnp.int32, (1, lanes), 1)
    picked[...] = jnp.zeros_like(picked)
    count = index.shape[0] // 8

    def one(n, carry):
        slot = n & 7
        row = jnp.where(odd == 1, slot, 7 - slot)
        st = row + 1 + (row >= 4).astype(jnp.int32)
        other = cut * (row >= 4).astype(jnp.int32)
        at = n - slot + jnp.where(other == 1, 7 - slot, slot)
        total = jnp.zeros((1, lanes), jnp.float32)
        for t in range(8):
            cell = index[at * 8 + t]
            y = lax.shift_right_logical(cell, 7) & (tile.ny - 1)
            values_row = tile.p[0][st, pl.ds(PAD + y, 1), :]
            total = total + jnp.where(lane == (cell & (lanes - 1)), values_row, 0.0) * weight[at * 8 + t]
        picked[pl.ds(offset + at + other * count, 1), :] = total
        return carry

    lax.fori_loop(0, count, one, 0)
    ones = jnp.ones((values.shape[0], lanes), jnp.float32)
    values[...] = lax.dot_general(
        ones, picked[...], (((1,), (1,)), ((), ())), precision=HIGH, preferred_element_type=jnp.float32
    )


def source_kernel(flags, wells, rate, out, q, sem):
    ny, nz = q.shape[1], q.shape[2]
    odd, chip = flags[0], flags[3]
    last = q.shape[0] - 1
    lane = lax.broadcasted_iota(jnp.int32, (1, nz), 1)
    q[...] = jnp.zeros_like(q)
    total = flags[4]

    def one(n, carry):
        cell = wells[n]
        x = lax.shift_right_logical(cell, 14)
        y = lax.shift_right_logical(cell, 7) & (ny - 1)
        behind = jnp.where(odd == 1, chip * 8 + 11 - x, x - chip * 8 + 4) & (total - 1)
        where = (jnp.minimum(behind, last), pl.ds(y, 1), slice(None))
        q[where] = q[where] + jnp.where(lane == (cell & (nz - 1)), rate[n], 0.0)
        return carry

    lax.fori_loop(0, wells.shape[0], one, 0, unroll=4)
    copy = pltpu.make_async_copy(q, out, sem)
    copy.start()
    copy.wait()


def solve_kernel(values, obs, var, noise, columns, out, coef):
    groups = obs.shape[0]
    ens = noise.shape[1]
    half = ens // 2
    spaces = groups * 8
    parts = []
    for g in range(groups):
        sides = []
        for core in range(2):
            total = None
            for near in range(4):
                chip = (4 * g + near - core) % (4 * groups)
                row = values[pl.ds(2 * chip + core, half, stride=spaces), :]
                total = row if total is None else total + row
            sides.append(total)
        parts.append(sides)
    lanes = values.shape[1]
    count = lanes // 4
    near = lax.broadcasted_iota(jnp.int32, (half, lanes), 1) < count
    ends = [values[pl.ds(at, half, stride=spaces), :] for at in (0, spaces - 1)]
    far = [pltpu.roll(end, lanes - count, 1) for end in ends]
    for core in range(2):
        own, foreign = ends[core], far[1 - core]
        parts[0][core] = parts[0][core] - own + jnp.where(near, own + foreign, 0.0)
    parts = [jnp.concatenate(sides, axis=0) for sides in parts]
    small = jnp.zeros((ens, ens), jnp.float32)
    right = jnp.zeros((ens, ens), jnp.float32)
    dims = (((1,), (1,)), ((), ()))
    for g in range(groups):
        predicted = parts[g]
        dev = predicted - jnp.mean(predicted, axis=0, keepdims=True)
        spread = INFLATION * var[pl.ds(g, 1), :]
        resid = obs[pl.ds(g, 1), :] + jnp.sqrt(spread) * noise[g] - predicted
        scaled = dev / spread
        small = small + lax.dot_general(
            scaled, dev, dims, precision=HIGH, preferred_element_type=jnp.float32
        )
        right = right + lax.dot_general(
            scaled, resid, dims, precision=HIGH, preferred_element_type=jnp.float32
        )
    row = lax.broadcasted_iota(jnp.int32, (ens, ens), 0)
    col = lax.broadcasted_iota(jnp.int32, (ens, ens), 1)
    left = small + jnp.where(row == col, ens - 1.0, 0.0)
    for k in range(ens):
        pivot = left[k : k + 1, k : k + 1]
        left_row = left[k : k + 1, :] / pivot
        right_row = right[k : k + 1, :] / pivot
        factor = left[:, k : k + 1]
        here = row == k
        left = jnp.where(here, left_row, left - factor * left_row)
        right = jnp.where(here, right_row, right - factor * right_row)
    mixing = right - jnp.mean(right, axis=0, keepdims=True) + jnp.where(row == col, 1.0, 0.0)
    rows, wide = columns.shape[2], columns.shape[3]

    def natural(place):
        return 2 * place if place < half else 2 * (place - half) + 1

    for j in range(ens):
        for m in range(ens):
            at = natural(j) * ens + natural(m)
            coef[at] = jnp.broadcast_to(mixing[j : j + 1, m : m + 1], (8, wide))

    def one(n, carry):
        part = [columns[j, n] for j in range(ens)]
        for m in range(ens):
            for r0 in range(0, rows, 8):
                total = coef[m] * part[0][r0 : r0 + 8]
                for j in range(1, ens):
                    total = total + coef[j * ens + m] * part[j][r0 : r0 + 8]
                out[m, n, r0 : r0 + 8, :] = total
        return carry

    lax.fori_loop(0, columns.shape[1], one, 0)


def body(
    log_perm,
    saturation,
    pressure_init,
    wells,
    well_rate,
    obs_index,
    obs_weight,
    obs_value,
    obs_var,
    noise,
):
    width, ny, nz = log_perm.shape[1:]
    spaces = lax.axis_size("space")
    mems = lax.axis_size("mem")
    place = lax.axis_index("space")
    odd = place % 2
    chip = place // 2
    chips = spaces // 2
    rows = spaces * width
    around = (chip + odd) % chips
    cut = jnp.where(odd == 1, chip == chips - 1, chip == 0).astype(jnp.int32)
    per = obs_index.shape[0] // rows
    slots = 8 * per
    flags = jnp.stack([odd, cut, (around % 4) * slots, chip, jnp.int32(rows)]).astype(jnp.int32)

    def part(field, start, size):
        return lax.dynamic_slice_in_dim(field, start, size, axis=0)

    other = part(log_perm, 1 - odd, 1)[0]
    swap_out = jnp.concatenate([other, saturation, pressure_init])
    edge_out = jnp.concatenate([other, part(saturation, odd * 2, 2), part(pressure_init, odd, 3)])
    swapped = lax.ppermute(swap_out, "space", [(i, i ^ 1) for i in range(spaces)])
    ends = spaces - 1
    edge_in = lax.ppermute(
        edge_out,
        "space",
        [(0, 0), (ends, ends)] + [(i, i + 1 if i % 2 else i - 1) for i in range(1, ends)],
    )
    grid = (ny, nz)

    def plane(count):
        return pltpu.VMEM((count,) + grid, jnp.float32)

    sems = pltpu.SemaphoreType.DMA((64,))
    q = pl.pallas_call(
        source_kernel,
        out_shape=pltpu.HBM((13,) + grid, jnp.float32),
        in_specs=[SMEM, SMEM, SMEM],
        out_specs=FAR,
        scratch_shapes=[plane(13), pltpu.SemaphoreType.DMA],
        name="sources",
        compiler_params=PARAMS,
    )(flags, wells, well_rate)
    keep, send, perm_tile = pl.pallas_call(
        first_kernel,
        out_shape=(plane(PLANES), plane(8), plane(8)),
        in_specs=[SMEM] + [FAR] * 3 + [VMEM, FAR],
        out_specs=(VMEM,) * 3,
        scratch_shapes=tile_scratch(ny, nz) + [plane(4), sems],
        name="first",
        compiler_params=PARAMS,
    )(flags, log_perm, saturation, pressure_init, near(swapped), q)
    onward = [(i, i + 2) for i in range(0, ends - 1, 2)] + [(ends - 1, ends)]
    onward += [(i, i - 2) for i in range(3, spaces, 2)] + [(1, 0)]
    back = [(b, a) for a, b in onward]
    got = lax.ppermute(send, "space", onward)

    def local(table):
        table = jnp.roll(table.reshape(per, rows, -1), 4, axis=1)
        return lax.dynamic_slice_in_dim(table, around * 8, 8, axis=1).reshape(-1)

    def ordered(table):
        table = jnp.roll(table.reshape(-1, per, rows), 4, axis=2)
        table = table.reshape(-1, per, chips // 4, 4, 8).transpose(2, 0, 3, 1, 4)
        return table.reshape(chips // 4, -1, 4 * slots)

    index, weight = local(obs_index), local(obs_weight)
    value, var = ordered(obs_value)[:, 0], ordered(obs_var)[:, 0]
    mixed_noise = ordered(jnp.concatenate([noise[0::2], noise[1::2]]))
    tables = (index, weight, value, var, mixed_noise)
    keep, send, perm_edge = pl.pallas_call(
        second_kernel,
        out_shape=(plane(PLANES), plane(PLANES), plane(8)),
        in_specs=[SMEM] + [VMEM] * 4 + [FAR] * (TABLES + 1),
        out_specs=(VMEM,) * 3,
        scratch_shapes=tile_scratch(ny, nz) + [sems],
        name="second",
        compiler_params=PARAMS,
    )(flags, near(keep), near(edge_in), near(got), near(perm_tile), q, *tables)
    got = lax.ppermute(send, "space", back)
    columns = lax.all_to_all(log_perm, "mem", split_axis=2, concat_axis=0, tiled=True)
    keep, send = pl.pallas_call(
        third_kernel,
        out_shape=(plane(PLANES), plane(PLANES)),
        in_specs=[SMEM] + [VMEM] * 3 + [FAR] * 2,
        out_specs=(VMEM,) * 2,
        scratch_shapes=tile_scratch(ny, nz) + [sems],
        name="third",
        compiler_params=PARAMS,
    )(flags, near(keep), near(got), near(perm_tile), q, columns)
    got = lax.ppermute(send, "space", onward)
    devices = mems * spaces
    values = pl.pallas_call(
        last_kernel,
        out_shape=pltpu.VMEM((devices, nz), jnp.float32),
        in_specs=[SMEM] * 3 + [VMEM] * 3 + [FAR],
        out_specs=VMEM,
        scratch_shapes=tile_scratch(ny, nz) + [sems, pltpu.VMEM((nz, nz), jnp.float32)],
        name="last",
        compiler_params=PARAMS,
    )(flags, index, weight, near(keep), near(got), near(perm_edge), q)
    values = lax.all_to_all(
        values.reshape(devices, 1, nz), ("mem", "space"), 0, 0, tiled=True
    ).reshape(devices, nz)
    return pl.pallas_call(
        solve_kernel,
        out_shape=jax.ShapeDtypeStruct(columns.shape, jnp.float32),
        in_specs=[VMEM] * 5,
        out_specs=VMEM,
        scratch_shapes=[pltpu.VMEM((noise.shape[0] ** 2, 8, nz), jnp.float32)],
        name="solve",
        compiler_params=PARAMS,
    )(near(values), value, var, mixed_noise, columns)


def solution(mesh):
    placed = (
        P("mem", "space", None, None),
        P("space", None, None),
        P("space", None, None),
        P(),
        P(),
        P(),
        P(),
        P(),
        P(),
        P(),
    )
    return jax.shard_map(
        body, mesh=mesh, in_specs=placed, out_specs=P(None, "space", "mem", None), check_vma=False
    )
```

time: 116 us -> 116 us (level)
  blocking collectives: 0 us -> 37.1 us
  waiting for transfers between devices: 38.2 us -> 10.6 us
  starting transfers between devices: 16.8 us -> 7.74 us
  local copies, waits for them, and re-layouts: 14.9 us -> 11.2 us
  other arithmetic: 0.49 us -> 2.03 us
    all_to_all x0 -> x2, blocking collectives: none -> 37.1 us  [the longest x1 22.2 us: body(): lax.all_to_all(values.reshape(devices, 1, nz), ('mem', 'space'), 0, 0, ti...]
    ppermute x1, waiting for transfers between devices: 12.9 us -> 0.01 us  [body(): got = lax.ppermute(send, 'space', back)]
    all_to_all x2 -> x0, starting transfers between devices: 9.76 us -> none  [the longest x1 5.34 us: body(): lax.all_to_all(values.reshape(devices, 1, nz), ('mem', 'space'), 0, 0, ti...]
    all_to_all x2 -> x0, waiting for transfers between devices: 7.72 us -> none  [the longest x1 7.72 us: body(): lax.all_to_all(values.reshape(devices, 1, nz), ('mem', 'space'), 0, 0, ti...]
    ppermute x2, waiting for transfers between devices: 17.6 us -> 10.6 us  [body(): got = lax.ppermute(send, 'space', onward)]
    unnamed x29, local copies, waits for them, and re-layouts: 6.59 us -> 3.48 us
    transpose x3, local copies, waits for them, and re-layouts: 0.21 us -> 1.86 us  [ordered(): table = table.reshape(-1, per, chips // 4, 4, 8).transpose(2, 0, 3, 1, 4)]
    ppermute x2, starting transfers between devices: 0.15 us -> 1.48 us  [body(): got = lax.ppermute(send, 'space', onward)]
  transfers between devices with their start and end apart: 7 -> 5, of which waited for: 4 -> 2; matrix products, arithmetic and copies ran while one was open for 7% -> 8% of each run, Pallas kernels for 17% -> 9%
where the time goes in v2:
time: 116 us; the launch traced here: 115 us
  Pallas kernels  45.7 us (39%)
  blocking collectives  37.1 us (32%)
  local copies, waits for them, and re-layouts  11.2 us (10%)
  waiting for transfers between devices  10.6 us (9%)
  starting transfers between devices  7.74 us (7%)
  other arithmetic  2.03 us (2%)
    all_to_all x1, blocking collectives, body(): lax.all_to_all(values.reshape(devices, 1, nz), ('mem', 'space'), 0, 0, ti...  22.2 us
    all_to_all x1, blocking collectives, body(): lax.all_to_all(log_perm, 'mem', split_axis=2, concat_axis=0, tiled=True)  14.9 us
    pallas_call x1, Pallas kernels, body(): pl.pallas_call(second_kernel, out_shape=(plane(PLANES), plane(PLANES), pl...  12.7 us
    pallas_call x1, Pallas kernels, body(): pl.pallas_call(third_kernel, out_shape=(plane(PLANES), plane(PLANES)), in...  12.1 us
    ppermute x2, waiting for transfers between devices, body(): got = lax.ppermute(send, 'space', onward)  10.6 us
    pallas_call x1, Pallas kernels, body(): pl.pallas_call(last_kernel, out_shape=pltpu.VMEM((devices, nz), jnp.float...  8.73 us
    pallas_call x1, Pallas kernels, body(): pl.pallas_call(first_kernel, out_shape=(plane(PLANES), plane(8), plane(8)...  8.08 us
    ppermute x1, starting transfers between devices, body(): lax.ppermute(edge_out, 'space', [(0, 0), (ends, ends)] + [(i, i + 1 if i...  5.94 us
  transfers between devices with their start and end apart: 5, of which 2 were waited for; matrix products, arithmetic and copies ran while one was open for 8% of the time, Pallas kernels for 9%

profile of v2, /device:TPU:0, one launch (start us, length us, event | category | flops | bytes accessed | tf_op | source)
XLA Modules:
  0.0 114.6 jit_solution(2869630302314466923)
XLA Ops:
  0.0 1.0 dynamic-slice_bitcast_fusion
  1.0 0.1 copy-done.4
  1.2 0.1 collective-permute-start
  1.3 0.9 pad_maximum_fusion.1
  2.2 5.9 %collective-permute-start.1 = (f32[9,128,128]{2,1,0:T(8,128)}, f32[9,128,128]{2,1,0:T(8,128)}, u32[]{:S(2)}, u32[]{:S(2)}) collective-permute-start(f32[9,128,128]{2,1,0:T(8,128)} %pad_maximum_fusion.1), channel_id=1, source_target_pairs={{0,0},{31,31},{1,2},{2,1},{3,4},{4,3},{5,6},{6,5},{7,8},{8,7},{9,1... | collective-permute-start | bytes 1769480 | tf_op jit(solution)/shard_map/ppermute | solution.py:519
  8.2 0.7 copy-done.7
  8.9 0.1 slice.56
  8.9 0.1 dynamic-slice_add_fusion
  9.0 0.6 copy-done.11
  9.7 0.6 slice.53
  10.3 0.1 copy.20
  10.3 0.1 reshape.40.refs_0_.index
  10.4 0.7 slice.58
  11.1 0.1 stack.23.flags
  11.2 1.9 %sources.1.q = f32[13,128,128]{2,1,0:T(8,128)} custom-call(s32[5]{0:T(128)S(1)} %stack.23.flags, s32[64]{0:T(128)S(1)} %copy-done.5, f32[64]{0:T(128)S(1)} %copy-done.6), custom_call_target="tpu_custom_call" | custom-call | tf_op jit(solution)/shard_map/sources/pallas_call | solution.py:530
  13.2 1.1 %copy-done = f32[13,128,128]{2,1,0:T(8,128)S(1)} copy-done((f32[13,128,128]{2,1,0:T(8,128)S(1)}, f32[13,128,128]{2,1,0:T(8,128)}, u32[]{:S(2)}) %copy-start) | copy-done | bytes 851992
  14.3 8.1 %first.1 = (f32[13,128,128]{2,1,0:T(8,128)S(1)}, f32[8,128,128]{2,1,0:T(8,128)}, f32[8,128,128]{2,1,0:T(8,128)S(1)}) custom-call(s32[5]{0:T(128)S(1)} %stack.23.flags, f32[2,4,128,128]{3,2,1,0:T(8,128)S(1)} %copy-done.2, f32[4,128,128]{2,1,0:T(8,128)S(1)} %copy-done.4, f32[4,128,128]{2,1,0:T(8,128)S(1)} %copy-done.3, ...), custom_call_target="tpu_custom_call" | custom-call | tf_op jit(solution)/shard_map/first/pallas_call | solution.py:539
  22.4 0.1 collective-permute-start.2
  22.5 0.1 dynamic-slice_maximum_fusion
  22.6 0.1 copy.21
  22.7 0.1 reshape.42.refs_1_.weight
  22.8 0.7 maximum_bitcast_fusion
  23.5 0.1 slice.60
  23.6 0.1 pad_maximum_fusion.2
  23.6 1.1 reshape.48
  24.7 1.8 %copy.24 = f32[4,8,4,4,8]{4,3,2,1,0:T(4,128)} copy(f32[4,8,4,4,8]{4,2,0,1,3:T(4,128)} %bitcast.39) | data formatting | bytes 32768 | tf_op jit(solution)/shard_map/transpose | solution.py:559
  26.5 1.2 %reshape.49.refs_4_.noise = f32[4,8,128]{2,1,0:T(8,128)S(1)} reshape(f32[4,8,4,4,8]{4,3,2,1,0:T(4,128)} %copy.24) | data formatting | bytes 32768 | tf_op jit(solution)/shard_map/reshape | solution.py:560
  27.8 0.1 slice.48
  27.8 0.1 pad_maximum_fusion.3
  27.9 0.1 reshape.44
  28.0 0.1 squeeze_reshape.6.refs_2_.obs
  28.1 0.6 copy-done.13
  28.7 0.1 slice.50
  28.8 0.1 pad_maximum_fusion.4
  28.8 0.1 reshape.46
  29.0 0.1 squeeze_reshape.7.refs_3_.var
  29.1 0.4 collective-permute-done.2.late_in
  29.5 12.7 %second.1 = (f32[13,128,128]{2,1,0:T(8,128)S(1)}, f32[13,128,128]{2,1,0:T(8,128)S(1)}, f32[8,128,128]{2,1,0:T(8,128)S(1)}) custom-call(s32[5]{0:T(128)S(1)} %stack.23.flags, f32[13,128,128]{2,1,0:T(8,128)S(1)} %get-tuple-element.13.kept, f32[9,128,128]{2,1,0:T(8,128)} %collective-permute-done.1.raw_in, f32[8,128,128]{2,1,0:T(8,128)S(1)} %collective-permute-done.2.late_in, ...), custom_call_target="tpu_custom_call" | custom-call | tf_op jit(solution)/shard_map/second/pallas_call | solution.py:566
  42.2 0.2 collective-permute-start.3
  42.5 0.3 copy.25
  42.8 14.9 %all_to_all.23 = f32[2,4,128,128]{3,1,0,2:T(4,128)S(1)} all-to-all(f32[2,4,128,128]{3,1,0,2:T(4,128)S(1)} %copy.25), channel_id=1, replica_groups=mesh['mem'=4,'space'=32] {'mem'}, dimensions={2} | all-to-all | bytes 1048576 | tf_op jit(solution)/shard_map/all_to_all | solution.py:576
  57.7 0.1 copy.26
  57.8 12.1 %third.1 = (f32[13,128,128]{2,1,0:T(8,128)S(1)}, f32[13,128,128]{2,1,0:T(8,128)S(1)}) custom-call(s32[5]{0:T(128)S(1)} %stack.23.flags, f32[13,128,128]{2,1,0:T(8,128)S(1)} %get-tuple-element.16.kept, f32[13,128,128]{2,1,0:T(8,128)S(1)} %collective-permute-done.3.got, f32[8,128,128]{2,1,0:T(8,128)S(1)} %get-tuple-element.15.perm_own.perm, ...), custom_call_target="tpu_custom_call" | custom-call | tf_op jit(solution)/shard_map/third/pallas_call | solution.py:577
  70.0 1.4 %collective-permute-start.4 = (f32[13,128,128]{2,1,0:T(8,128)S(1)}, f32[13,128,128]{2,1,0:T(8,128)S(1)}, u32[]{:S(2)}, u32[]{:S(2)}) collective-permute-start(f32[13,128,128]{2,1,0:T(8,128)S(1)} %get-tuple-element.19), channel_id=1, source_target_pairs={{0,2},{2,4},{4,6},{6,8},{8,10},{10,12},{12,14},{14,16},{16,18},{18... | collective-permute-start | bytes 2555912 | tf_op jit(solution)/shard_map/ppermute | solution.py:586
  71.4 10.2 %collective-permute-done.4.got = f32[13,128,128]{2,1,0:T(8,128)S(1)} collective-permute-done((f32[13,128,128]{2,1,0:T(8,128)S(1)}, f32[13,128,128]{2,1,0:T(8,128)S(1)}, u32[]{:S(2)}, u32[]{:S(2)}) %collective-permute-start.4) | collective-permute-done | bytes 852000 | tf_op jit(solution)/shard_map/ppermute | solution.py:586
  81.6 8.7 %last.1 = f32[128,128]{1,0:T(8,128)S(1)} custom-call(s32[5]{0:T(128)S(1)} %stack.23.flags, s32[256]{0:T(256)S(1)} %reshape.40.refs_0_.index, f32[256]{0:T(256)S(1)} %reshape.42.refs_1_.weight, f32[13,128,128]{2,1,0:T(8,128)S(1)} %get-tuple-element.18.kept, f32[13,128,128]{2,1,0:T(8,128)S(1)} %collective-permute-done.4.got, ...), custom_call_target="tpu_custom_call" | custom-call | tf_op jit(solution)/shard_map/last/pallas_call | solution.py:588
  90.3 22.2 %all_to_all.24 = f32[128,1,128]{2,1,0:T(1,128)S(1)} all-to-all(f32[128,1,128]{2,1,0:T(1,128)S(1)} %bitcast.36), channel_id=1, replica_groups=mesh['mem'=4,'space'=32] {'mem','space'}, dimensions={0} | all-to-all | bytes 131072 | tf_op jit(solution)/shard_map/all_to_all | solution.py:597
  112.5 2.2 %solve.1 = f32[8,4,32,128]{3,2,1,0:T(8,128)} custom-call(f32[128,128]{1,0:T(8,128)S(1)} %bitcast.37, f32[4,128]{1,0:T(4,128)S(1)} %squeeze_reshape.6.refs_2_.obs, f32[4,128]{1,0:T(4,128)S(1)} %squeeze_reshape.7.refs_3_.var, f32[4,8,128]{2,1,0:T(8,128)S(1)} %reshape.49.refs_4_.noise, f32[8,4,32,128]{3,2,1,0:T(8,128)S(1)} %bitcast.35), custom_call_target="tpu_custom_call" | custom-call | tf_op jit(solution)/shard_map/solve/pallas_call | solution.py:600
  (32 shorter events, 0.2 us)
Async XLA Ops:
  0.0 1.0 copy-start.3
  0.0 1.1 copy-start.4
  1.2 12.0 %collective-permute-start = (f32[12,128,128]{2,1,0:T(8,128)S(1)}, f32[12,128,128]{2,1,0:T(8,128)S(1)}, u32[]{:S(2)}, u32[]{:S(2)}) collective-permute-start(f32[12,128,128]{2,1,0:T(8,128)S(1)} %pad_maximum_fusion), channel_id=1, source_target_pairs={{0,1},{1,0},{2,3},{3,2},{4,5},{5,4},{6,7},{7,6},{8,9},{9,8},{10,11... | collective-permute-start | bytes 2359304 | tf_op jit(solution)/shard_map/ppermute | solution.py:517
  2.2 26.9 %collective-permute-start.1 = (f32[9,128,128]{2,1,0:T(8,128)}, f32[9,128,128]{2,1,0:T(8,128)}, u32[]{:S(2)}, u32[]{:S(2)}) collective-permute-start(f32[9,128,128]{2,1,0:T(8,128)} %pad_maximum_fusion.1), channel_id=1, source_target_pairs={{0,0},{31,31},{1,2},{2,1},{3,4},{4,3},{5,6},{6,5},{7,8},{8,7},{9,1... | collective-permute-start | bytes 1769480 | tf_op jit(solution)/shard_map/ppermute | solution.py:519
  8.1 0.7 copy-start.7
  8.2 3.1 %copy-start.5 = (s32[64]{0:T(128)S(1)}, s32[64]{0:T(128)}, u32[]{:S(2)}) copy-start(s32[64]{0:T(128)} %wells.1) | copy-start | bytes 772
  8.2 3.1 %copy-start.6 = (f32[64]{0:T(128)S(1)}, f32[64]{0:T(128)}, u32[]{:S(2)}) copy-start(f32[64]{0:T(128)} %rate.1) | copy-start | bytes 772
  8.2 2.3 %copy-start.8 = (f32[512,8]{0,1:T(8,128)S(1)}, f32[512,8]{0,1:T(8,128)}, u32[]{:S(2)}) copy-start(f32[512,8]{0,1:T(8,128)} %param.16) | copy-start | bytes 49156
  8.9 0.7 copy-start.11
  8.9 4.2 %copy-start.2 = (f32[2,4,128,128]{3,2,1,0:T(8,128)S(1)}, f32[2,4,128,128]{3,2,1,0:T(8,128)}, u32[]{:S(2)}) copy-start(f32[2,4,128,128]{3,2,1,0:T(8,128)} %log_perm.1) | copy-start | bytes 1572868
  13.2 1.2 %copy-start = (f32[13,128,128]{2,1,0:T(8,128)S(1)}, f32[13,128,128]{2,1,0:T(8,128)}, u32[]{:S(2)}) copy-start(f32[13,128,128]{2,1,0:T(8,128)} %sources.1.q) | copy-start | bytes 2555908
  14.3 8.2 %copy-start.9 = (f32[512,8]{0,1:T(8,128)S(1)}, f32[512,8]{0,1:T(8,128)}, u32[]{:S(2)}) copy-start(f32[512,8]{0,1:T(8,128)} %param.16) | copy-start | bytes 49156
  14.3 8.2 %copy-start.10 = (f32[4,4,8]{1,2,0:T(8,128)S(1)}, f32[4,4,8]{1,2,0:T(8,128)}, u32[]{:S(2)}) copy-start(f32[4,4,8]{1,2,0:T(8,128)} %slice.58) | copy-start | bytes 1540
  22.4 7.1 %copy-start.1 = (f32[13,128,128]{2,1,0:T(8,128)S(1)}, f32[13,128,128]{2,1,0:T(8,128)}, u32[]{:S(2)}) copy-start(f32[13,128,128]{2,1,0:T(8,128)} %sources.1.q) | copy-start | bytes 2555908
  22.4 7.1 %collective-permute-start.2 = (f32[8,128,128]{2,1,0:T(8,128)}, f32[8,128,128]{2,1,0:T(8,128)S(1)}, u32[]{:S(2)}, u32[]{:S(2)}) collective-permute-start(f32[8,128,128]{2,1,0:T(8,128)} %get-tuple-element.14), channel_id=1, source_target_pairs={{0,2},{2,4},{4,6},{6,8},{8,10},{10,12},{12,14},{14,16},{16,18},{18... | collective-permute-start | bytes 1572872 | tf_op jit(solution)/shard_map/ppermute | solution.py:551
  26.5 1.2 %copy-start.12 = (f32[512]{0:T(512)S(1)}, f32[512]{0:T(512)}, u32[]{:S(2)}) copy-start(f32[512]{0:T(512)} %param.17) | copy-start | bytes 6148
  28.0 0.7 copy-start.13
  42.2 15.6 %collective-permute-start.3 = (f32[13,128,128]{2,1,0:T(8,128)S(1)}, f32[13,128,128]{2,1,0:T(8,128)S(1)}, u32[]{:S(2)}, u32[]{:S(2)}) collective-permute-start(f32[13,128,128]{2,1,0:T(8,128)S(1)} %get-tuple-element.17), channel_id=1, source_target_pairs={{2,0},{4,2},{6,4},{8,6},{10,8},{12,10},{14,12},{16,14},{18,16},{20... | collective-permute-start | bytes 2555912 | tf_op jit(solution)/shard_map/ppermute | solution.py:575
  70.0 11.6 %collective-permute-start.4 = (f32[13,128,128]{2,1,0:T(8,128)S(1)}, f32[13,128,128]{2,1,0:T(8,128)S(1)}, u32[]{:S(2)}, u32[]{:S(2)}) collective-permute-start(f32[13,128,128]{2,1,0:T(8,128)S(1)} %get-tuple-element.19), channel_id=1, source_target_pairs={{0,2},{2,4},{4,6},{6,8},{8,10},{10,12},{12,14},{14,16},{16,18},{18... | collective-permute-start | bytes 2555912 | tf_op jit(solution)/shard_map/ppermute | solution.py:586

commit v3 on v2

--- a/solution.py
+++ b/solution.py
@@ -1,3 +1,5 @@
+import functools
+
 import jax
 import jax.numpy as jnp
 from jax import lax
@@ -17,8 +19,7 @@
 
 S0, P0, S1, P1, S2, L2 = (0, 1), (2, 3, 4), (5, 6, 7), (8, 9, 10), 11, 12
 PLANES = 13
-TABLES = 5
-PARAMS = pltpu.CompilerParams(vmem_limit_bytes=12 << 20)
+GRANT = 56 << 20
 
 
 def spot(row):
@@ -147,7 +148,7 @@
 def tile_scratch(ny, nz):
     tall = ny + 2 * PAD
     wide = [pltpu.VMEM((11, tall, nz), jnp.float32) for _ in range(6)]
-    flat = [pltpu.VMEM((count, ny, nz), jnp.float32) for count in (11, 11, 13)]
+    flat = [pltpu.VMEM((count, ny, nz), jnp.float32) for count in (11, 11, 12)]
     return wide + flat
 
 
@@ -165,6 +166,25 @@
         copy.wait()
 
 
+def move(pairs):
+    tall = min(src.shape[0] for src, _ in pairs)
+
+    def one(n, carry):
+        where = pl.ds(pl.multiple_of(n * CHUNK, CHUNK), CHUNK)
+        for src, dst in pairs:
+            dst[where, :] = src[where, :]
+        return carry
+
+    lax.fori_loop(0, tall // CHUNK, one, 0)
+
+
+def position(chips):
+    place = lax.axis_index("space")
+    odd, chip = place & 1, lax.shift_right_logical(place, 1)
+    end = jnp.where(odd == 1, chips - 1, 0)
+    return odd, chip, (chip == end).astype(jnp.int32)
+
+
 def beyond(tile, row):
     return jnp.where(tile.cut == 1, 5, spot(row))
 
@@ -172,15 +192,12 @@
 def give_early(tile, keep, send, send_early):
     pairs = []
     inner = pl.ds(PAD, tile.ny)
-    for d in range(2):
-        pairs.append((tile.s[0].at[spot(d)], keep.at[S0[d]]))
-    for d in range(3):
-        pairs.append((tile.p[0].at[spot(d), inner], keep.at[P0[d]]))
-    if send_early:
+    sides = [(keep, lambda d: d)] + ([(send, lambda d: 7 - d)] if send_early else [])
+    for out, row in sides:
         for d in range(2):
-            pairs.append((tile.s[0].at[spot(7 - d)], send.at[S0[d]]))
+            pairs.append((tile.s[0].at[spot(row(d))], out.at[S0[d]]))
         for d in range(3):
-            pairs.append((tile.p[0].at[spot(7 - d), inner], send.at[P0[d]]))
+            pairs.append((tile.p[0].at[spot(row(d)), inner], out.at[P0[d]]))
     return pairs
 
 
@@ -221,121 +238,114 @@
     return start, s_next, p_next, last
 
 
-def advance(tile, keep, send, sems, first, send_early):
+def advance(tile, keep, send, send_early):
     base = 0 if send_early else S1[0]
-    early = issue(give_early(tile, keep, send, send_early), sems, first)
-    first += len(early)
+    move(give_early(tile, keep, send, send_early))
     tile.saturate(0, 1, 6)
     tile.pressure(0, 2, 5)
-    late = issue(
-        give_late(tile, send, (7, -1), base) + give_late(tile, keep, (0, 1), 0), sems, first
-    )
-    first += len(late)
-    drain(early)
     tile.saturate(1, 3, 4)
-    last = issue(
-        give_last(tile, send, (7, -1), base) + give_last(tile, keep, (0, 1), 0), sems, first
-    )
-    drain(late)
-    drain(last)
-
-
-def first_kernel(flags, log_perm, own_sat, own_press, swapped, q, keep, send, perm, *refs):
+    pairs = []
+    for out, near_row, at in ((send, (7, -1), base), (keep, (0, 1), 0)):
+        pairs += give_late(tile, out, near_row, at) + give_last(tile, out, near_row, at)
+    move(pairs)
+
+
+def first_kernel(chips, log_perm, own_sat, own_press, q, swapped, keep, send, perm_out, *refs):
+    odd, _, _ = position(chips)
+    perm, raw, sems = refs[9:]
     tile = Tile(*refs[:8], perm, refs[8], lambda row: row + 4, jnp.int32(0))
-    raw, sems = refs[9], refs[10]
-    odd = flags[0]
     inner = pl.ds(PAD, tile.ny)
 
     def place(n):
         return jnp.where(odd == 1, 3 - n, n)
 
-    pairs = [(q, tile.q), (log_perm.at[odd], raw)]
+    pairs = [(log_perm.at[odd], raw)]
     for n in range(4):
         pairs.append((own_sat.at[place(n)], tile.s[0].at[spot(n)]))
         pairs.append((own_press.at[place(n)], tile.p[0].at[spot(n), inner]))
+    copies = issue(pairs, sems, 0)
+    q_copy = issue([(q, tile.q)], sems, len(pairs))
+    tile.clear()
+    pairs = []
+    for n in range(4):
         pairs.append((swapped.at[4 + place(n)], tile.s[0].at[spot(4 + n)]))
         pairs.append((swapped.at[8 + place(n)], tile.p[0].at[spot(4 + n), inner]))
-    copies = issue(pairs, sems, 0)
+    move(pairs)
+
+    def halve(src, base):
+        def one(n, carry):
+            for y0 in range(0, tile.ny, CHUNK):
+                where = pl.ds(y0, CHUNK)
+                perm[base + n, where, :] = 0.5 * jnp.exp(src[place(n), where, :])
+            return carry
+
+        lax.fori_loop(0, 4, one, 0)
+
+    halve(swapped, 4)
+    drain(copies)
+    halve(raw, 0)
+    perm_copy = issue([(perm, perm_out)], sems, 10)
+    tile.props(0, 0, 7)
+    drain(q_copy)
+    advance(tile, keep, send, False)
+    drain(perm_copy)
+
+
+def fill(tile, sides, perm_copy, q_copy):
     tile.clear()
-
-    def halve(n, carry):
-        for y0 in range(0, tile.ny, CHUNK):
-            where = pl.ds(y0, CHUNK)
-            perm[4 + n, where, :] = 0.5 * jnp.exp(swapped[place(n), where, :])
-        return carry
-
-    lax.fori_loop(0, 4, halve, 0)
-    drain(copies)
-
-    def halve_own(n, carry):
-        for y0 in range(0, tile.ny, CHUNK):
-            where = pl.ds(y0, CHUNK)
-            perm[n, where, :] = 0.5 * jnp.exp(raw[place(n), where, :])
-        return carry
-
-    lax.fori_loop(0, 4, halve_own, 0)
-    tile.props(0, 0, 7)
-    advance(tile, keep, send, sems, len(pairs), False)
-
-
-def fill(tile, q, sides, sems):
     groups = [sum((side[n] for side in sides), []) for n in range(4)]
-    groups[0].append((q, tile.q))
-    first, copies = 0, []
-    for group in groups[:3]:
-        copies.append(issue(group, sems, first))
-        first += len(group)
-    tile.clear()
-    drain(copies[0])
+    move(groups[0] + groups[1] + groups[2])
+    drain(perm_copy)
     tile.props(0, 2, 5)
-    tile.saturate(0, 3, 4)
-    drain(copies[1])
     tile.props(1, 0, 2)
     tile.props(1, 5, 7)
+    drain(q_copy)
+    tile.saturate(0, 3, 4)
     tile.pressure(0, 2, 5)
-    drain(copies[2])
-    last = issue(groups[3], sems, first)
-    drain(last)
+    move(groups[3])
     tile.props(0, 0, 0)
     tile.props(0, 7, 7)
     tile.saturate(1, 1, 6)
     tile.pressure(1, 0, 7)
-    return first + len(last)
 
 
 def edge_q(cut):
     return lambda row: jnp.where((cut == 1) & (row >= 4), row, 7 - row)
 
 
-def second_kernel(flags, kept, raw_in, late_in, perm_own, q, *refs):
-    keep, send, perm = refs[TABLES : TABLES + 3]
-    refs = refs[TABLES + 3 :]
-    tile = Tile(*refs[:8], perm, refs[8], edge_q(flags[1]), flags[1])
-    sems = refs[9]
-    straight = flags[0] ^ flags[1]
+def second_kernel(chips, perm_own, raw_in, q, kept, late_in, keep, send, perm_out, *refs):
+    odd, _, end = position(chips)
+    perm, raw, sems = refs[9:]
+    tile = Tile(*refs[:8], perm, refs[8], edge_q(end), end)
+    straight = odd ^ end
 
     def place(n, count):
         return jnp.where(straight == 1, n, count - 1 - n)
 
     def early(plane):
         if plane in S0:
-            return raw_in.at[4 + place(plane, 2)]
-        return raw_in.at[6 + place(plane - 2, 3)]
+            return raw.at[4 + place(plane, 2)]
+        return raw.at[6 + place(plane - 2, 3)]
+
+    copies = issue([(raw_in, raw)] + [(perm_own.at[3 - d], perm.at[d]) for d in range(4)], sems, 0)
+    q_copy = issue([(q, tile.q)], sems, 5)
+    drain(copies)
 
     def permeability(d, carry):
         for y0 in range(0, tile.ny, CHUNK):
             where = pl.ds(y0, CHUNK)
-            perm[3 - d, where, :] = perm_own[d, where, :]
-            perm[4 + d, where, :] = 0.5 * jnp.exp(raw_in[place(d, 4), where, :])
+            perm[4 + d, where, :] = 0.5 * jnp.exp(raw[place(d, 4), where, :])
         return carry
 
     lax.fori_loop(0, 4, permeability, 0)
+    perm_copy = issue([(perm, perm_out)], sems, 6)
     sides = (
         take(tile, lambda n: kept.at[n], lambda n: kept.at[n], 4, -1),
         take(tile, early, lambda n: late_in.at[n - S1[0]], 6, 1),
     )
-    first = fill(tile, q, sides, sems)
-    advance(tile, keep, send, sems, first, True)
+    fill(tile, sides, [], q_copy)
+    advance(tile, keep, send, True)
+    drain(perm_copy)
 
 
 def both_sides(tile, kept, got):
@@ -345,71 +355,100 @@
     )
 
 
-def third_kernel(flags, kept, got, perm, q, columns, keep, send, *refs):
+def third_kernel(perm, q, columns, kept, got, keep, send, *refs):
     del columns
-    tile = Tile(*refs[:8], perm, refs[8], lambda row: row + 4, jnp.int32(0))
-    first = fill(tile, q, both_sides(tile, kept, got), refs[9])
-    advance(tile, keep, send, refs[9], first, True)
-
-
-def last_kernel(flags, index, weight, kept, got, perm, q, values, *refs):
-    tile = Tile(*refs[:8], perm, refs[8], edge_q(flags[1]), flags[1])
-    sems, picked = refs[9], refs[10]
-    fill(tile, q, both_sides(tile, kept, got), sems)
-    odd, cut, offset = flags[0], flags[1], flags[2]
+    tile = Tile(*refs[:8], refs[9], refs[8], lambda row: row + 4, jnp.int32(0))
+    sems = refs[10]
+    perm_copy = issue([(perm, tile.perm)], sems, 0)
+    q_copy = issue([(q, tile.q)], sems, 1)
+    fill(tile, both_sides(tile, kept, got), perm_copy, q_copy)
+    advance(tile, keep, send, True)
+
+
+def last_kernel(chips, perm, q, index_in, weight_in, kept, got, values, *refs):
+    odd, chip, end = position(chips)
+    tile = Tile(*refs[:8], refs[9], refs[8], edge_q(end), end)
+    index, weight, picked, sems = refs[10:]
+    perm_copy = issue([(perm, tile.perm)], sems, 0)
+    q_copy = issue([(q, tile.q)], sems, 1)
+    tables = issue([(index_in, index), (weight_in, weight)], sems, 2)
+    fill(tile, both_sides(tile, kept, got), perm_copy, q_copy)
+    drain(tables)
+    around = (chip + odd) & (chips - 1)
+    total_rows = 8 * chips
+    per = index.shape[1] // total_rows
     lanes = kept.shape[2]
     lane = lax.broadcasted_iota(jnp.int32, (1, lanes), 1)
     picked[...] = jnp.zeros_like(picked)
-    count = index.shape[0] // 8
 
     def one(n, carry):
         slot = n & 7
         row = jnp.where(odd == 1, slot, 7 - slot)
         st = row + 1 + (row >= 4).astype(jnp.int32)
-        other = cut * (row >= 4).astype(jnp.int32)
-        at = n - slot + jnp.where(other == 1, 7 - slot, slot)
+        other = end * (row >= 4).astype(jnp.int32)
+        slot = jnp.where(other == 1, 7 - slot, slot)
+        column = lax.shift_right_logical(n, 3)
+        obs = column * total_rows + ((8 * around - 4 + slot) & (total_rows - 1))
         total = jnp.zeros((1, lanes), jnp.float32)
-        for t in range(8):
-            cell = index[at * 8 + t]
+        for t in range(index.shape[0]):
+            cell = index[t, obs]
             y = lax.shift_right_logical(cell, 7) & (tile.ny - 1)
             values_row = tile.p[0][st, pl.ds(PAD + y, 1), :]
-            total = total + jnp.where(lane == (cell & (lanes - 1)), values_row, 0.0) * weight[at * 8 + t]
-        picked[pl.ds(offset + at + other * count, 1), :] = total
+            total = total + jnp.where(lane == (cell & (lanes - 1)), values_row, 0.0) * weight[t, obs]
+        at = column * 32 + ((around & 3) + other) * 8 + slot
+        picked[pl.ds(at, 1), :] = total
         return carry
 
-    lax.fori_loop(0, count, one, 0)
+    lax.fori_loop(0, 8 * per, one, 0)
     ones = jnp.ones((values.shape[0], lanes), jnp.float32)
     values[...] = lax.dot_general(
         ones, picked[...], (((1,), (1,)), ((), ())), precision=HIGH, preferred_element_type=jnp.float32
     )
 
 
-def source_kernel(flags, wells, rate, out, q, sem):
+def prepare_kernel(chips, wells, rate, log_perm, value, var, noise, q_out, blocks, tables, q, sems):
+    rows = log_perm.shape[2] // blocks.shape[0]
+    copies = issue(
+        [(log_perm.at[:, :, pl.ds(b * rows, rows), :], blocks.at[b]) for b in range(blocks.shape[0])],
+        sems,
+        0,
+    )
+    odd, chip, _ = position(chips)
     ny, nz = q.shape[1], q.shape[2]
-    odd, chip = flags[0], flags[3]
-    last = q.shape[0] - 1
     lane = lax.broadcasted_iota(jnp.int32, (1, nz), 1)
     q[...] = jnp.zeros_like(q)
-    total = flags[4]
 
     def one(n, carry):
         cell = wells[n]
         x = lax.shift_right_logical(cell, 14)
         y = lax.shift_right_logical(cell, 7) & (ny - 1)
-        behind = jnp.where(odd == 1, chip * 8 + 11 - x, x - chip * 8 + 4) & (total - 1)
-        where = (jnp.minimum(behind, last), pl.ds(y, 1), slice(None))
-        q[where] = q[where] + jnp.where(lane == (cell & (nz - 1)), rate[n], 0.0)
+        behind = jnp.where(odd == 1, chip * 8 + 11 - x, x - chip * 8 + 4) & (8 * chips - 1)
+        where = (jnp.minimum(behind, q.shape[0] - 1), pl.ds(y, 1), slice(None))
+        here = jnp.where(behind < q.shape[0], cell & (nz - 1), -1)
+        q[where] = q[where] + jnp.where(lane == here, rate[n], 0.0)
         return carry
 
     lax.fori_loop(0, wells.shape[0], one, 0, unroll=4)
-    copy = pltpu.make_async_copy(q, out, sem)
-    copy.start()
-    copy.wait()
-
-
-def solve_kernel(values, obs, var, noise, columns, out, coef):
-    groups = obs.shape[0]
-    ens = noise.shape[1]
+    copies += issue([(q, q_out)], sems, len(copies))
+    groups, lanes = value.shape
+    wide = lanes // groups
+    half = noise.shape[0] // 2
+    side = lax.broadcasted_iota(jnp.int32, (1, lanes), 1) // wide
+    for g in range(groups):
+        total = None
+        for j in range(groups):
+            where = pl.ds(j * lanes, lanes)
+            parts = [noise[2 * n + c : 2 * n + c + 1, where] for c in range(2) for n in range(half)]
+            parts += [value[pl.ds(j, 1), :], var[pl.ds(j, 1), :], jnp.ones((6, lanes), jnp.float32)]
+            column = pltpu.roll(jnp.concatenate(parts, axis=0), (4 + wide * (j - g)) % lanes, 1)
+            total = column if total is None else jnp.where(side == j, column, total)
+        tables[g] = total
+    drain(copies)
+
+
+def solve_kernel(values, tables, columns, out, coef):
+    groups = tables.shape[0]
+    ens = columns.shape[0]
     half = ens // 2
     spaces = groups * 8
     parts = []
@@ -424,13 +463,12 @@
             sides.append(total)
         parts.append(sides)
     lanes = values.shape[1]
-    count = lanes // 4
-    near = lax.broadcasted_iota(jnp.int32, (half, lanes), 1) < count
+    near_lane = (lax.broadcasted_iota(jnp.int32, (half, lanes), 1) & 31) < 8
     ends = [values[pl.ds(at, half, stride=spaces), :] for at in (0, spaces - 1)]
-    far = [pltpu.roll(end, lanes - count, 1) for end in ends]
+    far = [pltpu.roll(end, lanes - 8, 1) for end in ends]
     for core in range(2):
         own, foreign = ends[core], far[1 - core]
-        parts[0][core] = parts[0][core] - own + jnp.where(near, own + foreign, 0.0)
+        parts[0][core] = parts[0][core] - own + jnp.where(near_lane, own + foreign, 0.0)
     parts = [jnp.concatenate(sides, axis=0) for sides in parts]
     small = jnp.zeros((ens, ens), jnp.float32)
     right = jnp.zeros((ens, ens), jnp.float32)
@@ -438,8 +476,8 @@
     for g in range(groups):
         predicted = parts[g]
         dev = predicted - jnp.mean(predicted, axis=0, keepdims=True)
-        spread = INFLATION * var[pl.ds(g, 1), :]
-        resid = obs[pl.ds(g, 1), :] + jnp.sqrt(spread) * noise[g] - predicted
+        spread = INFLATION * tables[g, ens + 1 : ens + 2, :]
+        resid = tables[g, ens : ens + 1, :] + jnp.sqrt(spread) * tables[g, 0:ens, :] - predicted
         scaled = dev / spread
         small = small + lax.dot_general(
             scaled, dev, dims, precision=HIGH, preferred_element_type=jnp.float32
@@ -494,118 +532,111 @@
     obs_var,
     noise,
 ):
-    width, ny, nz = log_perm.shape[1:]
+    members, width, ny, nz = log_perm.shape
     spaces = lax.axis_size("space")
     mems = lax.axis_size("mem")
-    place = lax.axis_index("space")
-    odd = place % 2
-    chip = place // 2
+    odd = lax.axis_index("space") % 2
     chips = spaces // 2
-    rows = spaces * width
-    around = (chip + odd) % chips
-    cut = jnp.where(odd == 1, chip == chips - 1, chip == 0).astype(jnp.int32)
-    per = obs_index.shape[0] // rows
-    slots = 8 * per
-    flags = jnp.stack([odd, cut, (around % 4) * slots, chip, jnp.int32(rows)]).astype(jnp.int32)
+    devices = mems * spaces
+    ens = members * mems
+    grid = (ny, nz)
+    f32 = jnp.float32
 
     def part(field, start, size):
         return lax.dynamic_slice_in_dim(field, start, size, axis=0)
 
+    def plane(count):
+        return pltpu.VMEM((count,) + grid, f32)
+
+    def call(kernel, name, **more):
+        return pl.pallas_call(
+            functools.partial(kernel, chips) if kernel is not third_kernel else kernel,
+            name=name,
+            **more,
+        )
+
+    grant = pltpu.CompilerParams(vmem_limit_bytes=GRANT)
     other = part(log_perm, 1 - odd, 1)[0]
     swap_out = jnp.concatenate([other, saturation, pressure_init])
+    swapped = lax.ppermute(swap_out, "space", [(i, i ^ 1) for i in range(spaces)])
     edge_out = jnp.concatenate([other, part(saturation, odd * 2, 2), part(pressure_init, odd, 3)])
-    swapped = lax.ppermute(swap_out, "space", [(i, i ^ 1) for i in range(spaces)])
     ends = spaces - 1
     edge_in = lax.ppermute(
         edge_out,
         "space",
         [(0, 0), (ends, ends)] + [(i, i + 1 if i % 2 else i - 1) for i in range(1, ends)],
     )
-    grid = (ny, nz)
-
-    def plane(count):
-        return pltpu.VMEM((count,) + grid, jnp.float32)
-
-    sems = pltpu.SemaphoreType.DMA((64,))
-    q = pl.pallas_call(
-        source_kernel,
-        out_shape=pltpu.HBM((13,) + grid, jnp.float32),
-        in_specs=[SMEM, SMEM, SMEM],
-        out_specs=FAR,
-        scratch_shapes=[plane(13), pltpu.SemaphoreType.DMA],
-        name="sources",
-        compiler_params=PARAMS,
-    )(flags, wells, well_rate)
-    keep, send, perm_tile = pl.pallas_call(
+    sems = pltpu.SemaphoreType.DMA((16,))
+    q, blocks, tables = call(
+        prepare_kernel,
+        "prepare",
+        out_shape=(
+            pltpu.HBM((12,) + grid, f32),
+            pltpu.HBM((mems, members, width, ny // mems, nz), f32),
+            jax.ShapeDtypeStruct((4, 16, nz), f32),
+        ),
+        in_specs=[SMEM, SMEM, FAR] + [VMEM] * 3,
+        out_specs=(FAR, FAR, VMEM),
+        scratch_shapes=[plane(12), sems],
+        compiler_params=grant,
+    )(wells, well_rate, log_perm, obs_value.reshape(4, nz), obs_var.reshape(4, nz), noise)
+    scratch = tile_scratch(ny, nz) + [plane(8)]
+    keep, send, perm_tile = call(
         first_kernel,
-        out_shape=(plane(PLANES), plane(8), plane(8)),
-        in_specs=[SMEM] + [FAR] * 3 + [VMEM, FAR],
-        out_specs=(VMEM,) * 3,
-        scratch_shapes=tile_scratch(ny, nz) + [plane(4), sems],
-        name="first",
-        compiler_params=PARAMS,
-    )(flags, log_perm, saturation, pressure_init, near(swapped), q)
+        "first",
+        out_shape=(plane(PLANES), plane(8), pltpu.HBM((8,) + grid, f32)),
+        in_specs=[FAR] * 4 + [VMEM],
+        out_specs=(VMEM, VMEM, FAR),
+        scratch_shapes=scratch + [plane(4), sems],
+        compiler_params=pltpu.CompilerParams(vmem_limit_bytes=GRANT + 1_400_000),
+    )(log_perm, saturation, pressure_init, q, near(swapped))
     onward = [(i, i + 2) for i in range(0, ends - 1, 2)] + [(ends - 1, ends)]
     onward += [(i, i - 2) for i in range(3, spaces, 2)] + [(1, 0)]
     back = [(b, a) for a, b in onward]
     got = lax.ppermute(send, "space", onward)
-
-    def local(table):
-        table = jnp.roll(table.reshape(per, rows, -1), 4, axis=1)
-        return lax.dynamic_slice_in_dim(table, around * 8, 8, axis=1).reshape(-1)
-
-    def ordered(table):
-        table = jnp.roll(table.reshape(-1, per, rows), 4, axis=2)
-        table = table.reshape(-1, per, chips // 4, 4, 8).transpose(2, 0, 3, 1, 4)
-        return table.reshape(chips // 4, -1, 4 * slots)
-
-    index, weight = local(obs_index), local(obs_weight)
-    value, var = ordered(obs_value)[:, 0], ordered(obs_var)[:, 0]
-    mixed_noise = ordered(jnp.concatenate([noise[0::2], noise[1::2]]))
-    tables = (index, weight, value, var, mixed_noise)
-    keep, send, perm_edge = pl.pallas_call(
+    keep, send, perm_edge = call(
         second_kernel,
-        out_shape=(plane(PLANES), plane(PLANES), plane(8)),
-        in_specs=[SMEM] + [VMEM] * 4 + [FAR] * (TABLES + 1),
-        out_specs=(VMEM,) * 3,
-        scratch_shapes=tile_scratch(ny, nz) + [sems],
-        name="second",
-        compiler_params=PARAMS,
-    )(flags, near(keep), near(edge_in), near(got), near(perm_tile), q, *tables)
+        "second",
+        out_shape=(plane(PLANES), plane(PLANES), pltpu.HBM((8,) + grid, f32)),
+        in_specs=[FAR] * 3 + [VMEM] * 2,
+        out_specs=(VMEM, VMEM, FAR),
+        scratch_shapes=scratch + [plane(9), sems],
+        compiler_params=grant,
+    )(perm_tile, edge_in, q, near(keep), near(got))
     got = lax.ppermute(send, "space", back)
-    columns = lax.all_to_all(log_perm, "mem", split_axis=2, concat_axis=0, tiled=True)
-    keep, send = pl.pallas_call(
+    columns = lax.all_to_all(blocks, "mem", 0, 0, tiled=True).reshape(ens, width, ny // mems, nz)
+    keep, send = call(
         third_kernel,
+        "third",
         out_shape=(plane(PLANES), plane(PLANES)),
-        in_specs=[SMEM] + [VMEM] * 3 + [FAR] * 2,
+        in_specs=[FAR] * 3 + [VMEM] * 2,
         out_specs=(VMEM,) * 2,
-        scratch_shapes=tile_scratch(ny, nz) + [sems],
-        name="third",
-        compiler_params=PARAMS,
-    )(flags, near(keep), near(got), near(perm_tile), q, columns)
+        scratch_shapes=scratch + [sems],
+        compiler_params=grant,
+    )(perm_tile, q, columns, near(keep), near(got))
     got = lax.ppermute(send, "space", onward)
-    devices = mems * spaces
-    values = pl.pallas_call(
+    taps = obs_index.T.shape
+    values = call(
         last_kernel,
-        out_shape=pltpu.VMEM((devices, nz), jnp.float32),
-        in_specs=[SMEM] * 3 + [VMEM] * 3 + [FAR],
+        "last",
+        out_shape=pltpu.HBM((devices, nz), f32),
+        in_specs=[FAR] * 4 + [VMEM] * 2,
         out_specs=VMEM,
-        scratch_shapes=tile_scratch(ny, nz) + [sems, pltpu.VMEM((nz, nz), jnp.float32)],
-        name="last",
-        compiler_params=PARAMS,
-    )(flags, index, weight, near(keep), near(got), near(perm_edge), q)
+        scratch_shapes=scratch
+        + [pltpu.SMEM(taps, jnp.int32), pltpu.SMEM(taps, f32), pltpu.VMEM((nz, nz), f32), sems],
+        compiler_params=grant,
+    )(perm_edge, q, obs_index.T, obs_weight.T, near(keep), near(got))
     values = lax.all_to_all(
         values.reshape(devices, 1, nz), ("mem", "space"), 0, 0, tiled=True
     ).reshape(devices, nz)
     return pl.pallas_call(
         solve_kernel,
-        out_shape=jax.ShapeDtypeStruct(columns.shape, jnp.float32),
-        in_specs=[VMEM] * 5,
+        out_shape=jax.ShapeDtypeStruct(columns.shape, f32),
+        in_specs=[VMEM] * 3,
         out_specs=VMEM,
-        scratch_shapes=[pltpu.VMEM((noise.shape[0] ** 2, 8, nz), jnp.float32)],
+        scratch_shapes=[pltpu.VMEM((ens**2, 8, nz), f32)],
         name="solve",
-        compiler_params=PARAMS,
-    )(near(values), value, var, mixed_noise, columns)
+    )(values, tables, columns)
 
 
 def solution(mesh):

time: 116 us -> 113 us (0.974); the launches traced: 115 us -> 113 us
  local copies, waits for them, and re-layouts: 11.2 us -> 1.14 us
  waiting for transfers between devices: 10.6 us -> 16.9 us
  Pallas kernels: 45.7 us -> 48.6 us
  blocking collectives: 37.1 us -> 39.6 us
  other arithmetic: 2.03 us -> 0.09 us
  starting transfers between devices: 7.74 us -> 6.47 us
    ppermute x2, waiting for transfers between devices: 10.6 us -> 16.9 us  [body(): got = lax.ppermute(send, 'space', onward)]
    ppermute x1, starting transfers between devices: 5.94 us -> 0.7 us  [body(): lax.ppermute(edge_out, 'space', [(0, 0), (ends, ends)] + [(i, i + 1 if i...]
    unnamed x29 -> x8, local copies, waits for them, and re-layouts: 3.48 us -> 0.08 us
    reshape x6 -> x0, local copies, waits for them, and re-layouts: 2.65 us -> none  [the longest x3 1.26 us: ordered(): table = table.reshape(-1, per, chips // 4, 4, 8).transpose(2, 0, 3, 1, 4)]
    all_to_all x1, blocking collectives: 22.2 us -> 24.7 us  [body(): lax.all_to_all(values.reshape(devices, 1, nz), ('mem', 'space'), 0, 0, ti...]
    ppermute x2, starting transfers between devices: 1.48 us -> 3.97 us  [body(): got = lax.ppermute(send, 'space', onward)]
    transpose x3 -> x0, local copies, waits for them, and re-layouts: 1.86 us -> none  [ordered(): table = table.reshape(-1, per, chips // 4, 4, 8).transpose(2, 0, 3, 1, 4)]
    pallas_call x5, Pallas kernels: 43.5 us -> 45.3 us  [the longest x1 18.6 us: body(): call(prepare_kernel, 'prepare', out_shape=(pltpu.HBM((12,) + grid, f32),...]
  transfers between devices with their start and end apart: 5 -> 5, of which waited for: 2 -> 2; matrix products, arithmetic and copies ran while one was open for 8% -> 0% of each run, Pallas kernels for 9% -> 20%
where the time goes in v3:
time: 113 us
  Pallas kernels  48.6 us (43%)
  blocking collectives  39.6 us (35%)
  waiting for transfers between devices  16.9 us (15%)
  starting transfers between devices  6.47 us (6%)
  local copies, waits for them, and re-layouts  1.14 us (1%)
    all_to_all x1, blocking collectives, body(): lax.all_to_all(values.reshape(devices, 1, nz), ('mem', 'space'), 0, 0, ti...  24.7 us
    pallas_call x1, Pallas kernels, body(): call(prepare_kernel, 'prepare', out_shape=(pltpu.HBM((12,) + grid, f32),...  18.6 us
    ppermute x2, waiting for transfers between devices, body(): got = lax.ppermute(send, 'space', onward)  16.9 us
    all_to_all x1, blocking collectives, body(): lax.all_to_all(blocks, 'mem', 0, 0, tiled=True)  14.9 us
    pallas_call x1, Pallas kernels, body(): call(second_kernel, 'second', out_shape=(plane(PLANES), plane(PLANES), pl...  7.92 us
    pallas_call x1, Pallas kernels, body(): call(third_kernel, 'third', out_shape=(plane(PLANES), plane(PLANES)), in_...  7.68 us
    pallas_call x1, Pallas kernels, body(): call(last_kernel, 'last', out_shape=pltpu.HBM((devices, nz), f32), in_spe...  7.09 us
    pallas_call x1, Pallas kernels, body(): call(first_kernel, 'first', out_shape=(plane(PLANES), plane(8), pltpu.HBM...  4.07 us
  transfers between devices with their start and end apart: 5, of which 2 were waited for; matrix products, arithmetic and copies ran while one was open for 0% of the time, Pallas kernels for 20%

profile of v3, /device:TPU:0, one launch (start us, length us, event | category | flops | bytes accessed | tf_op | source)
XLA Modules:
  0.0 112.9 jit_solution(7121876427611891689)
XLA Ops:
  0.0 0.0 copy-start
  0.0 0.0 copy-start.1
  0.0 1.0 dynamic-slice_bitcast_fusion
  1.0 0.0 copy-done
  1.0 0.1 copy-done.1
  1.1 0.1 pad_maximum_fusion
  1.2 0.1 collective-permute-start
  1.4 0.7 collective-permute-start.1
  2.1 18.6 %prepare.1 = (f32[12,128,128]{2,1,0:T(8,128)}, f32[4,2,4,32,128]{4,3,2,1,0:T(8,128)}, f32[4,16,128]{2,1,0:T(8,128)}) custom-call(s32[64]{0:T(128)} %wells.1, f32[64]{0:T(128)} %rate.1, f32[2,4,128,128]{3,2,1,0:T(8,128)} %log_perm.3, f32[4,128]{1,0:T(4,128)} %bitcast.17, f32[4,128]{1,0:T(4,128)} %bitcast.18, f32[8,512]{1,0:T(8,128)} %noise.1), custom_call_target="tpu_custom_call" | custom-call | tf_op jit(solution)/shard_map/prepare/pallas_call | solution.py:570
  20.6 0.0 collective-permute-done.swapped
  20.6 4.1 %first.1 = (f32[13,128,128]{2,1,0:T(8,128)S(1)}, f32[8,128,128]{2,1,0:T(8,128)S(1)}, f32[8,128,128]{2,1,0:T(8,128)}) custom-call(f32[2,4,128,128]{3,2,1,0:T(8,128)} %log_perm.3, f32[4,128,128]{2,1,0:T(8,128)} %own_sat.1, f32[4,128,128]{2,1,0:T(8,128)} %own_press.1, f32[12,128,128]{2,1,0:T(8,128)} %get-tuple-element.16.q, ...), custom_call_target="tpu_custom_call" | custom-call | tf_op jit(solution)/shard_map/first/pallas_call | solution.py:584
  24.7 3.4 %collective-permute-start.2 = (f32[8,128,128]{2,1,0:T(8,128)S(1)}, f32[8,128,128]{2,1,0:T(8,128)S(1)}, u32[]{:S(2)}, u32[]{:S(2)}) collective-permute-start(f32[8,128,128]{2,1,0:T(8,128)S(1)} %get-tuple-element.19), channel_id=1, source_target_pairs={{0,2},{2,4},{4,6},{6,8},{8,10},{10,12},{12,14},{14,16},{16,18},{18... | collective-permute-start | bytes 1572872 | tf_op jit(solution)/shard_map/ppermute | solution.py:596
  28.1 0.0 collective-permute-done.1.raw_in
  28.1 0.0 copy-start.2
  28.1 6.7 %collective-permute-done.2.late_in = f32[8,128,128]{2,1,0:T(8,128)S(1)} collective-permute-done((f32[8,128,128]{2,1,0:T(8,128)S(1)}, f32[8,128,128]{2,1,0:T(8,128)S(1)}, u32[]{:S(2)}, u32[]{:S(2)}) %collective-permute-start.2) | collective-permute-done | bytes 524320 | tf_op jit(solution)/shard_map/ppermute | solution.py:596
  34.8 0.0 copy-done.2
  34.8 0.0 copy-start.3
  34.8 7.9 %second.1 = (f32[13,128,128]{2,1,0:T(8,128)S(1)}, f32[13,128,128]{2,1,0:T(8,128)S(1)}, f32[8,128,128]{2,1,0:T(8,128)}) custom-call(f32[8,128,128]{2,1,0:T(8,128)} %get-tuple-element.17.perm_own.perm, f32[9,128,128]{2,1,0:T(8,128)} %copy-done.2, f32[12,128,128]{2,1,0:T(8,128)} %get-tuple-element.16.q, f32[13,128,128]{2,1,0:T(8,128)S(1)} %get-tuple-element.18.kept, ...), custom_call_target="tpu_custom_call" | custom-call | tf_op jit(solution)/shard_map/second/pallas_call | solution.py:597
  42.7 1.7 %collective-permute-start.3 = (f32[13,128,128]{2,1,0:T(8,128)S(1)}, f32[13,128,128]{2,1,0:T(8,128)S(1)}, u32[]{:S(2)}, u32[]{:S(2)}) collective-permute-start(f32[13,128,128]{2,1,0:T(8,128)S(1)} %get-tuple-element.23), channel_id=1, source_target_pairs={{2,0},{4,2},{6,4},{8,6},{10,8},{12,10},{14,12},{16,14},{18,16},{20... | collective-permute-start | bytes 2555912 | tf_op jit(solution)/shard_map/ppermute | solution.py:606
  44.5 0.0 copy-done.3
  44.5 14.9 %all_to_all.10 = f32[4,2,4,32,128]{4,3,2,1,0:T(8,128)} all-to-all(f32[4,2,4,32,128]{4,3,2,1,0:T(8,128)S(1)} %copy-done.3), channel_id=1, replica_groups=mesh['mem'=4,'space'=32] {'mem'}, dimensions={0} | all-to-all | bytes 1048576 | tf_op jit(solution)/shard_map/all_to_all | solution.py:607
  59.3 0.0 collective-permute-done.3.got
  59.3 7.7 %third.1 = (f32[13,128,128]{2,1,0:T(8,128)S(1)}, f32[13,128,128]{2,1,0:T(8,128)S(1)}) custom-call(f32[8,128,128]{2,1,0:T(8,128)} %get-tuple-element.17.perm_own.perm, f32[12,128,128]{2,1,0:T(8,128)} %get-tuple-element.16.q, f32[8,4,32,128]{3,2,1,0:T(8,128)} %bitcast.11, f32[13,128,128]{2,1,0:T(8,128)S(1)} %get-tuple-element.22.kept, ...), custom_call_target="tpu_custom_call" | custom-call | tf_op jit(solution)/shard_map/third/pallas_call | solution.py:608
  67.0 0.6 collective-permute-start.4
  67.6 10.2 %collective-permute-done.4.got = f32[13,128,128]{2,1,0:T(8,128)S(1)} collective-permute-done((f32[13,128,128]{2,1,0:T(8,128)S(1)}, f32[13,128,128]{2,1,0:T(8,128)S(1)}, u32[]{:S(2)}, u32[]{:S(2)}) %collective-permute-start.4) | collective-permute-done | bytes 852000 | tf_op jit(solution)/shard_map/ppermute | solution.py:617
  77.8 7.1 %last.1 = f32[128,128]{1,0:T(8,128)} custom-call(f32[8,128,128]{2,1,0:T(8,128)} %get-tuple-element.20.perm, f32[12,128,128]{2,1,0:T(8,128)} %get-tuple-element.16.q, s32[8,512]{1,0:T(8,128)} %bitcast.15, f32[8,512]{1,0:T(8,128)} %bitcast.16, f32[13,128,128]{2,1,0:T(8,128)S(1)} %get-tuple-element.24.kept, f32[13,128,128]{2,1,0:T(8,128)S(1)} %collective-permute-done.4.got), custom_call_target="tpu_custom_call" | custom-call | tf_op jit(solution)/shard_map/last/pallas_call | solution.py:619
  84.9 24.7 %all_to_all.11 = f32[128,1,128]{2,1,0:T(1,128)} all-to-all(f32[128,1,128]{2,1,0:T(1,128)} %bitcast.13), channel_id=1, replica_groups=mesh['mem'=4,'space'=32] {'mem','space'}, dimensions={0} | all-to-all | bytes 131072 | tf_op jit(solution)/shard_map/all_to_all | solution.py:629
  109.6 3.2 %solve.1 = f32[8,4,32,128]{3,2,1,0:T(8,128)} custom-call(f32[128,128]{1,0:T(8,128)} %bitcast.14, f32[4,16,128]{2,1,0:T(8,128)} %get-tuple-element.26.tables, f32[8,4,32,128]{3,2,1,0:T(8,128)} %bitcast.12), custom_call_target="tpu_custom_call" | custom-call | tf_op jit(solution)/shard_map/solve/pallas_call | solution.py:632
  (3 shorter events, 0.1 us)
Async XLA Ops:
  0.0 1.0 copy-start
  0.0 1.1 copy-start.1
  1.2 19.5 %collective-permute-start = (f32[12,128,128]{2,1,0:T(8,128)S(1)}, f32[12,128,128]{2,1,0:T(8,128)S(1)}, u32[]{:S(2)}, u32[]{:S(2)}) collective-permute-start(f32[12,128,128]{2,1,0:T(8,128)S(1)} %pad_maximum_fusion), channel_id=1, source_target_pairs={{0,1},{1,0},{2,3},{3,2},{4,5},{5,4},{6,7},{7,6},{8,9},{9,8},{10,11... | collective-permute-start | bytes 2359304 | tf_op jit(solution)/shard_map/ppermute | solution.py:561
  1.4 26.7 %collective-permute-start.1 = (f32[9,128,128]{2,1,0:T(8,128)S(1)}, f32[9,128,128]{2,1,0:T(8,128)S(1)}, u32[]{:S(2)}, u32[]{:S(2)}) collective-permute-start(f32[9,128,128]{2,1,0:T(8,128)S(1)} %pad_maximum_fusion.1), channel_id=1, source_target_pairs={{0,0},{31,31},{1,2},{2,1},{3,4},{4,3},{5,6},{6,5},{7,8},{8,7},{9,1... | collective-permute-start | bytes 1769480 | tf_op jit(solution)/shard_map/ppermute | solution.py:564
  24.7 10.1 %collective-permute-start.2 = (f32[8,128,128]{2,1,0:T(8,128)S(1)}, f32[8,128,128]{2,1,0:T(8,128)S(1)}, u32[]{:S(2)}, u32[]{:S(2)}) collective-permute-start(f32[8,128,128]{2,1,0:T(8,128)S(1)} %get-tuple-element.19), channel_id=1, source_target_pairs={{0,2},{2,4},{4,6},{6,8},{8,10},{10,12},{12,14},{14,16},{16,18},{18... | collective-permute-start | bytes 1572872 | tf_op jit(solution)/shard_map/ppermute | solution.py:596
  28.1 6.7 %copy-start.2 = (f32[9,128,128]{2,1,0:T(8,128)}, f32[9,128,128]{2,1,0:T(8,128)S(1)}, u32[]{:S(2)}) copy-start(f32[9,128,128]{2,1,0:T(8,128)S(1)} %collective-permute-done.1.raw_in) | copy-start | bytes 1769476
  34.8 9.7 %copy-start.3 = (f32[4,2,4,32,128]{4,3,2,1,0:T(8,128)S(1)}, f32[4,2,4,32,128]{4,3,2,1,0:T(8,128)}, u32[]{:S(2)}) copy-start(f32[4,2,4,32,128]{4,3,2,1,0:T(8,128)} %get-tuple-element.21) | copy-start | bytes 1572868
  42.7 16.6 %collective-permute-start.3 = (f32[13,128,128]{2,1,0:T(8,128)S(1)}, f32[13,128,128]{2,1,0:T(8,128)S(1)}, u32[]{:S(2)}, u32[]{:S(2)}) collective-permute-start(f32[13,128,128]{2,1,0:T(8,128)S(1)} %get-tuple-element.23), channel_id=1, source_target_pairs={{2,0},{4,2},{6,4},{8,6},{10,8},{12,10},{14,12},{16,14},{18,16},{20... | collective-permute-start | bytes 2555912 | tf_op jit(solution)/shard_map/ppermute | solution.py:606
  67.0 10.8 %collective-permute-start.4 = (f32[13,128,128]{2,1,0:T(8,128)S(1)}, f32[13,128,128]{2,1,0:T(8,128)S(1)}, u32[]{:S(2)}, u32[]{:S(2)}) collective-permute-start(f32[13,128,128]{2,1,0:T(8,128)S(1)} %get-tuple-element.25), channel_id=1, source_target_pairs={{0,2},{2,4},{4,6},{6,8},{8,10},{10,12},{12,14},{14,16},{16,18},{18... | collective-permute-start | bytes 2555912 | tf_op jit(solution)/shard_map/ppermute | solution.py:617

commit v4 on v3

--- a/solution.py
+++ b/solution.py
@@ -406,13 +406,10 @@
     )
 
 
-def prepare_kernel(chips, wells, rate, log_perm, value, var, noise, q_out, blocks, tables, q, sems):
+def prepare_kernel(chips, wells, rate, log_perm, value, var, noise, q_out, blocks, tables, q, held, sems):
     rows = log_perm.shape[2] // blocks.shape[0]
-    copies = issue(
-        [(log_perm.at[:, :, pl.ds(b * rows, rows), :], blocks.at[b]) for b in range(blocks.shape[0])],
-        sems,
-        0,
-    )
+    count = blocks.shape[0]
+    load = issue([(log_perm, held)], sems, count)
     odd, chip, _ = position(chips)
     ny, nz = q.shape[1], q.shape[2]
     lane = lax.broadcasted_iota(jnp.int32, (1, nz), 1)
@@ -429,7 +426,11 @@
         return carry
 
     lax.fori_loop(0, wells.shape[0], one, 0, unroll=4)
-    copies += issue([(q, q_out)], sems, len(copies))
+    copies = issue([(q, q_out)], sems, count + 1)
+    drain(load)
+    copies += issue(
+        [(held.at[:, :, pl.ds(b * rows, rows), :], blocks.at[b]) for b in range(count)], sems, 0
+    )
     groups, lanes = value.shape
     wide = lanes // groups
     half = noise.shape[0] // 2
@@ -446,7 +447,10 @@
     drain(copies)
 
 
-def solve_kernel(values, tables, columns, out, coef):
+def solve_kernel(values, tables, columns_in, out_to, coef, columns, out, sems):
+    count = columns.shape[1]
+    loads = issue([(columns_in.at[:, n], columns.at[:, n]) for n in range(count)], sems, 0)
+
     groups = tables.shape[0]
     ens = columns.shape[0]
     half = ens // 2
@@ -507,7 +511,9 @@
             at = natural(j) * ens + natural(m)
             coef[at] = jnp.broadcast_to(mixing[j : j + 1, m : m + 1], (8, wide))
 
-    def one(n, carry):
+    stores = []
+    for n in range(count):
+        loads[n].wait()
         part = [columns[j, n] for j in range(ens)]
         for m in range(ens):
             for r0 in range(0, rows, 8):
@@ -515,9 +521,8 @@
                 for j in range(1, ens):
                     total = total + coef[j * ens + m] * part[j][r0 : r0 + 8]
                 out[m, n, r0 : r0 + 8, :] = total
-        return carry
-
-    lax.fori_loop(0, columns.shape[1], one, 0)
+        stores += issue([(out.at[:, n], out_to.at[:, n])], sems, count + n)
+    drain(stores)
 
 
 def body(
@@ -577,7 +582,7 @@
         ),
         in_specs=[SMEM, SMEM, FAR] + [VMEM] * 3,
         out_specs=(FAR, FAR, VMEM),
-        scratch_shapes=[plane(12), sems],
+        scratch_shapes=[plane(12), pltpu.VMEM(log_perm.shape, f32), sems],
         compiler_params=grant,
     )(wells, well_rate, log_perm, obs_value.reshape(4, nz), obs_var.reshape(4, nz), noise)
     scratch = tile_scratch(ny, nz) + [plane(8)]
@@ -632,9 +637,11 @@
     return pl.pallas_call(
         solve_kernel,
         out_shape=jax.ShapeDtypeStruct(columns.shape, f32),
-        in_specs=[VMEM] * 3,
-        out_specs=VMEM,
-        scratch_shapes=[pltpu.VMEM((ens**2, 8, nz), f32)],
+        in_specs=[VMEM, VMEM, FAR],
+        out_specs=FAR,
+        scratch_shapes=[pltpu.VMEM((ens**2, 8, nz), f32)]
+        + [pltpu.VMEM(columns.shape, f32) for _ in range(2)]
+        + [sems],
         name="solve",
     )(values, tables, columns)
 

time: 113 us -> 98 us (0.87)
  Pallas kernels: 48.6 us -> 33.1 us
    pallas_call x1, Pallas kernels: 18.6 us -> 3.4 us  [body(): call(prepare_kernel, 'prepare', out_shape=(pltpu.HBM((12,) + grid, f32),...]
  transfers between devices with their start and end apart: 5 -> 5, of which waited for: 2 -> 2; matrix products, arithmetic and copies ran while one was open for 0% -> 0% of each run, Pallas kernels for 20% -> 8%
where the time goes in v4:
time: 98 us; the launch traced here: 97.5 us
  blocking collectives  39.6 us (40%)
  Pallas kernels  33.1 us (34%)
  waiting for transfers between devices  16.9 us (17%)
  starting transfers between devices  6.47 us (7%)
  local copies, waits for them, and re-layouts  1.14 us (1%)
    all_to_all x1, blocking collectives, body(): lax.all_to_all(values.reshape(devices, 1, nz), ('mem', 'space'), 0, 0, ti...  24.7 us
    ppermute x2, waiting for transfers between devices, body(): got = lax.ppermute(send, 'space', onward)  16.9 us
    all_to_all x1, blocking collectives, body(): lax.all_to_all(blocks, 'mem', 0, 0, tiled=True)  14.9 us
    pallas_call x1, Pallas kernels, body(): call(second_kernel, 'second', out_shape=(plane(PLANES), plane(PLANES), pl...  7.92 us
    pallas_call x1, Pallas kernels, body(): call(third_kernel, 'third', out_shape=(plane(PLANES), plane(PLANES)), in_...  7.68 us
    pallas_call x1, Pallas kernels, body(): call(last_kernel, 'last', out_shape=pltpu.HBM((devices, nz), f32), in_spe...  7.09 us
    pallas_call x1, Pallas kernels, body(): call(first_kernel, 'first', out_shape=(plane(PLANES), plane(8), pltpu.HBM...  4.07 us
    ppermute x2, starting transfers between devices, body(): got = lax.ppermute(send, 'space', onward)  3.97 us
  transfers between devices with their start and end apart: 5, of which 2 were waited for; matrix products, arithmetic and copies ran while one was open for 0% of the time, Pallas kernels for 8%

profile of v4, /device:TPU:0, one launch (start us, length us, event | category | flops | bytes accessed | tf_op | source)
XLA Modules:
  0.0 97.5 jit_solution(7246451229734931269)
XLA Ops:
  0.0 0.0 copy-start
  0.0 0.0 copy-start.1
  0.0 1.0 %dynamic-slice_bitcast_fusion = f32[4,128,128]{2,1,0:T(8,128)S(1)} fusion(f32[2,4,128,128]{3,2,1,0:T(8,128)} %log_perm.3, s32[]{:T(128)S(6)} %select_n.17), kind=kLoop, calls=%fused_computation.2 | loop fusion | bytes 524292 | tf_op jit(solution)/shard_map/squeeze | solution.py:564
  1.0 0.0 copy-done
  1.0 0.1 copy-done.1
  1.1 0.1 pad_maximum_fusion
  1.2 0.1 collective-permute-start
  1.4 0.7 collective-permute-start.1
  2.1 3.4 %prepare.1 = (f32[12,128,128]{2,1,0:T(8,128)}, f32[4,2,4,32,128]{4,3,2,1,0:T(8,128)}, f32[4,16,128]{2,1,0:T(8,128)}) custom-call(s32[64]{0:T(128)} %wells.1, f32[64]{0:T(128)} %rate.1, f32[2,4,128,128]{3,2,1,0:T(8,128)} %log_perm.3, f32[4,128]{1,0:T(4,128)} %bitcast.17, f32[4,128]{1,0:T(4,128)} %bitcast.18, f32[8,512]{1,0:T(8,128)} %noise.1), custom_call_target="tpu_custom_call" | custom-call | tf_op jit(solution)/shard_map/prepare/pallas_call | solution.py:575
  5.5 0.0 collective-permute-done.swapped
  5.5 4.1 %first.1 = (f32[13,128,128]{2,1,0:T(8,128)S(1)}, f32[8,128,128]{2,1,0:T(8,128)S(1)}, f32[8,128,128]{2,1,0:T(8,128)}) custom-call(f32[2,4,128,128]{3,2,1,0:T(8,128)} %log_perm.3, f32[4,128,128]{2,1,0:T(8,128)} %own_sat.1, f32[4,128,128]{2,1,0:T(8,128)} %own_press.1, f32[12,128,128]{2,1,0:T(8,128)} %get-tuple-element.16.q, ...), custom_call_target="tpu_custom_call" | custom-call | tf_op jit(solution)/shard_map/first/pallas_call | solution.py:589
  9.6 3.4 %collective-permute-start.2 = (f32[8,128,128]{2,1,0:T(8,128)S(1)}, f32[8,128,128]{2,1,0:T(8,128)S(1)}, u32[]{:S(2)}, u32[]{:S(2)}) collective-permute-start(f32[8,128,128]{2,1,0:T(8,128)S(1)} %get-tuple-element.19), channel_id=1, source_target_pairs={{0,2},{2,4},{4,6},{6,8},{8,10},{10,12},{12,14},{14,16},{16,18},{18... | collective-permute-start | bytes 1572872 | tf_op jit(solution)/shard_map/ppermute | solution.py:601
  13.0 0.0 collective-permute-done.1.raw_in
  13.0 0.0 copy-start.2
  13.0 6.7 %collective-permute-done.2.late_in = f32[8,128,128]{2,1,0:T(8,128)S(1)} collective-permute-done((f32[8,128,128]{2,1,0:T(8,128)S(1)}, f32[8,128,128]{2,1,0:T(8,128)S(1)}, u32[]{:S(2)}, u32[]{:S(2)}) %collective-permute-start.2) | collective-permute-done | bytes 524320 | tf_op jit(solution)/shard_map/ppermute | solution.py:601
  19.7 0.0 copy-done.2
  19.7 0.0 copy-start.3
  19.7 7.9 %second.1 = (f32[13,128,128]{2,1,0:T(8,128)S(1)}, f32[13,128,128]{2,1,0:T(8,128)S(1)}, f32[8,128,128]{2,1,0:T(8,128)}) custom-call(f32[8,128,128]{2,1,0:T(8,128)} %get-tuple-element.17.perm_own.perm, f32[9,128,128]{2,1,0:T(8,128)} %copy-done.2, f32[12,128,128]{2,1,0:T(8,128)} %get-tuple-element.16.q, f32[13,128,128]{2,1,0:T(8,128)S(1)} %get-tuple-element.18.kept, ...), custom_call_target="tpu_custom_call" | custom-call | tf_op jit(solution)/shard_map/second/pallas_call | solution.py:602
  27.6 1.7 %collective-permute-start.3 = (f32[13,128,128]{2,1,0:T(8,128)S(1)}, f32[13,128,128]{2,1,0:T(8,128)S(1)}, u32[]{:S(2)}, u32[]{:S(2)}) collective-permute-start(f32[13,128,128]{2,1,0:T(8,128)S(1)} %get-tuple-element.23), channel_id=1, source_target_pairs={{2,0},{4,2},{6,4},{8,6},{10,8},{12,10},{14,12},{16,14},{18,16},{20... | collective-permute-start | bytes 2555912 | tf_op jit(solution)/shard_map/ppermute | solution.py:611
  29.3 0.0 copy-done.3
  29.3 14.9 %all_to_all.10 = f32[4,2,4,32,128]{4,3,2,1,0:T(8,128)} all-to-all(f32[4,2,4,32,128]{4,3,2,1,0:T(8,128)S(1)} %copy-done.3), channel_id=1, replica_groups=mesh['mem'=4,'space'=32] {'mem'}, dimensions={0} | all-to-all | bytes 1048576 | tf_op jit(solution)/shard_map/all_to_all | solution.py:612
  44.2 0.0 collective-permute-done.3.got
  44.2 7.7 %third.1 = (f32[13,128,128]{2,1,0:T(8,128)S(1)}, f32[13,128,128]{2,1,0:T(8,128)S(1)}) custom-call(f32[8,128,128]{2,1,0:T(8,128)} %get-tuple-element.17.perm_own.perm, f32[12,128,128]{2,1,0:T(8,128)} %get-tuple-element.16.q, f32[8,4,32,128]{3,2,1,0:T(8,128)} %bitcast.11, f32[13,128,128]{2,1,0:T(8,128)S(1)} %get-tuple-element.22.kept, ...), custom_call_target="tpu_custom_call" | custom-call | tf_op jit(solution)/shard_map/third/pallas_call | solution.py:613
  51.9 0.6 collective-permute-start.4
  52.5 10.2 %collective-permute-done.4.got = f32[13,128,128]{2,1,0:T(8,128)S(1)} collective-permute-done((f32[13,128,128]{2,1,0:T(8,128)S(1)}, f32[13,128,128]{2,1,0:T(8,128)S(1)}, u32[]{:S(2)}, u32[]{:S(2)}) %collective-permute-start.4) | collective-permute-done | bytes 852000 | tf_op jit(solution)/shard_map/ppermute | solution.py:622
  62.7 7.1 %last.1 = f32[128,128]{1,0:T(8,128)} custom-call(f32[8,128,128]{2,1,0:T(8,128)} %get-tuple-element.20.perm, f32[12,128,128]{2,1,0:T(8,128)} %get-tuple-element.16.q, s32[8,512]{1,0:T(8,128)} %bitcast.15, f32[8,512]{1,0:T(8,128)} %bitcast.16, f32[13,128,128]{2,1,0:T(8,128)S(1)} %get-tuple-element.24.kept, f32[13,128,128]{2,1,0:T(8,128)S(1)} %collective-permute-done.4.got), custom_call_target="tpu_custom_call" | custom-call | tf_op jit(solution)/shard_map/last/pallas_call | solution.py:624
  69.8 24.7 %all_to_all.11 = f32[128,1,128]{2,1,0:T(1,128)} all-to-all(f32[128,1,128]{2,1,0:T(1,128)} %bitcast.13), channel_id=1, replica_groups=mesh['mem'=4,'space'=32] {'mem','space'}, dimensions={0} | all-to-all | bytes 131072 | tf_op jit(solution)/shard_map/all_to_all | solution.py:634
  94.5 3.0 %solve.1 = f32[8,4,32,128]{3,2,1,0:T(8,128)} custom-call(f32[128,128]{1,0:T(8,128)} %bitcast.14, f32[4,16,128]{2,1,0:T(8,128)} %get-tuple-element.26.tables, f32[8,4,32,128]{3,2,1,0:T(8,128)} %bitcast.12), custom_call_target="tpu_custom_call" | custom-call | tf_op jit(solution)/shard_map/solve/pallas_call | solution.py:637
  (3 shorter events, 0.1 us)
Async XLA Ops:
  0.0 1.0 %copy-start = (f32[4,128,128]{2,1,0:T(8,128)S(1)}, f32[4,128,128]{2,1,0:T(8,128)}, u32[]{:S(2)}) copy-start(f32[4,128,128]{2,1,0:T(8,128)} %own_press.1) | copy-start | bytes 786436
  0.0 1.1 %copy-start.1 = (f32[4,128,128]{2,1,0:T(8,128)S(1)}, f32[4,128,128]{2,1,0:T(8,128)}, u32[]{:S(2)}) copy-start(f32[4,128,128]{2,1,0:T(8,128)} %own_sat.1) | copy-start | bytes 786436
  1.2 4.3 %collective-permute-start = (f32[12,128,128]{2,1,0:T(8,128)S(1)}, f32[12,128,128]{2,1,0:T(8,128)S(1)}, u32[]{:S(2)}, u32[]{:S(2)}) collective-permute-start(f32[12,128,128]{2,1,0:T(8,128)S(1)} %pad_maximum_fusion), channel_id=1, source_target_pairs={{0,1},{1,0},{2,3},{3,2},{4,5},{5,4},{6,7},{7,6},{8,9},{9,8},{10,11... | collective-permute-start | bytes 2359304 | tf_op jit(solution)/shard_map/ppermute | solution.py:566
  1.4 11.6 %collective-permute-start.1 = (f32[9,128,128]{2,1,0:T(8,128)S(1)}, f32[9,128,128]{2,1,0:T(8,128)S(1)}, u32[]{:S(2)}, u32[]{:S(2)}) collective-permute-start(f32[9,128,128]{2,1,0:T(8,128)S(1)} %pad_maximum_fusion.1), channel_id=1, source_target_pairs={{0,0},{31,31},{1,2},{2,1},{3,4},{4,3},{5,6},{6,5},{7,8},{8,7},{9,1... | collective-permute-start | bytes 1769480 | tf_op jit(solution)/shard_map/ppermute | solution.py:569
  9.6 10.1 %collective-permute-start.2 = (f32[8,128,128]{2,1,0:T(8,128)S(1)}, f32[8,128,128]{2,1,0:T(8,128)S(1)}, u32[]{:S(2)}, u32[]{:S(2)}) collective-permute-start(f32[8,128,128]{2,1,0:T(8,128)S(1)} %get-tuple-element.19), channel_id=1, source_target_pairs={{0,2},{2,4},{4,6},{6,8},{8,10},{10,12},{12,14},{14,16},{16,18},{18... | collective-permute-start | bytes 1572872 | tf_op jit(solution)/shard_map/ppermute | solution.py:601
  13.0 6.7 %copy-start.2 = (f32[9,128,128]{2,1,0:T(8,128)}, f32[9,128,128]{2,1,0:T(8,128)S(1)}, u32[]{:S(2)}) copy-start(f32[9,128,128]{2,1,0:T(8,128)S(1)} %collective-permute-done.1.raw_in) | copy-start | bytes 1769476
  19.7 9.7 %copy-start.3 = (f32[4,2,4,32,128]{4,3,2,1,0:T(8,128)S(1)}, f32[4,2,4,32,128]{4,3,2,1,0:T(8,128)}, u32[]{:S(2)}) copy-start(f32[4,2,4,32,128]{4,3,2,1,0:T(8,128)} %get-tuple-element.21) | copy-start | bytes 1572868
  27.6 16.6 %collective-permute-start.3 = (f32[13,128,128]{2,1,0:T(8,128)S(1)}, f32[13,128,128]{2,1,0:T(8,128)S(1)}, u32[]{:S(2)}, u32[]{:S(2)}) collective-permute-start(f32[13,128,128]{2,1,0:T(8,128)S(1)} %get-tuple-element.23), channel_id=1, source_target_pairs={{2,0},{4,2},{6,4},{8,6},{10,8},{12,10},{14,12},{16,14},{18,16},{20... | collective-permute-start | bytes 2555912 | tf_op jit(solution)/shard_map/ppermute | solution.py:611
  51.9 10.8 %collective-permute-start.4 = (f32[13,128,128]{2,1,0:T(8,128)S(1)}, f32[13,128,128]{2,1,0:T(8,128)S(1)}, u32[]{:S(2)}, u32[]{:S(2)}) collective-permute-start(f32[13,128,128]{2,1,0:T(8,128)S(1)} %get-tuple-element.25), channel_id=1, source_target_pairs={{0,2},{2,4},{4,6},{6,8},{8,10},{10,12},{12,14},{14,16},{16,18},{18... | collective-permute-start | bytes 2555912 | tf_op jit(solution)/shard_map/ppermute | solution.py:622

commit v5 on v4

--- a/solution.py
+++ b/solution.py
@@ -27,11 +27,12 @@
 
 
 class Tile:
-    def __init__(self, lam_a, lam_b, frac_a, frac_b, p_a, p_b, s_a, s_b, perm, q, q_row, cut):
+    def __init__(self, lam_a, lam_b, frac_a, frac_b, p_a, p_b, s_a, s_b, sides, perm, q, q_row, cut):
         self.lam = (lam_a, lam_b)
         self.frac = (frac_a, frac_b)
         self.p = (p_a, p_b)
         self.s = (s_a, s_b)
+        self.sides = sides
         self.perm = perm
         self.q = q
         self.q_row = q_row
@@ -47,18 +48,45 @@
                 ref[r, tall - PAD : tall, :] = edge
             ref[5, :, :] = jnp.zeros((tall, wide), jnp.float32)
 
+    def places(self, row):
+        st = row + 1 + (row >= 4).astype(jnp.int32)
+        joined = 1 - self.cut
+        up = st + 1 + jnp.where(row == 3, joined, 0)
+        down = st - 1 - jnp.where(row == 4, joined, 0)
+        return st, up, down
+
     def rows(self, first, last, fn):
         def one(row, carry):
-            far = row >= 4
-            st = row + 1 + far.astype(jnp.int32)
-            joined = 1 - self.cut
-            up = st + 1 + jnp.where(row == 3, joined, 0)
-            down = st - 1 - jnp.where(row == 4, joined, 0)
             for y0 in range(0, self.ny, CHUNK):
-                fn(row, st, up, down, y0)
+                fn(row, *self.places(row), y0)
             return carry
 
         lax.fori_loop(first, last + 1, one, 0)
+
+    def run(self, phases, primed=False, then=None):
+        def all_of(row, slot, which):
+            for y0 in range(0, self.ny, CHUNK):
+                which(row, *self.places(row), y0, slot)
+
+        if not primed:
+            all_of(jnp.int32(phases[0][0]), 0, phases[0][2])
+        for phase, follower in zip(phases, phases[1:] + [then]):
+            first, last, ahead, fn = phase
+
+            def two(n, carry, first=first, ahead=ahead, fn=fn):
+                row = first + 2 * n
+                all_of(row + 1, 1, ahead)
+                all_of(row, 0, fn)
+                all_of(row + 2, 0, ahead)
+                all_of(row + 1, 1, fn)
+                return carry
+
+            lax.fori_loop(0, (last - first) // 2, two, 0)
+            all_of(jnp.int32(last), 1, ahead)
+            all_of(jnp.int32(last - 1), 0, fn)
+            if follower is not None:
+                all_of(jnp.int32(follower[0]), 0, follower[2])
+            all_of(jnp.int32(last), 1, fn)
 
     def props(self, level, first, last):
         def fn(row, st, up, down, y0):
@@ -77,7 +105,17 @@
         lane = lax.broadcasted_iota(jnp.int32, (CHUNK, lanes), 1)
         is_first, is_last = lane == 0, lane == lanes - 1
 
-        def fn(row, st, up, down, y0):
+        def ahead(row, st, up, down, y0, slot):
+            inner = pl.ds(PAD + y0, CHUNK)
+            lam, frac, press = lam_r[st, inner, :], frac_r[st, inner, :], p_r[st, inner, :]
+            flux = (lam + pltpu.roll(lam, lanes - 1, 1)) * (press - pltpu.roll(press, lanes - 1, 1))
+            moved = flux * jnp.where(flux > 0.0, frac, pltpu.roll(frac, lanes - 1, 1))
+            edge = jnp.maximum(lam * press, 0.0) * frac
+            out = jnp.where(is_last, edge, moved)
+            out = out + jnp.where(is_first, edge, pltpu.roll(-moved, 1, 1))
+            self.sides[2 * slot, pl.ds(y0, CHUNK), :] = out
+
+        def fn(row, st, up, down, y0, slot):
             inner = pl.ds(PAD + y0, CHUNK)
             lam, frac, press = lam_r[st, inner, :], frac_r[st, inner, :], p_r[st, inner, :]
 
@@ -88,11 +126,7 @@
             out = face(up, inner) + face(down, inner)
             out = out + face(st, pl.ds(PAD + y0 + 1, CHUNK))
             out = out + face(st, pl.ds(PAD + y0 - 1, CHUNK))
-            flux = (lam + pltpu.roll(lam, lanes - 1, 1)) * (press - pltpu.roll(press, lanes - 1, 1))
-            moved = flux * jnp.where(flux > 0.0, frac, pltpu.roll(frac, lanes - 1, 1))
-            edge = jnp.maximum(lam * press, 0.0) * frac
-            out = out + jnp.where(is_last, edge, moved)
-            out = out + jnp.where(is_first, edge, pltpu.roll(-moved, 1, 1))
+            out = out + self.sides[2 * slot, pl.ds(y0, CHUNK), :]
             q = self.q[self.q_row(row), pl.ds(y0, CHUNK), :]
             water = q * jnp.where(q > 0.0, 1.0, frac)
             sat = self.s[level][st, pl.ds(y0, CHUNK), :]
@@ -102,7 +136,7 @@
             self.lam[new][st, inner, :] = lam
             self.frac[new][st, inner, :] = frac
 
-        self.rows(first, last, fn)
+        return first, last, ahead, fn
 
     def pressure(self, level, first, last):
         new = 1 - level
@@ -111,11 +145,23 @@
         lane = lax.broadcasted_iota(jnp.int32, (CHUNK, lanes), 1)
         not_first, not_last = lane > 0, lane < lanes - 1
 
-        def fn(row, st, up, down, y0):
+        def ahead(row, st, up, down, y0, slot):
+            inner = pl.ds(PAD + y0, CHUNK)
+            lam, press = lam_r[st, inner, :], p_r[st, inner, :]
+            numer, denom = 0.0, 0.0
+            for shift, mask in ((lanes - 1, not_last), (1, not_first)):
+                trans = lam + jnp.where(mask, pltpu.roll(lam, shift, 1), 0.0)
+                numer = numer + trans * jnp.where(mask, pltpu.roll(press, shift, 1), 0.0)
+                denom = denom + trans
+            self.sides[2 * slot, pl.ds(y0, CHUNK), :] = numer
+            self.sides[2 * slot + 1, pl.ds(y0, CHUNK), :] = denom
+
+        def fn(row, st, up, down, y0, slot):
             inner = pl.ds(PAD + y0, CHUNK)
             lam, press = lam_r[st, inner, :], p_r[st, inner, :]
             numer = press + self.q[self.q_row(row), pl.ds(y0, CHUNK), :]
-            denom = jnp.ones_like(lam)
+            numer = numer + self.sides[2 * slot, pl.ds(y0, CHUNK), :]
+            denom = 1.0 + self.sides[2 * slot + 1, pl.ds(y0, CHUNK), :]
             for index, where in (
                 (up, inner),
                 (down, inner),
@@ -125,13 +171,9 @@
                 trans = lam + lam_r[index, where, :]
                 numer = numer + trans * p_r[index, where, :]
                 denom = denom + trans
-            for shift, mask in ((lanes - 1, not_last), (1, not_first)):
-                trans = lam + jnp.where(mask, pltpu.roll(lam, shift, 1), 0.0)
-                numer = numer + trans * jnp.where(mask, pltpu.roll(press, shift, 1), 0.0)
-                denom = denom + trans
             out_r[st, inner, :] = numer / denom
 
-        self.rows(first, last, fn)
+        return first, last, ahead, fn
 
 
 def props(perm_half, sat):
@@ -148,7 +190,7 @@
 def tile_scratch(ny, nz):
     tall = ny + 2 * PAD
     wide = [pltpu.VMEM((11, tall, nz), jnp.float32) for _ in range(6)]
-    flat = [pltpu.VMEM((count, ny, nz), jnp.float32) for count in (11, 11, 12)]
+    flat = [pltpu.VMEM((count, ny, nz), jnp.float32) for count in (11, 11, 4, 12)]
     return wide + flat
 
 
@@ -238,22 +280,20 @@
     return start, s_next, p_next, last
 
 
-def advance(tile, keep, send, send_early):
+def advance(tile, keep, send, send_early, primed=True):
     base = 0 if send_early else S1[0]
     move(give_early(tile, keep, send, send_early))
-    tile.saturate(0, 1, 6)
-    tile.pressure(0, 2, 5)
-    tile.saturate(1, 3, 4)
+    tile.run([tile.saturate(0, 1, 6), tile.pressure(0, 2, 5), tile.saturate(1, 3, 4)], primed)
     pairs = []
     for out, near_row, at in ((send, (7, -1), base), (keep, (0, 1), 0)):
         pairs += give_late(tile, out, near_row, at) + give_last(tile, out, near_row, at)
     move(pairs)
 
 
-def first_kernel(chips, log_perm, own_sat, own_press, q, swapped, keep, send, perm_out, *refs):
+def first_kernel(chips, wells, rate, log_perm, own_sat, own_press, swapped, keep, send, perm_out, q_out, *refs):
     odd, _, _ = position(chips)
-    perm, raw, sems = refs[9:]
-    tile = Tile(*refs[:8], perm, refs[8], lambda row: row + 4, jnp.int32(0))
+    perm, raw, sems = refs[10:]
+    tile = Tile(*refs[:9], perm, refs[9], lambda row: row + 4, jnp.int32(0))
     inner = pl.ds(PAD, tile.ny)
 
     def place(n):
@@ -264,8 +304,9 @@
         pairs.append((own_sat.at[place(n)], tile.s[0].at[spot(n)]))
         pairs.append((own_press.at[place(n)], tile.p[0].at[spot(n), inner]))
     copies = issue(pairs, sems, 0)
-    q_copy = issue([(q, tile.q)], sems, len(pairs))
     tile.clear()
+    fill_sources(chips, wells, rate, tile.q)
+    out_copies = issue([(tile.q, q_out)], sems, 9)
     pairs = []
     for n in range(4):
         pairs.append((swapped.at[4 + place(n)], tile.s[0].at[spot(4 + n)]))
@@ -284,14 +325,13 @@
     halve(swapped, 4)
     drain(copies)
     halve(raw, 0)
-    perm_copy = issue([(perm, perm_out)], sems, 10)
+    out_copies += issue([(perm, perm_out)], sems, 10)
     tile.props(0, 0, 7)
-    drain(q_copy)
-    advance(tile, keep, send, False)
-    drain(perm_copy)
-
-
-def fill(tile, sides, perm_copy, q_copy):
+    advance(tile, keep, send, False, False)
+    drain(out_copies)
+
+
+def fill(tile, sides, perm_copy, q_copy, then=None):
     tile.clear()
     groups = [sum((side[n] for side in sides), []) for n in range(4)]
     move(groups[0] + groups[1] + groups[2])
@@ -300,23 +340,28 @@
     tile.props(1, 0, 2)
     tile.props(1, 5, 7)
     drain(q_copy)
-    tile.saturate(0, 3, 4)
-    tile.pressure(0, 2, 5)
     move(groups[3])
     tile.props(0, 0, 0)
     tile.props(0, 7, 7)
-    tile.saturate(1, 1, 6)
-    tile.pressure(1, 0, 7)
+    tile.run(
+        [
+            tile.saturate(0, 3, 4),
+            tile.pressure(0, 2, 5),
+            tile.saturate(1, 1, 6),
+            tile.pressure(1, 0, 7),
+        ],
+        then=then,
+    )
 
 
 def edge_q(cut):
     return lambda row: jnp.where((cut == 1) & (row >= 4), row, 7 - row)
 
 
-def second_kernel(chips, perm_own, raw_in, q, kept, late_in, keep, send, perm_out, *refs):
+def second_kernel(chips, perm_own, raw_in, q, log_perm, value_in, var_in, noise_in, kept, late_in, keep, send, perm_out, blocks, tables, *refs):
     odd, _, end = position(chips)
-    perm, raw, sems = refs[9:]
-    tile = Tile(*refs[:8], perm, refs[8], edge_q(end), end)
+    perm, raw, held, value, var, noise, sems = refs[10:]
+    tile = Tile(*refs[:9], perm, refs[9], edge_q(end), end)
     straight = odd ^ end
 
     def place(n, count):
@@ -329,6 +374,7 @@
 
     copies = issue([(raw_in, raw)] + [(perm_own.at[3 - d], perm.at[d]) for d in range(4)], sems, 0)
     q_copy = issue([(q, tile.q)], sems, 5)
+    load = issue([(log_perm, held), (value_in, value), (var_in, var), (noise_in, noise)], sems, 7)
     drain(copies)
 
     def permeability(d, carry):
@@ -343,9 +389,17 @@
         take(tile, lambda n: kept.at[n], lambda n: kept.at[n], 4, -1),
         take(tile, early, lambda n: late_in.at[n - S1[0]], 6, 1),
     )
-    fill(tile, sides, [], q_copy)
+    fill(tile, sides, [], q_copy, tile.saturate(0, 1, 6))
+    drain(load)
+    count = blocks.shape[0]
+    rows = log_perm.shape[2] // count
+    pieces = issue(
+        [(held.at[:, :, pl.ds(b * rows, rows), :], blocks.at[b]) for b in range(count)], sems, 11
+    )
+    order_tables(value, var, noise, tables)
     advance(tile, keep, send, True)
     drain(perm_copy)
+    drain(pieces)
 
 
 def both_sides(tile, kept, got):
@@ -357,18 +411,18 @@
 
 def third_kernel(perm, q, columns, kept, got, keep, send, *refs):
     del columns
-    tile = Tile(*refs[:8], refs[9], refs[8], lambda row: row + 4, jnp.int32(0))
-    sems = refs[10]
+    tile = Tile(*refs[:9], refs[10], refs[9], lambda row: row + 4, jnp.int32(0))
+    sems = refs[11]
     perm_copy = issue([(perm, tile.perm)], sems, 0)
     q_copy = issue([(q, tile.q)], sems, 1)
-    fill(tile, both_sides(tile, kept, got), perm_copy, q_copy)
+    fill(tile, both_sides(tile, kept, got), perm_copy, q_copy, tile.saturate(0, 1, 6))
     advance(tile, keep, send, True)
 
 
 def last_kernel(chips, perm, q, index_in, weight_in, kept, got, values, *refs):
     odd, chip, end = position(chips)
-    tile = Tile(*refs[:8], refs[9], refs[8], edge_q(end), end)
-    index, weight, picked, sems = refs[10:]
+    tile = Tile(*refs[:9], refs[10], refs[9], edge_q(end), end)
+    index, weight, picked, sems = refs[11:]
     perm_copy = issue([(perm, tile.perm)], sems, 0)
     q_copy = issue([(q, tile.q)], sems, 1)
     tables = issue([(index_in, index), (weight_in, weight)], sems, 2)
@@ -399,17 +453,14 @@
         picked[pl.ds(at, 1), :] = total
         return carry
 
-    lax.fori_loop(0, 8 * per, one, 0)
+    lax.fori_loop(0, 8 * per, one, 0, unroll=4)
     ones = jnp.ones((values.shape[0], lanes), jnp.float32)
     values[...] = lax.dot_general(
         ones, picked[...], (((1,), (1,)), ((), ())), precision=HIGH, preferred_element_type=jnp.float32
     )
 
 
-def prepare_kernel(chips, wells, rate, log_perm, value, var, noise, q_out, blocks, tables, q, held, sems):
-    rows = log_perm.shape[2] // blocks.shape[0]
-    count = blocks.shape[0]
-    load = issue([(log_perm, held)], sems, count)
+def fill_sources(chips, wells, rate, q):
     odd, chip, _ = position(chips)
     ny, nz = q.shape[1], q.shape[2]
     lane = lax.broadcasted_iota(jnp.int32, (1, nz), 1)
@@ -426,11 +477,9 @@
         return carry
 
     lax.fori_loop(0, wells.shape[0], one, 0, unroll=4)
-    copies = issue([(q, q_out)], sems, count + 1)
-    drain(load)
-    copies += issue(
-        [(held.at[:, :, pl.ds(b * rows, rows), :], blocks.at[b]) for b in range(count)], sems, 0
-    )
+
+
+def order_tables(value, var, noise, tables):
     groups, lanes = value.shape
     wide = lanes // groups
     half = noise.shape[0] // 2
@@ -444,7 +493,6 @@
             column = pltpu.roll(jnp.concatenate(parts, axis=0), (4 + wide * (j - g)) % lanes, 1)
             total = column if total is None else jnp.where(side == j, column, total)
         tables[g] = total
-    drain(copies)
 
 
 def solve_kernel(values, tables, columns_in, out_to, coef, columns, out, sems):
@@ -572,42 +620,44 @@
         [(0, 0), (ends, ends)] + [(i, i + 1 if i % 2 else i - 1) for i in range(1, ends)],
     )
     sems = pltpu.SemaphoreType.DMA((16,))
-    q, blocks, tables = call(
-        prepare_kernel,
-        "prepare",
-        out_shape=(
-            pltpu.HBM((12,) + grid, f32),
-            pltpu.HBM((mems, members, width, ny // mems, nz), f32),
-            jax.ShapeDtypeStruct((4, 16, nz), f32),
-        ),
-        in_specs=[SMEM, SMEM, FAR] + [VMEM] * 3,
-        out_specs=(FAR, FAR, VMEM),
-        scratch_shapes=[plane(12), pltpu.VMEM(log_perm.shape, f32), sems],
-        compiler_params=grant,
-    )(wells, well_rate, log_perm, obs_value.reshape(4, nz), obs_var.reshape(4, nz), noise)
     scratch = tile_scratch(ny, nz) + [plane(8)]
-    keep, send, perm_tile = call(
+    keep, send, perm_tile, q = call(
         first_kernel,
         "first",
-        out_shape=(plane(PLANES), plane(8), pltpu.HBM((8,) + grid, f32)),
-        in_specs=[FAR] * 4 + [VMEM],
-        out_specs=(VMEM, VMEM, FAR),
+        out_shape=(
+            plane(PLANES),
+            plane(8),
+            pltpu.HBM((8,) + grid, f32),
+            pltpu.HBM((12,) + grid, f32),
+        ),
+        in_specs=[SMEM] * 2 + [FAR] * 3 + [VMEM],
+        out_specs=(VMEM, VMEM, FAR, FAR),
         scratch_shapes=scratch + [plane(4), sems],
         compiler_params=pltpu.CompilerParams(vmem_limit_bytes=GRANT + 1_400_000),
-    )(log_perm, saturation, pressure_init, q, near(swapped))
+    )(wells, well_rate, log_perm, saturation, pressure_init, near(swapped))
     onward = [(i, i + 2) for i in range(0, ends - 1, 2)] + [(ends - 1, ends)]
     onward += [(i, i - 2) for i in range(3, spaces, 2)] + [(1, 0)]
     back = [(b, a) for a, b in onward]
     got = lax.ppermute(send, "space", onward)
-    keep, send, perm_edge = call(
+    small = (obs_value.reshape(4, nz), obs_var.reshape(4, nz), noise)
+    keep, send, perm_edge, blocks, tables = call(
         second_kernel,
         "second",
-        out_shape=(plane(PLANES), plane(PLANES), pltpu.HBM((8,) + grid, f32)),
-        in_specs=[FAR] * 3 + [VMEM] * 2,
-        out_specs=(VMEM, VMEM, FAR),
-        scratch_shapes=scratch + [plane(9), sems],
+        out_shape=(
+            plane(PLANES),
+            plane(PLANES),
+            pltpu.HBM((8,) + grid, f32),
+            pltpu.HBM((mems, members, width, ny // mems, nz), f32),
+            jax.ShapeDtypeStruct((4, 16, nz), f32),
+        ),
+        in_specs=[FAR] * 7 + [VMEM] * 2,
+        out_specs=(VMEM, VMEM, FAR, FAR, VMEM),
+        scratch_shapes=scratch
+        + [plane(9), pltpu.VMEM(log_perm.shape, f32)]
+        + [pltpu.VMEM(table.shape, f32) for table in small]
+        + [sems],
         compiler_params=grant,
-    )(perm_tile, edge_in, q, near(keep), near(got))
+    )(perm_tile, edge_in, q, log_perm, *small, near(keep), near(got))
     got = lax.ppermute(send, "space", back)
     columns = lax.all_to_all(blocks, "mem", 0, 0, tiled=True).reshape(ens, width, ny // mems, nz)
     keep, send = call(

time: 98 us -> 91.9 us (0.938)
  Pallas kernels: 33.1 us -> 27 us
  waiting for transfers between devices: 16.9 us -> 19.6 us
  blocking collectives: 39.6 us -> 38.1 us
  starting transfers between devices: 6.47 us -> 5.18 us
    pallas_call x1 -> x0, Pallas kernels: 3.4 us -> none  [body(): call(prepare_kernel, 'prepare', out_shape=(pltpu.HBM((12,) + grid, f32),...]
    all_to_all x1, blocking collectives: 24.7 us -> 23.2 us  [body(): lax.all_to_all(values.reshape(devices, 1, nz), ('mem', 'space'), 0, 0, ti...]
    ppermute x1, waiting for transfers between devices: 0.01 us -> 1.45 us  [body(): lax.ppermute(swap_out, 'space', [(i, i ^ 1) for i in range(spaces)])]
    pallas_call x1, Pallas kernels: 7.68 us -> 6.26 us  [body(): call(third_kernel, 'third', out_shape=(plane(PLANES), plane(PLANES)), in_...]
    ppermute x2, waiting for transfers between devices: 16.9 us -> 18.2 us  [body(): got = lax.ppermute(send, 'space', onward)]
  transfers between devices with their start and end apart: 5 -> 5, of which waited for: 2 -> 3; matrix products, arithmetic and copies ran while one was open for 0% -> 0% of each run, Pallas kernels for 8% -> 5%
where the time goes in v5:
time: 91.9 us; the launch traced here: 91.4 us
  blocking collectives  38.1 us (41%)
  Pallas kernels  27 us (29%)
  waiting for transfers between devices  19.6 us (21%)
  starting transfers between devices  5.18 us (6%)
  local copies, waits for them, and re-layouts  1.14 us (1%)
    all_to_all x1, blocking collectives, body(): lax.all_to_all(values.reshape(devices, 1, nz), ('mem', 'space'), 0, 0, ti...  23.2 us
    ppermute x2, waiting for transfers between devices, body(): got = lax.ppermute(send, 'space', onward)  18.2 us
    all_to_all x1, blocking collectives, body(): lax.all_to_all(blocks, 'mem', 0, 0, tiled=True)  14.9 us
    pallas_call x1, Pallas kernels, body(): call(second_kernel, 'second', out_shape=(plane(PLANES), plane(PLANES), pl...  7.26 us
    pallas_call x1, Pallas kernels, body(): call(last_kernel, 'last', out_shape=pltpu.HBM((devices, nz), f32), in_spe...  6.34 us
    pallas_call x1, Pallas kernels, body(): call(third_kernel, 'third', out_shape=(plane(PLANES), plane(PLANES)), in_...  6.26 us
    pallas_call x1, Pallas kernels, body(): call(first_kernel, 'first', out_shape=(plane(PLANES), plane(8), pltpu.HBM...  4.14 us
    ppermute x2, starting transfers between devices, body(): got = lax.ppermute(send, 'space', onward)  3.36 us
  transfers between devices with their start and end apart: 5, of which 3 were waited for; matrix products, arithmetic and copies ran while one was open for 0% of the time, Pallas kernels for 5%

profile of v5, /device:TPU:0, one launch (start us, length us, event | category | flops | bytes accessed | tf_op | source)
XLA Modules:
  0.0 91.4 jit_solution(12811700968326769049)
XLA Ops:
  0.0 0.0 copy-start
  0.0 0.0 copy-start.1
  0.0 1.0 %dynamic-slice_bitcast_fusion = f32[4,128,128]{2,1,0:T(8,128)S(1)} fusion(f32[2,4,128,128]{3,2,1,0:T(8,128)} %log_perm.3, s32[]{:T(128)S(6)} %select_n.17), kind=kLoop, calls=%fused_computation.2 | loop fusion | bytes 524292 | tf_op jit(solution)/shard_map/squeeze | solution.py:612
  1.0 0.0 copy-done
  1.0 0.1 copy-done.1
  1.1 0.1 pad_maximum_fusion
  1.2 0.1 collective-permute-start
  1.4 0.7 collective-permute-start.1
  2.1 1.5 %collective-permute-done.swapped = f32[12,128,128]{2,1,0:T(8,128)S(1)} collective-permute-done((f32[12,128,128]{2,1,0:T(8,128)S(1)}, f32[12,128,128]{2,1,0:T(8,128)S(1)}, u32[]{:S(2)}, u32[]{:S(2)}) %collective-permute-start) | collective-permute-done | bytes 786464 | tf_op jit(solution)/shard_map/ppermute | solution.py:614
  3.5 4.1 %first.1 = (f32[13,128,128]{2,1,0:T(8,128)S(1)}, f32[8,128,128]{2,1,0:T(8,128)S(1)}, f32[8,128,128]{2,1,0:T(8,128)}, f32[12,128,128]{2,1,0:T(8,128)}) custom-call(s32[64]{0:T(128)} %wells.1, f32[64]{0:T(128)} %rate.1, f32[2,4,128,128]{3,2,1,0:T(8,128)} %log_perm.3, f32[4,128,128]{2,1,0:T(8,128)} %own_sat.1, f32[4,128,128]{2,1,0:T(8,128)} %own_press.1, ...), custom_call_target="tpu_custom_call" | custom-call | tf_op jit(solution)/shard_map/first/pallas_call | solution.py:624
  7.7 2.1 %collective-permute-start.2 = (f32[8,128,128]{2,1,0:T(8,128)S(1)}, f32[8,128,128]{2,1,0:T(8,128)S(1)}, u32[]{:S(2)}, u32[]{:S(2)}) collective-permute-start(f32[8,128,128]{2,1,0:T(8,128)S(1)} %get-tuple-element.19), channel_id=1, source_target_pairs={{0,2},{2,4},{4,6},{6,8},{8,10},{10,12},{12,14},{14,16},{16,18},{18... | collective-permute-start | bytes 1572872 | tf_op jit(solution)/shard_map/ppermute | solution.py:641
  9.8 0.0 collective-permute-done.1.raw_in
  9.8 0.0 copy-start.2
  9.8 8.0 %collective-permute-done.2.late_in = f32[8,128,128]{2,1,0:T(8,128)S(1)} collective-permute-done((f32[8,128,128]{2,1,0:T(8,128)S(1)}, f32[8,128,128]{2,1,0:T(8,128)S(1)}, u32[]{:S(2)}, u32[]{:S(2)}) %collective-permute-start.2) | collective-permute-done | bytes 524320 | tf_op jit(solution)/shard_map/ppermute | solution.py:641
  17.7 0.0 copy-done.2
  17.7 7.3 %second.1 = (f32[13,128,128]{2,1,0:T(8,128)S(1)}, f32[13,128,128]{2,1,0:T(8,128)S(1)}, f32[8,128,128]{2,1,0:T(8,128)}, f32[4,2,4,32,128]{4,3,2,1,0:T(8,128)}, f32[4,16,128]{2,1,0:T(8,128)}) custom-call(f32[8,128,128]{2,1,0:T(8,128)} %get-tuple-element.16.perm_own.perm, f32[9,128,128]{2,1,0:T(8,128)} %copy-done.2, f32[12,128,128]{2,1,0:T(8,128)} %get-tuple-element.17.q, ...), custom_call_target="tpu_custom_call" | custom-call | tf_op jit(solution)/shard_map/second/pallas_call | solution.py:643
  25.0 1.0 %collective-permute-start.3 = (f32[13,128,128]{2,1,0:T(8,128)S(1)}, f32[13,128,128]{2,1,0:T(8,128)S(1)}, u32[]{:S(2)}, u32[]{:S(2)}) collective-permute-start(f32[13,128,128]{2,1,0:T(8,128)S(1)} %get-tuple-element.23), channel_id=1, source_target_pairs={{2,0},{4,2},{6,4},{8,6},{10,8},{12,10},{14,12},{16,14},{18,16},{20... | collective-permute-start | bytes 2555912 | tf_op jit(solution)/shard_map/ppermute | solution.py:661
  26.0 14.9 %all_to_all.10 = f32[4,2,4,32,128]{4,3,2,1,0:T(8,128)} all-to-all(f32[4,2,4,32,128]{4,3,2,1,0:T(8,128)} %get-tuple-element.21), channel_id=1, replica_groups=mesh['mem'=4,'space'=32] {'mem'}, dimensions={0} | all-to-all | bytes 1048576 | tf_op jit(solution)/shard_map/all_to_all | solution.py:662
  41.0 0.0 collective-permute-done.3.got
  41.0 6.3 %third.1 = (f32[13,128,128]{2,1,0:T(8,128)S(1)}, f32[13,128,128]{2,1,0:T(8,128)S(1)}) custom-call(f32[8,128,128]{2,1,0:T(8,128)} %get-tuple-element.16.perm_own.perm, f32[12,128,128]{2,1,0:T(8,128)} %get-tuple-element.17.q, f32[8,4,32,128]{3,2,1,0:T(8,128)} %bitcast.11, f32[13,128,128]{2,1,0:T(8,128)S(1)} %get-tuple-element.22.kept, ...), custom_call_target="tpu_custom_call" | custom-call | tf_op jit(solution)/shard_map/third/pallas_call | solution.py:663
  47.2 1.3 %collective-permute-start.4 = (f32[13,128,128]{2,1,0:T(8,128)S(1)}, f32[13,128,128]{2,1,0:T(8,128)S(1)}, u32[]{:S(2)}, u32[]{:S(2)}) collective-permute-start(f32[13,128,128]{2,1,0:T(8,128)S(1)} %get-tuple-element.25), channel_id=1, source_target_pairs={{0,2},{2,4},{4,6},{6,8},{8,10},{10,12},{12,14},{14,16},{16,18},{18... | collective-permute-start | bytes 2555912 | tf_op jit(solution)/shard_map/ppermute | solution.py:672
  48.5 10.2 %collective-permute-done.4.got = f32[13,128,128]{2,1,0:T(8,128)S(1)} collective-permute-done((f32[13,128,128]{2,1,0:T(8,128)S(1)}, f32[13,128,128]{2,1,0:T(8,128)S(1)}, u32[]{:S(2)}, u32[]{:S(2)}) %collective-permute-start.4) | collective-permute-done | bytes 852000 | tf_op jit(solution)/shard_map/ppermute | solution.py:672
  58.7 6.3 %last.1 = f32[128,128]{1,0:T(8,128)} custom-call(f32[8,128,128]{2,1,0:T(8,128)} %get-tuple-element.20.perm, f32[12,128,128]{2,1,0:T(8,128)} %get-tuple-element.17.q, s32[8,512]{1,0:T(8,128)} %bitcast.15, f32[8,512]{1,0:T(8,128)} %bitcast.16, f32[13,128,128]{2,1,0:T(8,128)S(1)} %get-tuple-element.24.kept, f32[13,128,128]{2,1,0:T(8,128)S(1)} %collective-permute-done.4.got), custom_call_target="tpu_custom_call" | custom-call | tf_op jit(solution)/shard_map/last/pallas_call | solution.py:674
  65.1 23.2 %all_to_all.11 = f32[128,1,128]{2,1,0:T(1,128)} all-to-all(f32[128,1,128]{2,1,0:T(1,128)} %bitcast.13), channel_id=1, replica_groups=mesh['mem'=4,'space'=32] {'mem','space'}, dimensions={0} | all-to-all | bytes 131072 | tf_op jit(solution)/shard_map/all_to_all | solution.py:684
  88.2 3.0 %solve.1 = f32[8,4,32,128]{3,2,1,0:T(8,128)} custom-call(f32[128,128]{1,0:T(8,128)} %bitcast.14, f32[4,16,128]{2,1,0:T(8,128)} %get-tuple-element.26.tables, f32[8,4,32,128]{3,2,1,0:T(8,128)} %bitcast.12), custom_call_target="tpu_custom_call" | custom-call | tf_op jit(solution)/shard_map/solve/pallas_call | solution.py:687
  (3 shorter events, 0.1 us)
Async XLA Ops:
  0.0 1.0 %copy-start = (f32[4,128,128]{2,1,0:T(8,128)S(1)}, f32[4,128,128]{2,1,0:T(8,128)}, u32[]{:S(2)}) copy-start(f32[4,128,128]{2,1,0:T(8,128)} %own_press.1) | copy-start | bytes 786436
  0.0 1.1 %copy-start.1 = (f32[4,128,128]{2,1,0:T(8,128)S(1)}, f32[4,128,128]{2,1,0:T(8,128)}, u32[]{:S(2)}) copy-start(f32[4,128,128]{2,1,0:T(8,128)} %own_sat.1) | copy-start | bytes 786436
  1.2 2.4 %collective-permute-start = (f32[12,128,128]{2,1,0:T(8,128)S(1)}, f32[12,128,128]{2,1,0:T(8,128)S(1)}, u32[]{:S(2)}, u32[]{:S(2)}) collective-permute-start(f32[12,128,128]{2,1,0:T(8,128)S(1)} %pad_maximum_fusion), channel_id=1, source_target_pairs={{0,1},{1,0},{2,3},{3,2},{4,5},{5,4},{6,7},{7,6},{8,9},{9,8},{10,11... | collective-permute-start | bytes 2359304 | tf_op jit(solution)/shard_map/ppermute | solution.py:614
  1.4 8.4 %collective-permute-start.1 = (f32[9,128,128]{2,1,0:T(8,128)S(1)}, f32[9,128,128]{2,1,0:T(8,128)S(1)}, u32[]{:S(2)}, u32[]{:S(2)}) collective-permute-start(f32[9,128,128]{2,1,0:T(8,128)S(1)} %pad_maximum_fusion.1), channel_id=1, source_target_pairs={{0,0},{31,31},{1,2},{2,1},{3,4},{4,3},{5,6},{6,5},{7,8},{8,7},{9,1... | collective-permute-start | bytes 1769480 | tf_op jit(solution)/shard_map/ppermute | solution.py:617
  7.7 10.1 %collective-permute-start.2 = (f32[8,128,128]{2,1,0:T(8,128)S(1)}, f32[8,128,128]{2,1,0:T(8,128)S(1)}, u32[]{:S(2)}, u32[]{:S(2)}) collective-permute-start(f32[8,128,128]{2,1,0:T(8,128)S(1)} %get-tuple-element.19), channel_id=1, source_target_pairs={{0,2},{2,4},{4,6},{6,8},{8,10},{10,12},{12,14},{14,16},{16,18},{18... | collective-permute-start | bytes 1572872 | tf_op jit(solution)/shard_map/ppermute | solution.py:641
  9.8 8.0 %copy-start.2 = (f32[9,128,128]{2,1,0:T(8,128)}, f32[9,128,128]{2,1,0:T(8,128)S(1)}, u32[]{:S(2)}) copy-start(f32[9,128,128]{2,1,0:T(8,128)S(1)} %collective-permute-done.1.raw_in) | copy-start | bytes 1769476
  25.0 16.0 %collective-permute-start.3 = (f32[13,128,128]{2,1,0:T(8,128)S(1)}, f32[13,128,128]{2,1,0:T(8,128)S(1)}, u32[]{:S(2)}, u32[]{:S(2)}) collective-permute-start(f32[13,128,128]{2,1,0:T(8,128)S(1)} %get-tuple-element.23), channel_id=1, source_target_pairs={{2,0},{4,2},{6,4},{8,6},{10,8},{12,10},{14,12},{16,14},{18,16},{20... | collective-permute-start | bytes 2555912 | tf_op jit(solution)/shard_map/ppermute | solution.py:661
  47.2 11.5 %collective-permute-start.4 = (f32[13,128,128]{2,1,0:T(8,128)S(1)}, f32[13,128,128]{2,1,0:T(8,128)S(1)}, u32[]{:S(2)}, u32[]{:S(2)}) collective-permute-start(f32[13,128,128]{2,1,0:T(8,128)S(1)} %get-tuple-element.25), channel_id=1, source_target_pairs={{0,2},{2,4},{4,6},{6,8},{8,10},{10,12},{12,14},{14,16},{16,18},{18... | collective-permute-start | bytes 2555912 | tf_op jit(solution)/shard_map/ppermute | solution.py:672

commit v6 on v5

--- a/solution.py
+++ b/solution.py
@@ -27,12 +27,13 @@
 
 
 class Tile:
-    def __init__(self, lam_a, lam_b, frac_a, frac_b, p_a, p_b, s_a, s_b, sides, perm, q, q_row, cut):
+    def __init__(self, lam_a, lam_b, frac_a, frac_b, p_a, p_b, s_a, s_b, sides, steps, perm, q, q_row, cut):
         self.lam = (lam_a, lam_b)
         self.frac = (frac_a, frac_b)
         self.p = (p_a, p_b)
         self.s = (s_a, s_b)
         self.sides = sides
+        self.steps = steps
         self.perm = perm
         self.q = q
         self.q_row = q_row
@@ -114,6 +115,13 @@
             out = jnp.where(is_last, edge, moved)
             out = out + jnp.where(is_first, edge, pltpu.roll(-moved, 1, 1))
             self.sides[2 * slot, pl.ds(y0, CHUNK), :] = out
+            low = 0 if y0 == 0 else PAD + y0
+            here = pl.ds(low, PAD + y0 + CHUNK - low)
+            after = pl.ds(low + 1, PAD + y0 + CHUNK - low)
+            flux = (lam_r[st, here, :] + lam_r[st, after, :]) * (p_r[st, here, :] - p_r[st, after, :])
+            self.steps[slot, here, :] = flux * jnp.where(
+                flux > 0.0, frac_r[st, here, :], frac_r[st, after, :]
+            )
 
         def fn(row, st, up, down, y0, slot):
             inner = pl.ds(PAD + y0, CHUNK)
@@ -124,8 +132,7 @@
                 return flux * jnp.where(flux > 0.0, frac, frac_r[index, where, :])
 
             out = face(up, inner) + face(down, inner)
-            out = out + face(st, pl.ds(PAD + y0 + 1, CHUNK))
-            out = out + face(st, pl.ds(PAD + y0 - 1, CHUNK))
+            out = out + self.steps[slot, inner, :] - self.steps[slot, pl.ds(PAD + y0 - 1, CHUNK), :]
             out = out + self.sides[2 * slot, pl.ds(y0, CHUNK), :]
             q = self.q[self.q_row(row), pl.ds(y0, CHUNK), :]
             water = q * jnp.where(q > 0.0, 1.0, frac)
@@ -191,6 +198,7 @@
     tall = ny + 2 * PAD
     wide = [pltpu.VMEM((11, tall, nz), jnp.float32) for _ in range(6)]
     flat = [pltpu.VMEM((count, ny, nz), jnp.float32) for count in (11, 11, 4, 12)]
+    flat.insert(3, pltpu.VMEM((2, ny + PAD, nz), jnp.float32))
     return wide + flat
 
 
@@ -292,8 +300,8 @@
 
 def first_kernel(chips, wells, rate, log_perm, own_sat, own_press, swapped, keep, send, perm_out, q_out, *refs):
     odd, _, _ = position(chips)
-    perm, raw, sems = refs[10:]
-    tile = Tile(*refs[:9], perm, refs[9], lambda row: row + 4, jnp.int32(0))
+    perm, raw, sems = refs[11:]
+    tile = Tile(*refs[:10], perm, refs[10], lambda row: row + 4, jnp.int32(0))
     inner = pl.ds(PAD, tile.ny)
 
     def place(n):
@@ -360,8 +368,8 @@
 
 def second_kernel(chips, perm_own, raw_in, q, log_perm, value_in, var_in, noise_in, kept, late_in, keep, send, perm_out, blocks, tables, *refs):
     odd, _, end = position(chips)
-    perm, raw, held, value, var, noise, sems = refs[10:]
-    tile = Tile(*refs[:9], perm, refs[9], edge_q(end), end)
+    perm, raw, held, value, var, noise, sems = refs[11:]
+    tile = Tile(*refs[:10], perm, refs[10], edge_q(end), end)
     straight = odd ^ end
 
     def place(n, count):
@@ -411,8 +419,8 @@
 
 def third_kernel(perm, q, columns, kept, got, keep, send, *refs):
     del columns
-    tile = Tile(*refs[:9], refs[10], refs[9], lambda row: row + 4, jnp.int32(0))
-    sems = refs[11]
+    tile = Tile(*refs[:10], refs[11], refs[10], lambda row: row + 4, jnp.int32(0))
+    sems = refs[12]
     perm_copy = issue([(perm, tile.perm)], sems, 0)
     q_copy = issue([(q, tile.q)], sems, 1)
     fill(tile, both_sides(tile, kept, got), perm_copy, q_copy, tile.saturate(0, 1, 6))
@@ -421,8 +429,8 @@
 
 def last_kernel(chips, perm, q, index_in, weight_in, kept, got, values, *refs):
     odd, chip, end = position(chips)
-    tile = Tile(*refs[:9], refs[10], refs[9], edge_q(end), end)
-    index, weight, picked, sems = refs[11:]
+    tile = Tile(*refs[:10], refs[11], refs[10], edge_q(end), end)
+    index, weight, picked, sems = refs[12:]
     perm_copy = issue([(perm, tile.perm)], sems, 0)
     q_copy = issue([(q, tile.q)], sems, 1)
     tables = issue([(index_in, index), (weight_in, weight)], sems, 2)
@@ -693,7 +701,7 @@
         + [pltpu.VMEM(columns.shape, f32) for _ in range(2)]
         + [sems],
         name="solve",
-    )(values, tables, columns)
+    )(near(values), near(tables), columns)
 
 
 def solution(mesh):

time: 91.9 us -> 90.1 us (0.980)
  Pallas kernels: 27 us -> 25.9 us
where the time goes in v6:
time: 90.1 us; the launch traced here: 89.6 us
  blocking collectives  37.7 us (42%)
  Pallas kernels  25.9 us (29%)
  waiting for transfers between devices  19.7 us (22%)
  starting transfers between devices  4.97 us (6%)
  local copies, waits for them, and re-layouts  1.14 us (1%)
    all_to_all x1, blocking collectives, body(): lax.all_to_all(values.reshape(devices, 1, nz), ('mem', 'space'), 0, 0, ti...  22.7 us
    ppermute x2, waiting for transfers between devices, body(): got = lax.ppermute(send, 'space', onward)  18.2 us
    all_to_all x1, blocking collectives, body(): lax.all_to_all(blocks, 'mem', 0, 0, tiled=True)  14.9 us
    pallas_call x1, Pallas kernels, body(): call(second_kernel, 'second', out_shape=(plane(PLANES), plane(PLANES), pl...  7.21 us
    pallas_call x1, Pallas kernels, body(): call(last_kernel, 'last', out_shape=pltpu.HBM((devices, nz), f32), in_spe...  6.29 us
    pallas_call x1, Pallas kernels, body(): call(third_kernel, 'third', out_shape=(plane(PLANES), plane(PLANES)), in_...  6.18 us
    pallas_call x1, Pallas kernels, body(): call(first_kernel, 'first', out_shape=(plane(PLANES), plane(8), pltpu.HBM...  4.11 us
    ppermute x2, starting transfers between devices, body(): got = lax.ppermute(send, 'space', onward)  3.18 us
  transfers between devices with their start and end apart: 5, of which 3 were waited for; matrix products, arithmetic and copies ran while one was open for 0% of the time, Pallas kernels for 5%

profile of v6, /device:TPU:0, one launch (start us, length us, event | category | flops | bytes accessed | tf_op | source)
XLA Modules:
  0.0 89.6 jit_solution(8970468444193057911)
XLA Ops:
  0.0 0.0 copy-start.1
  0.0 0.0 copy-start.2
  0.0 1.0 %dynamic-slice_bitcast_fusion = f32[4,128,128]{2,1,0:T(8,128)S(1)} fusion(f32[2,4,128,128]{3,2,1,0:T(8,128)} %log_perm.3, s32[]{:T(128)S(6)} %select_n.17), kind=kLoop, calls=%fused_computation.2 | loop fusion | bytes 524292 | tf_op jit(solution)/shard_map/squeeze | solution.py:620
  1.0 0.0 copy-done.1
  1.0 0.1 copy-done.2
  1.1 0.1 pad_maximum_fusion
  1.2 0.1 collective-permute-start
  1.4 0.7 collective-permute-start.1
  2.1 1.5 %collective-permute-done.swapped = f32[12,128,128]{2,1,0:T(8,128)S(1)} collective-permute-done((f32[12,128,128]{2,1,0:T(8,128)S(1)}, f32[12,128,128]{2,1,0:T(8,128)S(1)}, u32[]{:S(2)}, u32[]{:S(2)}) %collective-permute-start) | collective-permute-done | bytes 786464 | tf_op jit(solution)/shard_map/ppermute | solution.py:622
  3.5 4.1 %first.1 = (f32[13,128,128]{2,1,0:T(8,128)S(1)}, f32[8,128,128]{2,1,0:T(8,128)S(1)}, f32[8,128,128]{2,1,0:T(8,128)}, f32[12,128,128]{2,1,0:T(8,128)}) custom-call(s32[64]{0:T(128)} %wells.1, f32[64]{0:T(128)} %rate.1, f32[2,4,128,128]{3,2,1,0:T(8,128)} %log_perm.3, f32[4,128,128]{2,1,0:T(8,128)} %own_sat.1, f32[4,128,128]{2,1,0:T(8,128)} %own_press.1, ...), custom_call_target="tpu_custom_call" | custom-call | tf_op jit(solution)/shard_map/first/pallas_call | solution.py:632
  7.6 2.1 %collective-permute-start.2 = (f32[8,128,128]{2,1,0:T(8,128)S(1)}, f32[8,128,128]{2,1,0:T(8,128)S(1)}, u32[]{:S(2)}, u32[]{:S(2)}) collective-permute-start(f32[8,128,128]{2,1,0:T(8,128)S(1)} %get-tuple-element.19), channel_id=1, source_target_pairs={{0,2},{2,4},{4,6},{6,8},{8,10},{10,12},{12,14},{14,16},{16,18},{18... | collective-permute-start | bytes 1572872 | tf_op jit(solution)/shard_map/ppermute | solution.py:649
  9.7 0.0 collective-permute-done.1.raw_in
  9.7 0.0 copy-start.3
  9.8 8.0 %collective-permute-done.2.late_in = f32[8,128,128]{2,1,0:T(8,128)S(1)} collective-permute-done((f32[8,128,128]{2,1,0:T(8,128)S(1)}, f32[8,128,128]{2,1,0:T(8,128)S(1)}, u32[]{:S(2)}, u32[]{:S(2)}) %collective-permute-start.2) | collective-permute-done | bytes 524320 | tf_op jit(solution)/shard_map/ppermute | solution.py:649
  17.7 0.0 copy-done.3
  17.7 7.2 %second.1 = (f32[13,128,128]{2,1,0:T(8,128)S(1)}, f32[13,128,128]{2,1,0:T(8,128)S(1)}, f32[8,128,128]{2,1,0:T(8,128)}, f32[4,2,4,32,128]{4,3,2,1,0:T(8,128)}, f32[4,16,128]{2,1,0:T(8,128)}) custom-call(f32[8,128,128]{2,1,0:T(8,128)} %get-tuple-element.16.perm_own.perm, f32[9,128,128]{2,1,0:T(8,128)} %copy-done.3, f32[12,128,128]{2,1,0:T(8,128)} %get-tuple-element.17.q, ...), custom_call_target="tpu_custom_call" | custom-call | tf_op jit(solution)/shard_map/second/pallas_call | solution.py:651
  25.0 1.0 %collective-permute-start.3 = (f32[13,128,128]{2,1,0:T(8,128)S(1)}, f32[13,128,128]{2,1,0:T(8,128)S(1)}, u32[]{:S(2)}, u32[]{:S(2)}) collective-permute-start(f32[13,128,128]{2,1,0:T(8,128)S(1)} %get-tuple-element.23), channel_id=1, source_target_pairs={{2,0},{4,2},{6,4},{8,6},{10,8},{12,10},{14,12},{16,14},{18,16},{20... | collective-permute-start | bytes 2555912 | tf_op jit(solution)/shard_map/ppermute | solution.py:669
  26.0 14.9 %all_to_all.10 = f32[4,2,4,32,128]{4,3,2,1,0:T(8,128)} all-to-all(f32[4,2,4,32,128]{4,3,2,1,0:T(8,128)} %get-tuple-element.21), channel_id=1, replica_groups=mesh['mem'=4,'space'=32] {'mem'}, dimensions={0} | all-to-all | bytes 1048576 | tf_op jit(solution)/shard_map/all_to_all | solution.py:670
  40.9 0.0 collective-permute-done.3.got
  40.9 6.2 %third.1 = (f32[13,128,128]{2,1,0:T(8,128)S(1)}, f32[13,128,128]{2,1,0:T(8,128)S(1)}) custom-call(f32[8,128,128]{2,1,0:T(8,128)} %get-tuple-element.16.perm_own.perm, f32[12,128,128]{2,1,0:T(8,128)} %get-tuple-element.17.q, f32[8,4,32,128]{3,2,1,0:T(8,128)} %bitcast.12, f32[13,128,128]{2,1,0:T(8,128)S(1)} %get-tuple-element.22.kept, ...), custom_call_target="tpu_custom_call" | custom-call | tf_op jit(solution)/shard_map/third/pallas_call | solution.py:671
  47.1 1.1 %collective-permute-start.4 = (f32[13,128,128]{2,1,0:T(8,128)S(1)}, f32[13,128,128]{2,1,0:T(8,128)S(1)}, u32[]{:S(2)}, u32[]{:S(2)}) collective-permute-start(f32[13,128,128]{2,1,0:T(8,128)S(1)} %get-tuple-element.25), channel_id=1, source_target_pairs={{0,2},{2,4},{4,6},{6,8},{8,10},{10,12},{12,14},{14,16},{16,18},{18... | collective-permute-start | bytes 2555912 | tf_op jit(solution)/shard_map/ppermute | solution.py:680
  48.2 10.2 %collective-permute-done.4.got = f32[13,128,128]{2,1,0:T(8,128)S(1)} collective-permute-done((f32[13,128,128]{2,1,0:T(8,128)S(1)}, f32[13,128,128]{2,1,0:T(8,128)S(1)}, u32[]{:S(2)}, u32[]{:S(2)}) %collective-permute-start.4) | collective-permute-done | bytes 852000 | tf_op jit(solution)/shard_map/ppermute | solution.py:680
  58.4 6.3 %last.1 = f32[128,128]{1,0:T(8,128)} custom-call(f32[8,128,128]{2,1,0:T(8,128)} %get-tuple-element.20.perm, f32[12,128,128]{2,1,0:T(8,128)} %get-tuple-element.17.q, s32[8,512]{1,0:T(8,128)} %bitcast.15, f32[8,512]{1,0:T(8,128)} %bitcast.16, f32[13,128,128]{2,1,0:T(8,128)S(1)} %get-tuple-element.24.kept, f32[13,128,128]{2,1,0:T(8,128)S(1)} %collective-permute-done.4.got), custom_call_target="tpu_custom_call" | custom-call | tf_op jit(solution)/shard_map/last/pallas_call | solution.py:682
  64.7 0.0 copy-start
  64.7 22.7 %all_to_all.11 = f32[128,1,128]{2,1,0:T(1,128)S(1)} all-to-all(f32[128,1,128]{2,1,0:T(1,128)} %bitcast.14), channel_id=1, replica_groups=mesh['mem'=4,'space'=32] {'mem','space'}, dimensions={0} | all-to-all | bytes 131072 | tf_op jit(solution)/shard_map/all_to_all | solution.py:692
  87.4 0.0 copy-done
  87.4 2.1 %solve.1 = f32[8,4,32,128]{3,2,1,0:T(8,128)} custom-call(f32[128,128]{1,0:T(8,128)S(1)} %bitcast.11, f32[4,16,128]{2,1,0:T(8,128)S(1)} %copy-done, f32[8,4,32,128]{3,2,1,0:T(8,128)} %bitcast.13), custom_call_target="tpu_custom_call" | custom-call | tf_op jit(solution)/shard_map/solve/pallas_call | solution.py:695
  (3 shorter events, 0.1 us)
Async XLA Ops:
  0.0 1.0 %copy-start.1 = (f32[4,128,128]{2,1,0:T(8,128)S(1)}, f32[4,128,128]{2,1,0:T(8,128)}, u32[]{:S(2)}) copy-start(f32[4,128,128]{2,1,0:T(8,128)} %own_press.1) | copy-start | bytes 786436
  0.0 1.1 %copy-start.2 = (f32[4,128,128]{2,1,0:T(8,128)S(1)}, f32[4,128,128]{2,1,0:T(8,128)}, u32[]{:S(2)}) copy-start(f32[4,128,128]{2,1,0:T(8,128)} %own_sat.1) | copy-start | bytes 786436
  1.2 2.4 %collective-permute-start = (f32[12,128,128]{2,1,0:T(8,128)S(1)}, f32[12,128,128]{2,1,0:T(8,128)S(1)}, u32[]{:S(2)}, u32[]{:S(2)}) collective-permute-start(f32[12,128,128]{2,1,0:T(8,128)S(1)} %pad_maximum_fusion), channel_id=1, source_target_pairs={{0,1},{1,0},{2,3},{3,2},{4,5},{5,4},{6,7},{7,6},{8,9},{9,8},{10,11... | collective-permute-start | bytes 2359304 | tf_op jit(solution)/shard_map/ppermute | solution.py:622
  1.4 8.4 %collective-permute-start.1 = (f32[9,128,128]{2,1,0:T(8,128)S(1)}, f32[9,128,128]{2,1,0:T(8,128)S(1)}, u32[]{:S(2)}, u32[]{:S(2)}) collective-permute-start(f32[9,128,128]{2,1,0:T(8,128)S(1)} %pad_maximum_fusion.1), channel_id=1, source_target_pairs={{0,0},{31,31},{1,2},{2,1},{3,4},{4,3},{5,6},{6,5},{7,8},{8,7},{9,1... | collective-permute-start | bytes 1769480 | tf_op jit(solution)/shard_map/ppermute | solution.py:625
  7.6 10.1 %collective-permute-start.2 = (f32[8,128,128]{2,1,0:T(8,128)S(1)}, f32[8,128,128]{2,1,0:T(8,128)S(1)}, u32[]{:S(2)}, u32[]{:S(2)}) collective-permute-start(f32[8,128,128]{2,1,0:T(8,128)S(1)} %get-tuple-element.19), channel_id=1, source_target_pairs={{0,2},{2,4},{4,6},{6,8},{8,10},{10,12},{12,14},{14,16},{16,18},{18... | collective-permute-start | bytes 1572872 | tf_op jit(solution)/shard_map/ppermute | solution.py:649
  9.7 8.0 %copy-start.3 = (f32[9,128,128]{2,1,0:T(8,128)}, f32[9,128,128]{2,1,0:T(8,128)S(1)}, u32[]{:S(2)}) copy-start(f32[9,128,128]{2,1,0:T(8,128)S(1)} %collective-permute-done.1.raw_in) | copy-start | bytes 1769476
  25.0 15.9 %collective-permute-start.3 = (f32[13,128,128]{2,1,0:T(8,128)S(1)}, f32[13,128,128]{2,1,0:T(8,128)S(1)}, u32[]{:S(2)}, u32[]{:S(2)}) collective-permute-start(f32[13,128,128]{2,1,0:T(8,128)S(1)} %get-tuple-element.23), channel_id=1, source_target_pairs={{2,0},{4,2},{6,4},{8,6},{10,8},{12,10},{14,12},{16,14},{18,16},{20... | collective-permute-start | bytes 2555912 | tf_op jit(solution)/shard_map/ppermute | solution.py:669
  47.1 11.3 %collective-permute-start.4 = (f32[13,128,128]{2,1,0:T(8,128)S(1)}, f32[13,128,128]{2,1,0:T(8,128)S(1)}, u32[]{:S(2)}, u32[]{:S(2)}) collective-permute-start(f32[13,128,128]{2,1,0:T(8,128)S(1)} %get-tuple-element.25), channel_id=1, source_target_pairs={{0,2},{2,4},{4,6},{6,8},{8,10},{10,12},{12,14},{14,16},{16,18},{18... | collective-permute-start | bytes 2555912 | tf_op jit(solution)/shard_map/ppermute | solution.py:680
  64.7 22.8 %copy-start = (f32[4,16,128]{2,1,0:T(8,128)S(1)}, f32[4,16,128]{2,1,0:T(8,128)}, u32[]{:S(2)}) copy-start(f32[4,16,128]{2,1,0:T(8,128)} %get-tuple-element.26.tables) | copy-start | bytes 98308

commit v7 on v6

--- a/solution.py
+++ b/solution.py
@@ -12,6 +12,7 @@
 STEP = 0.1
 PAD = 8
 CHUNK = 32
+HALF = 16
 HIGH = lax.Precision.HIGHEST
 FAR = pl.BlockSpec(memory_space=pltpu.HBM)
 SMEM = pl.BlockSpec(memory_space=pltpu.SMEM)
@@ -65,29 +66,29 @@
         lax.fori_loop(first, last + 1, one, 0)
 
     def run(self, phases, primed=False, then=None):
-        def all_of(row, slot, which):
-            for y0 in range(0, self.ny, CHUNK):
+        def all_of(row, slot, which, chunk):
+            for y0 in range(0, self.ny, chunk):
                 which(row, *self.places(row), y0, slot)
 
         if not primed:
-            all_of(jnp.int32(phases[0][0]), 0, phases[0][2])
+            all_of(jnp.int32(phases[0][0]), 0, phases[0][2], phases[0][4])
         for phase, follower in zip(phases, phases[1:] + [then]):
-            first, last, ahead, fn = phase
-
-            def two(n, carry, first=first, ahead=ahead, fn=fn):
+            first, last, ahead, fn, chunk = phase
+
+            def two(n, carry, first=first, ahead=ahead, fn=fn, chunk=chunk):
                 row = first + 2 * n
-                all_of(row + 1, 1, ahead)
-                all_of(row, 0, fn)
-                all_of(row + 2, 0, ahead)
-                all_of(row + 1, 1, fn)
+                all_of(row + 1, 1, ahead, chunk)
+                all_of(row, 0, fn, chunk)
+                all_of(row + 2, 0, ahead, chunk)
+                all_of(row + 1, 1, fn, chunk)
                 return carry
 
             lax.fori_loop(0, (last - first) // 2, two, 0)
-            all_of(jnp.int32(last), 1, ahead)
-            all_of(jnp.int32(last - 1), 0, fn)
+            all_of(jnp.int32(last), 1, ahead, chunk)
+            all_of(jnp.int32(last - 1), 0, fn, chunk)
             if follower is not None:
-                all_of(jnp.int32(follower[0]), 0, follower[2])
-            all_of(jnp.int32(last), 1, fn)
+                all_of(jnp.int32(follower[0]), 0, follower[2], follower[4])
+            all_of(jnp.int32(last), 1, fn, chunk)
 
     def props(self, level, first, last):
         def fn(row, st, up, down, y0):
@@ -143,44 +144,44 @@
             self.lam[new][st, inner, :] = lam
             self.frac[new][st, inner, :] = frac
 
-        return first, last, ahead, fn
+        return first, last, ahead, fn, CHUNK
 
     def pressure(self, level, first, last):
         new = 1 - level
         lam_r, p_r, out_r = self.lam[new], self.p[level], self.p[new]
         lanes = lam_r.shape[2]
-        lane = lax.broadcasted_iota(jnp.int32, (CHUNK, lanes), 1)
+        lane = lax.broadcasted_iota(jnp.int32, (HALF, lanes), 1)
         not_first, not_last = lane > 0, lane < lanes - 1
 
         def ahead(row, st, up, down, y0, slot):
-            inner = pl.ds(PAD + y0, CHUNK)
+            inner = pl.ds(PAD + y0, HALF)
             lam, press = lam_r[st, inner, :], p_r[st, inner, :]
             numer, denom = 0.0, 0.0
             for shift, mask in ((lanes - 1, not_last), (1, not_first)):
                 trans = lam + jnp.where(mask, pltpu.roll(lam, shift, 1), 0.0)
                 numer = numer + trans * jnp.where(mask, pltpu.roll(press, shift, 1), 0.0)
                 denom = denom + trans
-            self.sides[2 * slot, pl.ds(y0, CHUNK), :] = numer
-            self.sides[2 * slot + 1, pl.ds(y0, CHUNK), :] = denom
+            self.sides[2 * slot, pl.ds(y0, HALF), :] = numer
+            self.sides[2 * slot + 1, pl.ds(y0, HALF), :] = denom
 
         def fn(row, st, up, down, y0, slot):
-            inner = pl.ds(PAD + y0, CHUNK)
+            inner = pl.ds(PAD + y0, HALF)
             lam, press = lam_r[st, inner, :], p_r[st, inner, :]
-            numer = press + self.q[self.q_row(row), pl.ds(y0, CHUNK), :]
-            numer = numer + self.sides[2 * slot, pl.ds(y0, CHUNK), :]
-            denom = 1.0 + self.sides[2 * slot + 1, pl.ds(y0, CHUNK), :]
+            numer = press + self.q[self.q_row(row), pl.ds(y0, HALF), :]
+            numer = numer + self.sides[2 * slot, pl.ds(y0, HALF), :]
+            denom = 1.0 + self.sides[2 * slot + 1, pl.ds(y0, HALF), :]
             for index, where in (
                 (up, inner),
                 (down, inner),
-                (st, pl.ds(PAD + y0 + 1, CHUNK)),
-                (st, pl.ds(PAD + y0 - 1, CHUNK)),
+                (st, pl.ds(PAD + y0 + 1, HALF)),
+                (st, pl.ds(PAD + y0 - 1, HALF)),
             ):
                 trans = lam + lam_r[index, where, :]
                 numer = numer + trans * p_r[index, where, :]
                 denom = denom + trans
             out_r[st, inner, :] = numer / denom
 
-        return first, last, ahead, fn
+        return first, last, ahead, fn, HALF
 
 
 def props(perm_half, sat):
@@ -339,16 +340,12 @@
     drain(out_copies)
 
 
-def fill(tile, sides, perm_copy, q_copy, then=None):
-    tile.clear()
-    groups = [sum((side[n] for side in sides), []) for n in range(4)]
-    move(groups[0] + groups[1] + groups[2])
-    drain(perm_copy)
+def fill(tile, sides, q_copy, then=None):
     tile.props(0, 2, 5)
     tile.props(1, 0, 2)
     tile.props(1, 5, 7)
     drain(q_copy)
-    move(groups[3])
+    move(sides[0][3] + sides[1][3])
     tile.props(0, 0, 0)
     tile.props(0, 7, 7)
     tile.run(
@@ -366,7 +363,7 @@
     return lambda row: jnp.where((cut == 1) & (row >= 4), row, 7 - row)
 
 
-def second_kernel(chips, perm_own, raw_in, q, log_perm, value_in, var_in, noise_in, kept, late_in, keep, send, perm_out, blocks, tables, *refs):
+def second_kernel(chips, perm_own, raw_in, q, log_perm, value_in, var_in, noise_in, kept, late_in, keep, send, perm_out, perm_next, blocks, tables, *refs):
     odd, _, end = position(chips)
     perm, raw, held, value, var, noise, sems = refs[11:]
     tile = Tile(*refs[:10], perm, refs[10], edge_q(end), end)
@@ -382,8 +379,19 @@
 
     copies = issue([(raw_in, raw)] + [(perm_own.at[3 - d], perm.at[d]) for d in range(4)], sems, 0)
     q_copy = issue([(q, tile.q)], sems, 5)
-    load = issue([(log_perm, held), (value_in, value), (var_in, var), (noise_in, noise)], sems, 7)
+    load = issue(
+        [(log_perm, held), (value_in, value), (var_in, var), (noise_in, noise), (perm_own, perm_next)],
+        sems,
+        7,
+    )
+    sides = (
+        take(tile, lambda n: kept.at[n], lambda n: kept.at[n], 4, -1),
+        take(tile, early, lambda n: late_in.at[n - S1[0]], 6, 1),
+    )
+    tile.clear()
+    move(sides[0][0] + sides[0][1] + sides[0][2] + sides[1][1] + sides[1][2])
     drain(copies)
+    move(sides[1][0])
 
     def permeability(d, carry):
         for y0 in range(0, tile.ny, CHUNK):
@@ -393,16 +401,12 @@
 
     lax.fori_loop(0, 4, permeability, 0)
     perm_copy = issue([(perm, perm_out)], sems, 6)
-    sides = (
-        take(tile, lambda n: kept.at[n], lambda n: kept.at[n], 4, -1),
-        take(tile, early, lambda n: late_in.at[n - S1[0]], 6, 1),
-    )
-    fill(tile, sides, [], q_copy, tile.saturate(0, 1, 6))
+    fill(tile, sides, q_copy, tile.saturate(0, 1, 6))
     drain(load)
     count = blocks.shape[0]
     rows = log_perm.shape[2] // count
     pieces = issue(
-        [(held.at[:, :, pl.ds(b * rows, rows), :], blocks.at[b]) for b in range(count)], sems, 11
+        [(held.at[:, :, pl.ds(b * rows, rows), :], blocks.at[b]) for b in range(count)], sems, 12
     )
     order_tables(value, var, noise, tables)
     advance(tile, keep, send, True)
@@ -417,24 +421,31 @@
     )
 
 
-def third_kernel(perm, q, columns, kept, got, keep, send, *refs):
+def gather(tile, kept, got):
+    sides = both_sides(tile, kept, got)
+    tile.clear()
+    move(sum((side[n] for side in sides for n in range(3)), []))
+    return sides
+
+
+def third_kernel(q, columns, perm_later, perm, kept, got, keep, send, perm_next, *refs):
     del columns
-    tile = Tile(*refs[:10], refs[11], refs[10], lambda row: row + 4, jnp.int32(0))
-    sems = refs[12]
-    perm_copy = issue([(perm, tile.perm)], sems, 0)
-    q_copy = issue([(q, tile.q)], sems, 1)
-    fill(tile, both_sides(tile, kept, got), perm_copy, q_copy, tile.saturate(0, 1, 6))
+    tile = Tile(*refs[:10], perm, refs[10], lambda row: row + 4, jnp.int32(0))
+    sems = refs[11]
+    q_copy = issue([(q, tile.q)], sems, 0)
+    hand_on = issue([(perm_later, perm_next)], sems, 1)
+    fill(tile, gather(tile, kept, got), q_copy, tile.saturate(0, 1, 6))
     advance(tile, keep, send, True)
-
-
-def last_kernel(chips, perm, q, index_in, weight_in, kept, got, values, *refs):
+    drain(hand_on)
+
+
+def last_kernel(chips, q, index_in, weight_in, perm, kept, got, values, *refs):
     odd, chip, end = position(chips)
-    tile = Tile(*refs[:10], refs[11], refs[10], edge_q(end), end)
-    index, weight, picked, sems = refs[12:]
-    perm_copy = issue([(perm, tile.perm)], sems, 0)
+    tile = Tile(*refs[:10], perm, refs[10], edge_q(end), end)
+    index, weight, picked, sems = refs[11:]
     q_copy = issue([(q, tile.q)], sems, 1)
     tables = issue([(index_in, index), (weight_in, weight)], sems, 2)
-    fill(tile, both_sides(tile, kept, got), perm_copy, q_copy)
+    fill(tile, gather(tile, kept, got), q_copy)
     drain(tables)
     around = (chip + odd) & (chips - 1)
     total_rows = 8 * chips
@@ -628,7 +639,7 @@
         [(0, 0), (ends, ends)] + [(i, i + 1 if i % 2 else i - 1) for i in range(1, ends)],
     )
     sems = pltpu.SemaphoreType.DMA((16,))
-    scratch = tile_scratch(ny, nz) + [plane(8)]
+    scratch = tile_scratch(ny, nz)
     keep, send, perm_tile, q = call(
         first_kernel,
         "first",
@@ -640,7 +651,7 @@
         ),
         in_specs=[SMEM] * 2 + [FAR] * 3 + [VMEM],
         out_specs=(VMEM, VMEM, FAR, FAR),
-        scratch_shapes=scratch + [plane(4), sems],
+        scratch_shapes=scratch + [plane(8), plane(4), sems],
         compiler_params=pltpu.CompilerParams(vmem_limit_bytes=GRANT + 1_400_000),
     )(wells, well_rate, log_perm, saturation, pressure_init, near(swapped))
     onward = [(i, i + 2) for i in range(0, ends - 1, 2)] + [(ends - 1, ends)]
@@ -648,47 +659,48 @@
     back = [(b, a) for a, b in onward]
     got = lax.ppermute(send, "space", onward)
     small = (obs_value.reshape(4, nz), obs_var.reshape(4, nz), noise)
-    keep, send, perm_edge, blocks, tables = call(
+    keep, send, perm_edge, perm_tile, blocks, tables = call(
         second_kernel,
         "second",
         out_shape=(
             plane(PLANES),
             plane(PLANES),
             pltpu.HBM((8,) + grid, f32),
+            plane(8),
             pltpu.HBM((mems, members, width, ny // mems, nz), f32),
             jax.ShapeDtypeStruct((4, 16, nz), f32),
         ),
         in_specs=[FAR] * 7 + [VMEM] * 2,
-        out_specs=(VMEM, VMEM, FAR, FAR, VMEM),
+        out_specs=(VMEM, VMEM, FAR, VMEM, FAR, VMEM),
         scratch_shapes=scratch
-        + [plane(9), pltpu.VMEM(log_perm.shape, f32)]
+        + [plane(8), plane(9), pltpu.VMEM(log_perm.shape, f32)]
         + [pltpu.VMEM(table.shape, f32) for table in small]
         + [sems],
         compiler_params=grant,
     )(perm_tile, edge_in, q, log_perm, *small, near(keep), near(got))
     got = lax.ppermute(send, "space", back)
     columns = lax.all_to_all(blocks, "mem", 0, 0, tiled=True).reshape(ens, width, ny // mems, nz)
-    keep, send = call(
+    keep, send, perm_edge = call(
         third_kernel,
         "third",
-        out_shape=(plane(PLANES), plane(PLANES)),
-        in_specs=[FAR] * 3 + [VMEM] * 2,
-        out_specs=(VMEM,) * 2,
+        out_shape=(plane(PLANES), plane(PLANES), plane(8)),
+        in_specs=[FAR] * 3 + [VMEM] * 3,
+        out_specs=(VMEM,) * 3,
         scratch_shapes=scratch + [sems],
         compiler_params=grant,
-    )(perm_tile, q, columns, near(keep), near(got))
+    )(q, columns, perm_edge, near(perm_tile), near(keep), near(got))
     got = lax.ppermute(send, "space", onward)
     taps = obs_index.T.shape
     values = call(
         last_kernel,
         "last",
         out_shape=pltpu.HBM((devices, nz), f32),
-        in_specs=[FAR] * 4 + [VMEM] * 2,
+        in_specs=[FAR] * 3 + [VMEM] * 3,
         out_specs=VMEM,
         scratch_shapes=scratch
         + [pltpu.SMEM(taps, jnp.int32), pltpu.SMEM(taps, f32), pltpu.VMEM((nz, nz), f32), sems],
         compiler_params=grant,
-    )(perm_edge, q, obs_index.T, obs_weight.T, near(keep), near(got))
+    )(q, obs_index.T, obs_weight.T, near(perm_edge), near(keep), near(got))
     values = lax.all_to_all(
         values.reshape(devices, 1, nz), ("mem", "space"), 0, 0, tiled=True
     ).reshape(devices, nz)

time: 90.1 us -> 89.5 us (level)
  no operation moved by 1% of the time
where the time goes in v7:
time: 89.5 us; the launch traced here: 89 us
  blocking collectives  37.7 us (42%)
  Pallas kernels  25.3 us (28%)
  waiting for transfers between devices  19.7 us (22%)
  starting transfers between devices  4.98 us (6%)
  local copies, waits for them, and re-layouts  1.14 us (1%)
    all_to_all x1, blocking collectives, body(): lax.all_to_all(values.reshape(devices, 1, nz), ('mem', 'space'), 0, 0, ti...  22.7 us
    ppermute x2, waiting for transfers between devices, body(): got = lax.ppermute(send, 'space', onward)  18.2 us
    all_to_all x1, blocking collectives, body(): lax.all_to_all(blocks, 'mem', 0, 0, tiled=True)  14.9 us
    pallas_call x1, Pallas kernels, body(): call(second_kernel, 'second', out_shape=(plane(PLANES), plane(PLANES), pl...  7.09 us
    pallas_call x1, Pallas kernels, body(): call(last_kernel, 'last', out_shape=pltpu.HBM((devices, nz), f32), in_spe...  6.05 us
    pallas_call x1, Pallas kernels, body(): call(third_kernel, 'third', out_shape=(plane(PLANES), plane(PLANES), plan...  5.93 us
    pallas_call x1, Pallas kernels, body(): call(first_kernel, 'first', out_shape=(plane(PLANES), plane(8), pltpu.HBM...  4.1 us
    ppermute x2, starting transfers between devices, body(): got = lax.ppermute(send, 'space', onward)  3.18 us
  transfers between devices with their start and end apart: 5, of which 3 were waited for; matrix products, arithmetic and copies ran while one was open for 0% of the time, Pallas kernels for 5%

profile of v7, /device:TPU:0, one launch (start us, length us, event | category | flops | bytes accessed | tf_op | source)
XLA Modules:
  0.0 89.0 jit_solution(7691383172525889065)
XLA Ops:
  0.0 0.0 copy-start.1
  0.0 0.0 copy-start.2
  0.0 1.0 %dynamic-slice_bitcast_fusion = f32[4,128,128]{2,1,0:T(8,128)S(1)} fusion(f32[2,4,128,128]{3,2,1,0:T(8,128)} %log_perm.3, s32[]{:T(128)S(6)} %select_n.17), kind=kLoop, calls=%fused_computation.2 | loop fusion | bytes 524292 | tf_op jit(solution)/shard_map/squeeze | solution.py:631
  1.0 0.0 copy-done.1
  1.0 0.1 copy-done.2
  1.1 0.1 pad_maximum_fusion
  1.2 0.1 collective-permute-start
  1.4 0.7 collective-permute-start.1
  2.1 1.5 %collective-permute-done.swapped = f32[12,128,128]{2,1,0:T(8,128)S(1)} collective-permute-done((f32[12,128,128]{2,1,0:T(8,128)S(1)}, f32[12,128,128]{2,1,0:T(8,128)S(1)}, u32[]{:S(2)}, u32[]{:S(2)}) %collective-permute-start) | collective-permute-done | bytes 786464 | tf_op jit(solution)/shard_map/ppermute | solution.py:633
  3.5 4.1 %first.1 = (f32[13,128,128]{2,1,0:T(8,128)S(1)}, f32[8,128,128]{2,1,0:T(8,128)S(1)}, f32[8,128,128]{2,1,0:T(8,128)}, f32[12,128,128]{2,1,0:T(8,128)}) custom-call(s32[64]{0:T(128)} %wells.1, f32[64]{0:T(128)} %rate.1, f32[2,4,128,128]{3,2,1,0:T(8,128)} %log_perm.3, f32[4,128,128]{2,1,0:T(8,128)} %own_sat.1, f32[4,128,128]{2,1,0:T(8,128)} %own_press.1, ...), custom_call_target="tpu_custom_call" | custom-call | tf_op jit(solution)/shard_map/first/pallas_call | solution.py:643
  7.6 2.1 %collective-permute-start.2 = (f32[8,128,128]{2,1,0:T(8,128)S(1)}, f32[8,128,128]{2,1,0:T(8,128)S(1)}, u32[]{:S(2)}, u32[]{:S(2)}) collective-permute-start(f32[8,128,128]{2,1,0:T(8,128)S(1)} %get-tuple-element.21), channel_id=1, source_target_pairs={{0,2},{2,4},{4,6},{6,8},{8,10},{10,12},{12,14},{14,16},{16,18},{18... | collective-permute-start | bytes 1572872 | tf_op jit(solution)/shard_map/ppermute | solution.py:660
  9.7 0.0 collective-permute-done.1.raw_in
  9.7 0.0 copy-start.3
  9.7 8.0 %collective-permute-done.2.late_in = f32[8,128,128]{2,1,0:T(8,128)S(1)} collective-permute-done((f32[8,128,128]{2,1,0:T(8,128)S(1)}, f32[8,128,128]{2,1,0:T(8,128)S(1)}, u32[]{:S(2)}, u32[]{:S(2)}) %collective-permute-start.2) | collective-permute-done | bytes 524320 | tf_op jit(solution)/shard_map/ppermute | solution.py:660
  17.7 0.0 copy-done.3
  17.7 7.1 %second.1 = (f32[13,128,128]{2,1,0:T(8,128)S(1)}, f32[13,128,128]{2,1,0:T(8,128)S(1)}, f32[8,128,128]{2,1,0:T(8,128)}, f32[8,128,128]{2,1,0:T(8,128)S(1)}, f32[4...) custom-call(f32[8,128,128]{2,1,0:T(8,128)} %get-tuple-element.19.perm_own, f32[9,128,128]{2,1,0:T(8,128)} %copy-done.3, ...), custom_call_target="tpu_custom_call" | custom-call | tf_op jit(solution)/shard_map/second/pallas_call | solution.py:662
  24.8 1.0 %collective-permute-start.3 = (f32[13,128,128]{2,1,0:T(8,128)S(1)}, f32[13,128,128]{2,1,0:T(8,128)S(1)}, u32[]{:S(2)}, u32[]{:S(2)}) collective-permute-start(f32[13,128,128]{2,1,0:T(8,128)S(1)} %get-tuple-element.26), channel_id=1, source_target_pairs={{2,0},{4,2},{6,4},{8,6},{10,8},{12,10},{14,12},{16,14},{18,16},{20... | collective-permute-start | bytes 2555912 | tf_op jit(solution)/shard_map/ppermute | solution.py:681
  25.9 14.9 %all_to_all.10 = f32[4,2,4,32,128]{4,3,2,1,0:T(8,128)} all-to-all(f32[4,2,4,32,128]{4,3,2,1,0:T(8,128)} %get-tuple-element.22), channel_id=1, replica_groups=mesh['mem'=4,'space'=32] {'mem'}, dimensions={0} | all-to-all | bytes 1048576 | tf_op jit(solution)/shard_map/all_to_all | solution.py:682
  40.8 0.0 collective-permute-done.3.got
  40.8 5.9 %third.1 = (f32[13,128,128]{2,1,0:T(8,128)S(1)}, f32[13,128,128]{2,1,0:T(8,128)S(1)}, f32[8,128,128]{2,1,0:T(8,128)S(1)}) custom-call(f32[12,128,128]{2,1,0:T(8,128)} %get-tuple-element.18.q, f32[8,4,32,128]{3,2,1,0:T(8,128)} %bitcast.12, f32[8,128,128]{2,1,0:T(8,128)} %get-tuple-element.23.perm_later, f32[8,128,128]{2,1,0:T(8,128)S(1)} %get-tuple-element.24.perm, ...), custom_call_target="tpu_custom_call" | custom-call | tf_op jit(solution)/shard_map/third/pallas_call | solution.py:683
  46.7 1.1 %collective-permute-start.4 = (f32[13,128,128]{2,1,0:T(8,128)S(1)}, f32[13,128,128]{2,1,0:T(8,128)S(1)}, u32[]{:S(2)}, u32[]{:S(2)}) collective-permute-start(f32[13,128,128]{2,1,0:T(8,128)S(1)} %get-tuple-element.29), channel_id=1, source_target_pairs={{0,2},{2,4},{4,6},{6,8},{8,10},{10,12},{12,14},{14,16},{16,18},{18... | collective-permute-start | bytes 2555912 | tf_op jit(solution)/shard_map/ppermute | solution.py:692
  47.8 10.2 %collective-permute-done.4.got = f32[13,128,128]{2,1,0:T(8,128)S(1)} collective-permute-done((f32[13,128,128]{2,1,0:T(8,128)S(1)}, f32[13,128,128]{2,1,0:T(8,128)S(1)}, u32[]{:S(2)}, u32[]{:S(2)}) %collective-permute-start.4) | collective-permute-done | bytes 852000 | tf_op jit(solution)/shard_map/ppermute | solution.py:692
  58.0 6.1 %last.1 = f32[128,128]{1,0:T(8,128)} custom-call(f32[12,128,128]{2,1,0:T(8,128)} %get-tuple-element.18.q, s32[8,512]{1,0:T(8,128)} %bitcast.15, f32[8,512]{1,0:T(8,128)} %bitcast.16, f32[8,128,128]{2,1,0:T(8,128)S(1)} %get-tuple-element.27.perm, f32[13,128,128]{2,1,0:T(8,128)S(1)} %get-tuple-element.28.kept, f32[13,128,128]{2,1,0:T(8,128)S(1)} %collective-permute-done.4.got), custom_call_target="tpu_custom_call" | custom-call | tf_op jit(solution)/shard_map/last/pallas_call | solution.py:694
  64.1 0.0 copy-start
  64.1 22.7 %all_to_all.11 = f32[128,1,128]{2,1,0:T(1,128)S(1)} all-to-all(f32[128,1,128]{2,1,0:T(1,128)} %bitcast.14), channel_id=1, replica_groups=mesh['mem'=4,'space'=32] {'mem','space'}, dimensions={0} | all-to-all | bytes 131072 | tf_op jit(solution)/shard_map/all_to_all | solution.py:704
  86.8 0.0 copy-done
  86.8 2.1 %solve.1 = f32[8,4,32,128]{3,2,1,0:T(8,128)} custom-call(f32[128,128]{1,0:T(8,128)S(1)} %bitcast.11, f32[4,16,128]{2,1,0:T(8,128)S(1)} %copy-done, f32[8,4,32,128]{3,2,1,0:T(8,128)} %bitcast.13), custom_call_target="tpu_custom_call" | custom-call | tf_op jit(solution)/shard_map/solve/pallas_call | solution.py:707
  (3 shorter events, 0.1 us)
Async XLA Ops:
  0.0 1.0 %copy-start.1 = (f32[4,128,128]{2,1,0:T(8,128)S(1)}, f32[4,128,128]{2,1,0:T(8,128)}, u32[]{:S(2)}) copy-start(f32[4,128,128]{2,1,0:T(8,128)} %own_press.1) | copy-start | bytes 786436
  0.0 1.1 %copy-start.2 = (f32[4,128,128]{2,1,0:T(8,128)S(1)}, f32[4,128,128]{2,1,0:T(8,128)}, u32[]{:S(2)}) copy-start(f32[4,128,128]{2,1,0:T(8,128)} %own_sat.1) | copy-start | bytes 786436
  1.2 2.4 %collective-permute-start = (f32[12,128,128]{2,1,0:T(8,128)S(1)}, f32[12,128,128]{2,1,0:T(8,128)S(1)}, u32[]{:S(2)}, u32[]{:S(2)}) collective-permute-start(f32[12,128,128]{2,1,0:T(8,128)S(1)} %pad_maximum_fusion), channel_id=1, source_target_pairs={{0,1},{1,0},{2,3},{3,2},{4,5},{5,4},{6,7},{7,6},{8,9},{9,8},{10,11... | collective-permute-start | bytes 2359304 | tf_op jit(solution)/shard_map/ppermute | solution.py:633
  1.4 8.4 %collective-permute-start.1 = (f32[9,128,128]{2,1,0:T(8,128)S(1)}, f32[9,128,128]{2,1,0:T(8,128)S(1)}, u32[]{:S(2)}, u32[]{:S(2)}) collective-permute-start(f32[9,128,128]{2,1,0:T(8,128)S(1)} %pad_maximum_fusion.1), channel_id=1, source_target_pairs={{0,0},{31,31},{1,2},{2,1},{3,4},{4,3},{5,6},{6,5},{7,8},{8,7},{9,1... | collective-permute-start | bytes 1769480 | tf_op jit(solution)/shard_map/ppermute | solution.py:636
  7.6 10.1 %collective-permute-start.2 = (f32[8,128,128]{2,1,0:T(8,128)S(1)}, f32[8,128,128]{2,1,0:T(8,128)S(1)}, u32[]{:S(2)}, u32[]{:S(2)}) collective-permute-start(f32[8,128,128]{2,1,0:T(8,128)S(1)} %get-tuple-element.21), channel_id=1, source_target_pairs={{0,2},{2,4},{4,6},{6,8},{8,10},{10,12},{12,14},{14,16},{16,18},{18... | collective-permute-start | bytes 1572872 | tf_op jit(solution)/shard_map/ppermute | solution.py:660
  9.7 8.0 %copy-start.3 = (f32[9,128,128]{2,1,0:T(8,128)}, f32[9,128,128]{2,1,0:T(8,128)S(1)}, u32[]{:S(2)}) copy-start(f32[9,128,128]{2,1,0:T(8,128)S(1)} %collective-permute-done.1.raw_in) | copy-start | bytes 1769476
  24.8 15.9 %collective-permute-start.3 = (f32[13,128,128]{2,1,0:T(8,128)S(1)}, f32[13,128,128]{2,1,0:T(8,128)S(1)}, u32[]{:S(2)}, u32[]{:S(2)}) collective-permute-start(f32[13,128,128]{2,1,0:T(8,128)S(1)} %get-tuple-element.26), channel_id=1, source_target_pairs={{2,0},{4,2},{6,4},{8,6},{10,8},{12,10},{14,12},{16,14},{18,16},{20... | collective-permute-start | bytes 2555912 | tf_op jit(solution)/shard_map/ppermute | solution.py:681
  46.7 11.3 %collective-permute-start.4 = (f32[13,128,128]{2,1,0:T(8,128)S(1)}, f32[13,128,128]{2,1,0:T(8,128)S(1)}, u32[]{:S(2)}, u32[]{:S(2)}) collective-permute-start(f32[13,128,128]{2,1,0:T(8,128)S(1)} %get-tuple-element.29), channel_id=1, source_target_pairs={{0,2},{2,4},{4,6},{6,8},{8,10},{10,12},{12,14},{14,16},{16,18},{18... | collective-permute-start | bytes 2555912 | tf_op jit(solution)/shard_map/ppermute | solution.py:692
  64.1 22.7 %copy-start = (f32[4,16,128]{2,1,0:T(8,128)S(1)}, f32[4,16,128]{2,1,0:T(8,128)}, u32[]{:S(2)}) copy-start(f32[4,16,128]{2,1,0:T(8,128)} %get-tuple-element.30.tables) | copy-start | bytes 98308

commit v8 on v7

--- a/solution.py
+++ b/solution.py
@@ -299,9 +299,9 @@
     move(pairs)
 
 
-def first_kernel(chips, wells, rate, log_perm, own_sat, own_press, swapped, keep, send, perm_out, q_out, *refs):
+def first_kernel(chips, wells, rate, log_perm, own_sat, own_press, swapped, keep, send, perm, q_out, *refs):
     odd, _, _ = position(chips)
-    perm, raw, sems = refs[11:]
+    raw, sems = refs[11:]
     tile = Tile(*refs[:10], perm, refs[10], lambda row: row + 4, jnp.int32(0))
     inner = pl.ds(PAD, tile.ny)
 
@@ -334,7 +334,6 @@
     halve(swapped, 4)
     drain(copies)
     halve(raw, 0)
-    out_copies += issue([(perm, perm_out)], sems, 10)
     tile.props(0, 0, 7)
     advance(tile, keep, send, False, False)
     drain(out_copies)
@@ -363,9 +362,12 @@
     return lambda row: jnp.where((cut == 1) & (row >= 4), row, 7 - row)
 
 
-def second_kernel(chips, perm_own, raw_in, q, log_perm, value_in, var_in, noise_in, kept, late_in, keep, send, perm_out, perm_next, blocks, tables, *refs):
+def second_kernel(
+    chips, q, log_perm, value_in, var_in, noise_in, perm_own, raw, kept, late_in,
+    keep, send, perm_out, blocks, tables, *refs
+):
     odd, _, end = position(chips)
-    perm, raw, held, value, var, noise, sems = refs[11:]
+    perm, held, value, var, noise, sems = refs[11:]
     tile = Tile(*refs[:10], perm, refs[10], edge_q(end), end)
     straight = odd ^ end
 
@@ -377,25 +379,21 @@
             return raw.at[4 + place(plane, 2)]
         return raw.at[6 + place(plane - 2, 3)]
 
-    copies = issue([(raw_in, raw)] + [(perm_own.at[3 - d], perm.at[d]) for d in range(4)], sems, 0)
     q_copy = issue([(q, tile.q)], sems, 5)
     load = issue(
-        [(log_perm, held), (value_in, value), (var_in, var), (noise_in, noise), (perm_own, perm_next)],
-        sems,
-        7,
+        [(log_perm, held), (value_in, value), (var_in, var), (noise_in, noise)], sems, 7
     )
     sides = (
         take(tile, lambda n: kept.at[n], lambda n: kept.at[n], 4, -1),
         take(tile, early, lambda n: late_in.at[n - S1[0]], 6, 1),
     )
     tile.clear()
-    move(sides[0][0] + sides[0][1] + sides[0][2] + sides[1][1] + sides[1][2])
-    drain(copies)
-    move(sides[1][0])
+    move(sum((side[n] for side in sides for n in range(3)), []))
 
     def permeability(d, carry):
         for y0 in range(0, tile.ny, CHUNK):
             where = pl.ds(y0, CHUNK)
+            perm[3 - d, where, :] = perm_own[d, where, :]
             perm[4 + d, where, :] = 0.5 * jnp.exp(raw[place(d, 4), where, :])
         return carry
 
@@ -646,12 +644,12 @@
         out_shape=(
             plane(PLANES),
             plane(8),
-            pltpu.HBM((8,) + grid, f32),
+            plane(8),
             pltpu.HBM((12,) + grid, f32),
         ),
         in_specs=[SMEM] * 2 + [FAR] * 3 + [VMEM],
-        out_specs=(VMEM, VMEM, FAR, FAR),
-        scratch_shapes=scratch + [plane(8), plane(4), sems],
+        out_specs=(VMEM, VMEM, VMEM, FAR),
+        scratch_shapes=scratch + [plane(4), sems],
         compiler_params=pltpu.CompilerParams(vmem_limit_bytes=GRANT + 1_400_000),
     )(wells, well_rate, log_perm, saturation, pressure_init, near(swapped))
     onward = [(i, i + 2) for i in range(0, ends - 1, 2)] + [(ends - 1, ends)]
@@ -659,25 +657,24 @@
     back = [(b, a) for a, b in onward]
     got = lax.ppermute(send, "space", onward)
     small = (obs_value.reshape(4, nz), obs_var.reshape(4, nz), noise)
-    keep, send, perm_edge, perm_tile, blocks, tables = call(
+    keep, send, perm_edge, blocks, tables = call(
         second_kernel,
         "second",
         out_shape=(
             plane(PLANES),
             plane(PLANES),
             pltpu.HBM((8,) + grid, f32),
-            plane(8),
             pltpu.HBM((mems, members, width, ny // mems, nz), f32),
             jax.ShapeDtypeStruct((4, 16, nz), f32),
         ),
-        in_specs=[FAR] * 7 + [VMEM] * 2,
-        out_specs=(VMEM, VMEM, FAR, VMEM, FAR, VMEM),
+        in_specs=[FAR] * 5 + [VMEM] * 4,
+        out_specs=(VMEM, VMEM, FAR, FAR, VMEM),
         scratch_shapes=scratch
-        + [plane(8), plane(9), pltpu.VMEM(log_perm.shape, f32)]
+        + [plane(8), pltpu.VMEM(log_perm.shape, f32)]
         + [pltpu.VMEM(table.shape, f32) for table in small]
         + [sems],
         compiler_params=grant,
-    )(perm_tile, edge_in, q, log_perm, *small, near(keep), near(got))
+    )(q, log_perm, *small, near(perm_tile), near(edge_in), near(keep), near(got))
     got = lax.ppermute(send, "space", back)
     columns = lax.all_to_all(blocks, "mem", 0, 0, tiled=True).reshape(ens, width, ny // mems, nz)
     keep, send, perm_edge = call(

time: 89.5 us -> 89.2 us (level)
  no operation moved by 1% of the time
where the time goes in v8:
time: 89.2 us; the launch traced here: 88.6 us
  blocking collectives  37.7 us (42%)
  Pallas kernels  25 us (28%)
  waiting for transfers between devices  19.7 us (22%)
  starting transfers between devices  4.98 us (6%)
  local copies, waits for them, and re-layouts  1.14 us (1%)
    all_to_all x1, blocking collectives, body(): lax.all_to_all(values.reshape(devices, 1, nz), ('mem', 'space'), 0, 0, ti...  22.7 us
    ppermute x2, waiting for transfers between devices, body(): got = lax.ppermute(send, 'space', onward)  18.2 us
    all_to_all x1, blocking collectives, body(): lax.all_to_all(blocks, 'mem', 0, 0, tiled=True)  14.9 us
    pallas_call x1, Pallas kernels, body(): call(second_kernel, 'second', out_shape=(plane(PLANES), plane(PLANES), pl...  6.75 us
    pallas_call x1, Pallas kernels, body(): call(last_kernel, 'last', out_shape=pltpu.HBM((devices, nz), f32), in_spe...  6.06 us
    pallas_call x1, Pallas kernels, body(): call(third_kernel, 'third', out_shape=(plane(PLANES), plane(PLANES), plan...  5.93 us
    pallas_call x1, Pallas kernels, body(): call(first_kernel, 'first', out_shape=(plane(PLANES), plane(8), plane(8),...  4.1 us
    ppermute x2, starting transfers between devices, body(): got = lax.ppermute(send, 'space', onward)  3.18 us
  transfers between devices with their start and end apart: 5, of which 3 were waited for; matrix products, arithmetic and copies ran while one was open for 0% of the time, Pallas kernels for 5%

profile of v8, /device:TPU:0, one launch (start us, length us, event | category | flops | bytes accessed | tf_op | source)
XLA Modules:
  0.0 88.6 jit_solution(1535220958437711883)
XLA Ops:
  0.0 0.0 copy-start.1
  0.0 0.0 copy-start.2
  0.0 1.0 %dynamic-slice_bitcast_fusion = f32[4,128,128]{2,1,0:T(8,128)S(1)} fusion(f32[2,4,128,128]{3,2,1,0:T(8,128)} %log_perm.3, s32[]{:T(128)S(6)} %select_n.17), kind=kLoop, calls=%fused_computation.2 | loop fusion | bytes 524292 | tf_op jit(solution)/shard_map/squeeze | solution.py:629
  1.0 0.0 copy-done.1
  1.0 0.1 copy-done.2
  1.1 0.1 pad_maximum_fusion
  1.2 0.1 collective-permute-start
  1.4 0.7 collective-permute-start.1
  2.1 1.5 %collective-permute-done.swapped = f32[12,128,128]{2,1,0:T(8,128)S(1)} collective-permute-done((f32[12,128,128]{2,1,0:T(8,128)S(1)}, f32[12,128,128]{2,1,0:T(8,128)S(1)}, u32[]{:S(2)}, u32[]{:S(2)}) %collective-permute-start) | collective-permute-done | bytes 786464 | tf_op jit(solution)/shard_map/ppermute | solution.py:631
  3.5 4.1 %first.1 = (f32[13,128,128]{2,1,0:T(8,128)S(1)}, f32[8,128,128]{2,1,0:T(8,128)S(1)}, f32[8,128,128]{2,1,0:T(8,128)S(1)}, f32[12,128,128]{2,1,0:T(8,128)}) custom-call(s32[64]{0:T(128)} %wells.1, f32[64]{0:T(128)} %rate.1, f32[2,4,128,128]{3,2,1,0:T(8,128)} %log_perm.3, f32[4,128,128]{2,1,0:T(8,128)} %own_sat.1, f32[4,128,128]{2,1,0:T(8,128)} %own_press.1, ...), custom_call_target="tpu_custom_call" | custom-call | tf_op jit(solution)/shard_map/first/pallas_call | solution.py:641
  7.6 2.1 %collective-permute-start.2 = (f32[8,128,128]{2,1,0:T(8,128)S(1)}, f32[8,128,128]{2,1,0:T(8,128)S(1)}, u32[]{:S(2)}, u32[]{:S(2)}) collective-permute-start(f32[8,128,128]{2,1,0:T(8,128)S(1)} %get-tuple-element.20), channel_id=1, source_target_pairs={{0,2},{2,4},{4,6},{6,8},{8,10},{10,12},{12,14},{14,16},{16,18},{18... | collective-permute-start | bytes 1572872 | tf_op jit(solution)/shard_map/ppermute | solution.py:658
  9.7 0.0 collective-permute-done.1.raw
  9.7 8.0 %collective-permute-done.2.late_in = f32[8,128,128]{2,1,0:T(8,128)S(1)} collective-permute-done((f32[8,128,128]{2,1,0:T(8,128)S(1)}, f32[8,128,128]{2,1,0:T(8,128)S(1)}, u32[]{:S(2)}, u32[]{:S(2)}) %collective-permute-start.2) | collective-permute-done | bytes 524320 | tf_op jit(solution)/shard_map/ppermute | solution.py:658
  17.7 6.8 %second.1 = (f32[13,128,128]{2,1,0:T(8,128)S(1)}, f32[13,128,128]{2,1,0:T(8,128)S(1)}, f32[8,128,128]{2,1,0:T(8,128)}, f32[4,2,4,32,128]{4,3,2,1,0:T(8,128)}, f32[4,16,128]{2,1,0:T(8,128)}) custom-call(f32[12,128,128]{2,1,0:T(8,128)} %get-tuple-element.17.q, f32[2,4,128,128]{3,2,1,0:T(8,128)} %log_perm.3, f32[4,128]{1,0:T(4,128)} %bitcast.17, ...), custom_call_target="tpu_custom_call" | custom-call | tf_op jit(solution)/shard_map/second/pallas_call | solution.py:660
  24.5 1.0 %collective-permute-start.3 = (f32[13,128,128]{2,1,0:T(8,128)S(1)}, f32[13,128,128]{2,1,0:T(8,128)S(1)}, u32[]{:S(2)}, u32[]{:S(2)}) collective-permute-start(f32[13,128,128]{2,1,0:T(8,128)S(1)} %get-tuple-element.24), channel_id=1, source_target_pairs={{2,0},{4,2},{6,4},{8,6},{10,8},{12,10},{14,12},{16,14},{18,16},{20... | collective-permute-start | bytes 2555912 | tf_op jit(solution)/shard_map/ppermute | solution.py:678
  25.5 14.9 %all_to_all.10 = f32[4,2,4,32,128]{4,3,2,1,0:T(8,128)} all-to-all(f32[4,2,4,32,128]{4,3,2,1,0:T(8,128)} %get-tuple-element.21), channel_id=1, replica_groups=mesh['mem'=4,'space'=32] {'mem'}, dimensions={0} | all-to-all | bytes 1048576 | tf_op jit(solution)/shard_map/all_to_all | solution.py:679
  40.4 0.0 collective-permute-done.3.got
  40.4 5.9 %third.1 = (f32[13,128,128]{2,1,0:T(8,128)S(1)}, f32[13,128,128]{2,1,0:T(8,128)S(1)}, f32[8,128,128]{2,1,0:T(8,128)S(1)}) custom-call(f32[12,128,128]{2,1,0:T(8,128)} %get-tuple-element.17.q, f32[8,4,32,128]{3,2,1,0:T(8,128)} %bitcast.12, f32[8,128,128]{2,1,0:T(8,128)} %get-tuple-element.22.perm_later, f32[8,128,128]{2,1,0:T(8,128)S(1)} %get-tuple-element.18.perm_own.perm, ...), custom_call_target="tpu_custom_call" | custom-call | tf_op jit(solution)/shard_map/third/pallas_call | solution.py:680
  46.4 1.1 %collective-permute-start.4 = (f32[13,128,128]{2,1,0:T(8,128)S(1)}, f32[13,128,128]{2,1,0:T(8,128)S(1)}, u32[]{:S(2)}, u32[]{:S(2)}) collective-permute-start(f32[13,128,128]{2,1,0:T(8,128)S(1)} %get-tuple-element.27), channel_id=1, source_target_pairs={{0,2},{2,4},{4,6},{6,8},{8,10},{10,12},{12,14},{14,16},{16,18},{18... | collective-permute-start | bytes 2555912 | tf_op jit(solution)/shard_map/ppermute | solution.py:689
  47.5 10.2 %collective-permute-done.4.got = f32[13,128,128]{2,1,0:T(8,128)S(1)} collective-permute-done((f32[13,128,128]{2,1,0:T(8,128)S(1)}, f32[13,128,128]{2,1,0:T(8,128)S(1)}, u32[]{:S(2)}, u32[]{:S(2)}) %collective-permute-start.4) | collective-permute-done | bytes 852000 | tf_op jit(solution)/shard_map/ppermute | solution.py:689
  57.7 6.1 %last.1 = f32[128,128]{1,0:T(8,128)} custom-call(f32[12,128,128]{2,1,0:T(8,128)} %get-tuple-element.17.q, s32[8,512]{1,0:T(8,128)} %bitcast.15, f32[8,512]{1,0:T(8,128)} %bitcast.16, f32[8,128,128]{2,1,0:T(8,128)S(1)} %get-tuple-element.25.perm, f32[13,128,128]{2,1,0:T(8,128)S(1)} %get-tuple-element.26.kept, f32[13,128,128]{2,1,0:T(8,128)S(1)} %collective-permute-done.4.got), custom_call_target="tpu_custom_call" | custom-call | tf_op jit(solution)/shard_map/last/pallas_call | solution.py:691
  63.7 0.0 copy-start
  63.7 22.7 %all_to_all.11 = f32[128,1,128]{2,1,0:T(1,128)S(1)} all-to-all(f32[128,1,128]{2,1,0:T(1,128)} %bitcast.14), channel_id=1, replica_groups=mesh['mem'=4,'space'=32] {'mem','space'}, dimensions={0} | all-to-all | bytes 131072 | tf_op jit(solution)/shard_map/all_to_all | solution.py:701
  86.5 0.0 copy-done
  86.5 2.1 %solve.1 = f32[8,4,32,128]{3,2,1,0:T(8,128)} custom-call(f32[128,128]{1,0:T(8,128)S(1)} %bitcast.11, f32[4,16,128]{2,1,0:T(8,128)S(1)} %copy-done, f32[8,4,32,128]{3,2,1,0:T(8,128)} %bitcast.13), custom_call_target="tpu_custom_call" | custom-call | tf_op jit(solution)/shard_map/solve/pallas_call | solution.py:704
  (3 shorter events, 0.1 us)
Async XLA Ops:
  0.0 1.0 %copy-start.1 = (f32[4,128,128]{2,1,0:T(8,128)S(1)}, f32[4,128,128]{2,1,0:T(8,128)}, u32[]{:S(2)}) copy-start(f32[4,128,128]{2,1,0:T(8,128)} %own_press.1) | copy-start | bytes 786436
  0.0 1.1 %copy-start.2 = (f32[4,128,128]{2,1,0:T(8,128)S(1)}, f32[4,128,128]{2,1,0:T(8,128)}, u32[]{:S(2)}) copy-start(f32[4,128,128]{2,1,0:T(8,128)} %own_sat.1) | copy-start | bytes 786436
  1.2 2.4 %collective-permute-start = (f32[12,128,128]{2,1,0:T(8,128)S(1)}, f32[12,128,128]{2,1,0:T(8,128)S(1)}, u32[]{:S(2)}, u32[]{:S(2)}) collective-permute-start(f32[12,128,128]{2,1,0:T(8,128)S(1)} %pad_maximum_fusion), channel_id=1, source_target_pairs={{0,1},{1,0},{2,3},{3,2},{4,5},{5,4},{6,7},{7,6},{8,9},{9,8},{10,11... | collective-permute-start | bytes 2359304 | tf_op jit(solution)/shard_map/ppermute | solution.py:631
  1.4 8.4 %collective-permute-start.1 = (f32[9,128,128]{2,1,0:T(8,128)S(1)}, f32[9,128,128]{2,1,0:T(8,128)S(1)}, u32[]{:S(2)}, u32[]{:S(2)}) collective-permute-start(f32[9,128,128]{2,1,0:T(8,128)S(1)} %pad_maximum_fusion.1), channel_id=1, source_target_pairs={{0,0},{31,31},{1,2},{2,1},{3,4},{4,3},{5,6},{6,5},{7,8},{8,7},{9,1... | collective-permute-start | bytes 1769480 | tf_op jit(solution)/shard_map/ppermute | solution.py:634
  7.6 10.1 %collective-permute-start.2 = (f32[8,128,128]{2,1,0:T(8,128)S(1)}, f32[8,128,128]{2,1,0:T(8,128)S(1)}, u32[]{:S(2)}, u32[]{:S(2)}) collective-permute-start(f32[8,128,128]{2,1,0:T(8,128)S(1)} %get-tuple-element.20), channel_id=1, source_target_pairs={{0,2},{2,4},{4,6},{6,8},{8,10},{10,12},{12,14},{14,16},{16,18},{18... | collective-permute-start | bytes 1572872 | tf_op jit(solution)/shard_map/ppermute | solution.py:658
  24.5 15.9 %collective-permute-start.3 = (f32[13,128,128]{2,1,0:T(8,128)S(1)}, f32[13,128,128]{2,1,0:T(8,128)S(1)}, u32[]{:S(2)}, u32[]{:S(2)}) collective-permute-start(f32[13,128,128]{2,1,0:T(8,128)S(1)} %get-tuple-element.24), channel_id=1, source_target_pairs={{2,0},{4,2},{6,4},{8,6},{10,8},{12,10},{14,12},{16,14},{18,16},{20... | collective-permute-start | bytes 2555912 | tf_op jit(solution)/shard_map/ppermute | solution.py:678
  46.4 11.3 %collective-permute-start.4 = (f32[13,128,128]{2,1,0:T(8,128)S(1)}, f32[13,128,128]{2,1,0:T(8,128)S(1)}, u32[]{:S(2)}, u32[]{:S(2)}) collective-permute-start(f32[13,128,128]{2,1,0:T(8,128)S(1)} %get-tuple-element.27), channel_id=1, source_target_pairs={{0,2},{2,4},{4,6},{6,8},{8,10},{10,12},{12,14},{14,16},{16,18},{18... | collective-permute-start | bytes 2555912 | tf_op jit(solution)/shard_map/ppermute | solution.py:689
  63.7 22.7 %copy-start = (f32[4,16,128]{2,1,0:T(8,128)S(1)}, f32[4,16,128]{2,1,0:T(8,128)}, u32[]{:S(2)}) copy-start(f32[4,16,128]{2,1,0:T(8,128)} %get-tuple-element.28.tables) | copy-start | bytes 98308
